TPU v7x, 256 devices: a whole 4x4x8 slice. The times are simulated.
256 devices in a mesh: gx: 32 (over x, z_hi, core), gy: 8 (over z_lo, y).
Axes of the slice: x: 4, y: 4, z: 8 (z_hi: 4, z_lo: 2; z = z_hi * 2 + z_lo), core: 2. Of those that a mesh axis runs over, the one named last changes fastest.
Arguments:
- populations: float32 [19, 128, 256, 128], P(None, 'gx', 'gy'), may hold values from 0 to 1, as said below
- labels: int32 [128, 256, 128], P('gx', 'gy'), may hold values from 0 to 3
- solid_mask: int32 [128, 256, 128], P('gx', 'gy'), may hold values 0 or 1
Outputs:
- new_populations: float32 [19, 128, 256, 128], P(None, 'gx', 'gy')
- phase: float32 [128, 256, 128], P('gx', 'gy')
Inputs may be any that keep to these rules, and one draw needn't show every extreme that they name: `populations`: every entry is positive.
All inputs are finite; a program needn't handle non-finite values. No bound on the sum of `solid_mask` on one device may be relied on, other than what follows from the above.
Results may differ from a plain program's by a relative error of at most 0.00011.
Values sent between devices are 32-bit elements; how exact they have to be, the bound alone decides.
No kernel may reach another device: no remote copies, remote signals or barrier semaphores. Data moves between devices by JAX's collectives and lax.ppermute only.
A program may use at most 64 MiB of HBM per device.

v0:
```python
import jax
import jax.numpy as jnp
import numpy as np
from jax import lax
from jax.experimental import pallas as pl
from jax.experimental.pallas import tpu as pltpu
from jax.sharding import PartitionSpec as P

VELOCITY_SET = [
    (0, 0, 0), (1, 0, 0), (-1, 0, 0), (0, 1, 0), (0, -1, 0), (0, 0, 1), (0, 0, -1),
    (1, 1, 0), (-1, -1, 0), (1, -1, 0), (-1, 1, 0), (1, 0, 1), (-1, 0, -1), (1, 0, -1),
    (-1, 0, 1), (0, 1, 1), (0, -1, -1), (0, 1, -1), (0, -1, 1),
]
DIRS = [
    (-1, 0, 0), (-1, 1, 0), (-1, -1, 0), (-1, 0, 1), (-1, 0, -1),
    (1, 0, 0), (1, 1, 0), (1, -1, 0), (1, 0, 1), (1, 0, -1),
    (0, 0, 0), (0, 1, 0), (0, -1, 0), (0, 0, 1), (0, 0, -1),
    (0, 1, 1), (0, -1, -1), (0, 1, -1), (0, -1, 1),
]
REF_OF = [VELOCITY_SET.index(d) for d in DIRS]
POS = {d: k for k, d in enumerate(DIRS)}
GROUPS = [(-1, 0), (-1, 1), (-1, -1), (1, 0), (1, 1), (1, -1), (0, 0), (0, 1), (0, -1)]
GPOS = {g: k for k, g in enumerate(GROUPS)}
NXL = 4
NYL = 32
EXT = 40
NT = 5
ROW0 = 8
SROWS = 56
YROWS = 256
W1 = 1.0 / 18.0
W2 = 1.0 / 36.0


def neg(d):
    return (-d[0], -d[1], -d[2])


def zroll(v, shift):
    if shift == 0:
        return v
    return pltpu.roll(v, shift % 128, 1)


def collide(f):
    def pair(a, b):
        pa, pb = f[a], f[b]
        return pa + pb, pa - pb

    s1, d1 = pair((1, 1, 0), (-1, -1, 0))
    s2, d2 = pair((1, -1, 0), (-1, 1, 0))
    xxyy, xy, xyy, xxy = s1 + s2, s1 - s2, d1 + d2, d1 - d2
    s1, d1 = pair((1, 0, 1), (-1, 0, -1))
    s2, d2 = pair((1, 0, -1), (-1, 0, 1))
    xxzz, xz, xzz, xxz = s1 + s2, s1 - s2, d1 + d2, d1 - d2
    s1, d1 = pair((0, 1, 1), (0, -1, -1))
    s2, d2 = pair((0, 1, -1), (0, -1, 1))
    yyzz, yz, yzz, yyz = s1 + s2, s1 - s2, d1 + d2, d1 - d2
    ax, dx = pair((1, 0, 0), (-1, 0, 0))
    ay, dy = pair((0, 1, 0), (0, -1, 0))
    az, dz = pair((0, 0, 1), (0, 0, -1))
    jx = dx + (xyy + xzz)
    jy = dy + (xxy + yzz)
    jz = dz + (xxz + yyz)
    mxx = ax + (xxyy + xxzz)
    myy = ay + (xxyy + yyzz)
    mzz = az + (xxzz + yyzz)
    rho = (f[(0, 0, 0)] + (ax + ay)) + (az + (xxyy + (xxzz + yyzz)))
    inv = 1.0 / rho
    ux, uy, uz = jx * inv, jy * inv, jz * inv
    qx, qy, qz = jx * ux, jy * uy, jz * uz
    third = rho * (1.0 / 3.0)
    nxx = mxx - third - qx
    nyy = myy - third - qy
    nzz = mzz - third - qz
    trace = nxx + nyy + nzz
    iso = trace * (-1.0 / 24.0)
    hxx = 0.625 * nxx + iso
    hyy = 0.625 * nyy + iso
    hzz = 0.625 * nzz + iso
    dxy = 0.3125 * (xy - jx * uy)
    dxz = 0.3125 * (xz - jx * uz)
    dyz = 0.3125 * (yz - jy * uz)
    kx, ky, kz = jx * 0.1, jy * 0.1, jz * 0.1
    dxyy = 0.3 * xyy - kx
    dxzz = 0.3 * xzz - kx
    dxxy = 0.3 * xxy - ky
    dyzz = 0.3 * yzz - ky
    dxxz = 0.3 * xxz - kz
    dyyz = 0.3 * yyz - kz
    base = (0.35 / 9.0) * rho + (0.35 / 3.0) * (qx + qy + qz)
    dxxyy = 0.35 * xxyy - (base - 0.175 * qz)
    dxxzz = 0.35 * xxzz - (base - 0.175 * qy)
    dyyzz = 0.35 * yyzz - (base - 0.175 * qx)
    out = {}

    def diagonal(quad, cross, la, lb, da, db):
        t1, t2 = quad + cross, quad - cross
        v1, v2 = la + lb, la - lb
        out_dirs = []
        for sa, sb in ((1, 1), (-1, -1), (1, -1), (-1, 1)):
            e = tuple(sa * p + sb * q for p, q in zip(da, db))
            out_dirs.append(e)
        out[out_dirs[0]] = f[out_dirs[0]] - (t1 + v1)
        out[out_dirs[1]] = f[out_dirs[1]] - (t1 - v1)
        out[out_dirs[2]] = f[out_dirs[2]] - (t2 + v2)
        out[out_dirs[3]] = f[out_dirs[3]] - (t2 - v2)

    X, Y, Z = (1, 0, 0), (0, 1, 0), (0, 0, 1)
    diagonal(dxxyy, dxy, dxyy, dxxy, X, Y)
    diagonal(dxxzz, dxz, dxzz, dxxz, X, Z)
    diagonal(dyyzz, dyz, dyzz, dyyz, Y, Z)

    def axis(half, q1, q2, l1, l2, d):
        even = half - 2.0 * (q1 + q2)
        odd = 2.0 * (l1 + l2)
        out[d] = f[d] - (even - odd)
        out[neg(d)] = f[neg(d)] - (even + odd)

    axis(hxx, dxxyy, dxxzz, dxyy, dxzz, X)
    axis(hyy, dxxyy, dyyzz, dxxy, dyzz, Y)
    axis(hzz, dxxzz, dyyzz, dxxz, dyyz, Z)
    out[(0, 0, 0)] = f[(0, 0, 0)] + trace - 4.0 * (dxxyy + dxxzz + dyyzz)
    return out, rho


def gradient(ph, plane, row):
    def at(dx, dy):
        return ph[plane + dx, pl.ds(row + dy, 8), :]

    c = at(0, 0)
    xp, xm, yp, ym = at(1, 0), at(-1, 0), at(0, 1), at(0, -1)
    d1 = at(1, 1) - at(-1, -1)
    d2 = at(1, -1) - at(-1, 1)
    ex = xp - xm
    ey = yp - ym
    h = 2.0 * c + ((xp + xm) + (yp + ym))
    k = 1.0 / 12.0
    gx = k * ((2.0 * ex + (d1 + d2)) + (zroll(ex, 1) + zroll(ex, -1)))
    gy = k * ((2.0 * ey + (d1 - d2)) + (zroll(ey, 1) + zroll(ey, -1)))
    gz = k * (zroll(h, -1) - zroll(h, 1))
    return c, gx, gy, gz


def finish(dirs, s_of, ph, rho, fluid, plane, row, fp, red):
    p, gx, gy, gz = gradient(ph, plane + 1, row)
    g2 = gx * gx + gy * gy + gz * gz
    inv = lax.rsqrt(jnp.maximum(g2, 0.01)) * fluid
    h1 = (0.1 * W1) * inv
    h2 = (0.1 * W2) * inv
    cc = (0.175 * rho) * ((1.0 - p * p) * inv)
    c1 = W1 * cc
    c2 = W2 * cc
    frac = 0.5 + 0.5 * p
    comp = (gx, gy, gz)
    sums = {}
    cache = {}
    for d in dirs:
        moving = [k for k in range(3) if d[k] != 0]
        if not moving:
            q, c = h1 * (6.0 * g2), None
        else:
            sign = d[moving[0]]
            key = d if sign > 0 else neg(d)
            if key not in cache:
                if len(moving) == 1:
                    a = comp[moving[0]]
                    cache[key] = (h1 * (a * a - g2), c1 * a)
                else:
                    u, v = moving
                    a = comp[u] + comp[v] if key[v] > 0 else comp[u] - comp[v]
                    cache[key] = (h2 * (a * a - g2), c2 * a)
            q, c = cache[key]
        val = s_of(d) + q
        fp[POS[d], plane, pl.ds(row, 8), :] = zroll(val, d[2])
        r = frac * val
        if c is not None:
            r = r + c if sign > 0 else r - c
        r = zroll(r, d[2])
        g = d[:2]
        sums[g] = r if g not in sums else sums[g] + r
    for g, r in sums.items():
        red[GPOS[g], plane, pl.ds(row, 8), :] = r


def arrived(d, fp, plane, row):
    return fp[POS[d], plane - d[0], pl.ds(row - d[1], 8), :]


def red_arrived(red, plane, row):
    total = None
    for g in GROUPS:
        v = red[GPOS[g], plane - g[0], pl.ds(row - g[1], 8), :]
        total = v if total is None else total + v
    return total


def tile_rows(t):
    return lax.broadcasted_iota(jnp.int32, (8, 128), 0) + (8 * t - 4)


def pack_y_kernel(pops, labels, solid, out_a, out_b):
    odd = lax.axis_index("gy") % 2

    def pack(out, high):
        for i in range(19):
            for x in range(NXL):
                r = NYL - 3 if high else 0
                out[pl.ds(i * 12 + x * 3, 3), :] = pops[i, x, pl.ds(r, 3), :]
        for x in range(NXL):
            r = NYL - 4 if high else 0
            out[pl.ds(228 + x * 4, 4), :] = labels[x, pl.ds(r, 4), :].astype(jnp.float32)
            r = NYL - 3 if high else 0
            out[pl.ds(244 + x * 3, 3), :] = solid[x, pl.ds(r, 3), :].astype(jnp.float32)

    @pl.when(odd == 0)
    def _():
        pack(out_a, True)
        pack(out_b, False)

    @pl.when(odd == 1)
    def _():
        pack(out_a, False)
        pack(out_b, True)


def first_kernel(pops, labels, solid, ya, yb, s_out, rho_out, fl_out, ph_out, xa, xb, raw, aux):
    gy = lax.axis_index("gy")
    odd = gy % 2
    low_edge = gy == 0
    high_edge = gy == lax.axis_size("gy") - 1

    def unpack(src, top):
        r = 1 if top else 4
        for i in range(19):
            for x in range(NXL):
                raw[i, x, pl.ds(r, 3), :] = src[pl.ds(i * 12 + x * 3, 3), :]
        for x in range(NXL):
            aux[0, x, pl.ds(0 if top else 4, 4), :] = src[pl.ds(228 + x * 4, 4), :]
            aux[1, x, pl.ds(r, 3), :] = src[pl.ds(244 + x * 3, 3), :]

    @pl.when(odd == 0)
    def _():
        unpack(ya, False)
        unpack(yb, True)

    @pl.when(odd == 1)
    def _():
        unpack(ya, True)
        unpack(yb, False)

    def plane(x, carry):
        for t in range(NT):
            def pick(own, halo):
                if 1 <= t <= 3:
                    return own(8 * t - 4, 8)
                if t == 0:
                    return jnp.concatenate([halo()[0:4], own(0, 4)], axis=0)
                return jnp.concatenate([own(NYL - 4, 4), halo()[4:8]], axis=0)

            f = {}
            for k, d in enumerate(DIRS):
                ref = REF_OF[k]
                f[d] = pick(
                    lambda r, n: pops[ref, x, pl.ds(r, n), :], lambda: raw[ref, x]
                )
            lab = pick(
                lambda r, n: labels[x, pl.ds(r, n), :].astype(jnp.float32),
                lambda: aux[0, x],
            )
            sol = pick(
                lambda r, n: solid[x, pl.ds(r, n), :].astype(jnp.float32),
                lambda: aux[1, x],
            )
            y = tile_rows(t)
            is_solid = sol > 0.5
            p = jnp.where(lab > 0.5, 1.0, -1.0)
            inside = None
            if t == 0:
                is_solid = is_solid | ((y == 0) & low_edge)
                inside = (y >= 0) | jnp.logical_not(low_edge)
            if t == NT - 1:
                is_solid = is_solid | ((y == NYL - 1) & high_edge)
                inside = (y < NYL) | jnp.logical_not(high_edge)
            relaxed, rho = collide(f)
            fl = jnp.where(is_solid, 0.0, 1.0)
            if inside is not None:
                fl = jnp.where(inside, fl, 0.0)
                p = jnp.where(inside, p, 0.0)
            rows = pl.ds(8 * t, 8)
            for d in DIRS:
                v = jnp.where(is_solid, f[neg(d)], relaxed[d])
                if inside is not None:
                    v = jnp.where(inside, v, 0.0)
                s_out[POS[d], x, rows, :] = v
            rho_out[x, rows, :] = rho
            fl_out[x, rows, :] = fl
            ph_out[x, rows, :] = p
        return carry

    lax.fori_loop(0, NXL, plane, 0)
    pack_x(s_out, ph_out, rho_out, fl_out, xa, xb)


def pack_x(s, ph, rho, fl, xa, xb):
    odd = lax.axis_index("gx") % 2

    def pack(out, high):
        base = jnp.where(high, 5, 0)
        face = jnp.where(high, NXL - 1, 0)
        second = jnp.where(high, NXL - 2, 1)
        for j in range(5):
            out[j] = s[base + j, face]
        out[5] = rho[face]
        out[6] = ph[face]
        out[7] = ph[second]
        if fl is not None:
            out[8] = fl[face]

    pack(xa, odd == 0)
    pack(xb, odd == 1)


def unpack_x(xa, xb, hx, ph, n):
    odd = lax.axis_index("gx") % 2

    def put(src, side):
        for j in range(n):
            if j not in (6, 7):
                hx[side, j] = src[j]
        near = jnp.where(side == 1, NXL + 2, 1)
        far = jnp.where(side == 1, NXL + 3, 0)
        ph[near, pl.ds(ROW0, EXT), :] = src[6]
        ph[far, pl.ds(ROW0, EXT), :] = src[7]

    put(xa, jnp.where(odd == 0, 1, 0))
    put(xb, jnp.where(odd == 0, 0, 1))


def interface(s, rho, fl, hx, hfl, ph, fp, red):
    def plane(x, carry):
        for t in range(NT):
            rows = pl.ds(8 * t, 8)
            finish(
                DIRS, lambda d: s[POS[d], x, rows, :], ph, rho[x, rows, :],
                fl[x, rows, :], x + 1, ROW0 + 8 * t, fp, red,
            )
        return carry

    lax.fori_loop(0, NXL, plane, 0)
    for side, plane_index, dirs in ((0, 0, DIRS[5:10]), (1, NXL + 1, DIRS[0:5])):
        for t in range(NT):
            rows = pl.ds(8 * t, 8)
            finish(
                dirs, lambda d: hx[side, dirs.index(d), rows, :], ph, hx[side, 5, rows, :],
                hfl[side, rows, :], plane_index, ROW0 + 8 * t, fp, red,
            )


def middle_kernel(s, rho, fl, p_in, xa, xb, s_out, rho_out, ph_out, hfl_out, xa_out, xb_out,
                  hx, ph, fp, red):
    gy = lax.axis_index("gy")
    low_edge = gy == 0
    high_edge = gy == lax.axis_size("gy") - 1
    unpack_x(xa, xb, hx, ph, 9)
    for x in range(NXL):
        ph[x + 2, pl.ds(ROW0, EXT), :] = p_in[x]
    for side in range(2):
        hfl_out[side] = hx[side, 8]
    interface(s, rho, fl, hx, hfl_out, ph, fp, red)

    def plane(x, carry):
        for t in range(NT):
            row = ROW0 + 8 * t
            rows = pl.ds(8 * t, 8)
            f = {d: arrived(d, fp, x + 1, row) for d in DIRS}
            relaxed, total = collide(f)
            p = 2.0 * red_arrived(red, x + 1, row) / total - 1.0
            y = tile_rows(t)
            inside = None
            if t == 0:
                inside = (y >= 0) | jnp.logical_not(low_edge)
            if t == NT - 1:
                inside = (y < NYL) | jnp.logical_not(high_edge)
            if inside is not None:
                p = jnp.where(inside, p, 0.0)
            is_fluid = fl[x, rows, :] > 0.5
            for d in DIRS:
                v = jnp.where(is_fluid, relaxed[d], f[neg(d)])
                if inside is not None:
                    v = jnp.where(inside, v, 0.0)
                s_out[POS[d], x, rows, :] = v
            rho_out[x, rows, :] = total
            ph_out[x, rows, :] = p
        return carry

    lax.fori_loop(0, NXL, plane, 0)
    pack_x(s_out, ph_out, rho_out, None, xa_out, xb_out)


def last_kernel(s, rho, fl, p_in, hfl, xa, xb, pops_out, phase_out, hx, ph, fp, red):
    unpack_x(xa, xb, hx, ph, 8)
    for x in range(NXL):
        ph[x + 2, pl.ds(ROW0, EXT), :] = p_in[x]
    interface(s, rho, fl, hx, hfl, ph, fp, red)

    def plane(x, carry):
        for t in range(NYL // 8):
            row = ROW0 + 4 + 8 * t
            rows = pl.ds(8 * t, 8)
            total = None
            for d in DIRS:
                v = arrived(d, fp, x + 1, row)
                pops_out[REF_OF[POS[d]], x, rows, :] = v
                total = v if total is None else total + v
            phase_out[x, rows, :] = 2.0 * red_arrived(red, x + 1, row) / total - 1.0
        return carry

    lax.fori_loop(0, NXL, plane, 0)


F32 = jnp.float32
VM = pl.BlockSpec(memory_space=pltpu.VMEM)
PARAMS = pltpu.CompilerParams(vmem_limit_bytes=40 * 1024 * 1024)


def shaped(*dims):
    return jax.ShapeDtypeStruct(dims, F32)


def call(kernel, n_in, outs, scratch, name):
    return pl.pallas_call(
        kernel,
        in_specs=[VM] * n_in,
        out_specs=[VM] * len(outs),
        out_shape=outs,
        scratch_shapes=[pltpu.VMEM(d, F32) for d in scratch],
        compiler_params=PARAMS,
        name=name,
    )


def pairs(count, first):
    out = []
    for i in range(first, count + first, 2):
        a, b = i % count, (i + 1) % count
        out += [(a, b), (b, a)]
    return out


def swap(a, b, axis):
    count = lax.axis_size(axis)
    got_b = lax.ppermute(b, axis, pairs(count, 1))
    got_a = lax.ppermute(a, axis, pairs(count, 0))
    return got_a, got_b


def on_device(populations, labels, solid_mask):
    ya, yb = call(pack_y_kernel, 3, [shaped(YROWS, 128)] * 2, [], "pack_y")(
        populations, labels, solid_mask
    )
    ya, yb = swap(ya, yb, "gy")
    s, rho, fl, ph, xa, xb = call(
        first_kernel, 5,
        [shaped(19, NXL, EXT, 128)] + [shaped(NXL, EXT, 128)] * 3 + [shaped(9, EXT, 128)] * 2,
        [(19, NXL, 8, 128), (2, NXL, 8, 128)], "first",
    )(populations, labels, solid_mask, ya, yb)
    xa, xb = swap(xa, xb, "gx")
    work = [
        (2, 9, EXT, 128), (NXL + 4, SROWS, 128), (19, NXL + 2, SROWS, 128),
        (9, NXL + 2, SROWS, 128),
    ]
    s, rho, ph, hfl, xa, xb = call(
        middle_kernel, 6,
        [shaped(19, NXL, EXT, 128)] + [shaped(NXL, EXT, 128)] * 2
        + [shaped(2, EXT, 128)] + [shaped(8, EXT, 128)] * 2,
        work, "middle",
    )(s, rho, fl, ph, xa, xb)
    xa, xb = swap(xa, xb, "gx")
    return call(
        last_kernel, 7, [shaped(19, NXL, NYL, 128), shaped(NXL, NYL, 128)], work, "last",
    )(s, rho, fl, ph, hfl, xa, xb)


def solution(mesh):
    in_specs = (P(None, "gx", "gy", None), P("gx", "gy", None), P("gx", "gy", None))
    out_specs = (P(None, "gx", "gy", None), P("gx", "gy", None))

    def run(populations, labels, solid_mask):
        new, phase = on_device(populations, labels, solid_mask)
        return new, phase

    return jax.shard_map(
        run, mesh=mesh, in_specs=in_specs, out_specs=out_specs, check_vma=False
    )
```

profile of v0, /device:TPU:24, one launch (start us, length us, event | category | flops | bytes accessed | tf_op | source)
XLA Modules:
  0.0 42.1 jit_solution(7956624681435987217)
XLA Ops:
  0.6 0.0 copy-start
  0.6 1.3 %copy-done = f32[19,4,32,128]{3,2,1,0:T(8,128)S(1)} copy-done((f32[19,4,32,128]{3,2,1,0:T(8,128)S(1)}, f32[19,4,32,128]{3,2,1,0:T(8,128)}, u32[]{:S(2)}) %copy-start) | copy-done | bytes 1245208
  1.9 0.0 copy-start.1
  1.9 0.8 %copy-done.1 = s32[4,32,128]{2,1,0:T(8,128)S(1)} copy-done((s32[4,32,128]{2,1,0:T(8,128)S(1)}, s32[4,32,128]{2,1,0:T(8,128)}, u32[]{:S(2)}) %copy-start.1) | copy-done | bytes 65560
  2.8 0.0 copy-start.2
  2.8 0.8 %copy-done.2 = s32[4,32,128]{2,1,0:T(8,128)S(1)} copy-done((s32[4,32,128]{2,1,0:T(8,128)S(1)}, s32[4,32,128]{2,1,0:T(8,128)}, u32[]{:S(2)}) %copy-start.2) | copy-done | bytes 65560
  3.6 0.1 pack_y.1
  3.7 0.8 %collective-permute-start = (f32[256,128]{1,0:T(8,128)S(1)}, f32[256,128]{1,0:T(8,128)S(1)}, u32[]{:S(2)}, u32[]{:S(2)}) collective-permute-start(f32[256,128]{1,0:T(8,128)S(1)} %get-tuple-element.16), channel_id=1, source_target_pairs={{0,1},{1,0},{2,3},{3,2},{4,5},{5,4},{6,7},{7,6},{8,9},{9,8},{10,11... | collective-permute-start | bytes 393224 | tf_op jit(solution)/shard_map/ppermute | solution.py:454
  4.5 2.4 %collective-permute-start.1 = (f32[256,128]{1,0:T(8,128)S(1)}, f32[256,128]{1,0:T(8,128)S(1)}, u32[]{:S(2)}, u32[]{:S(2)}) collective-permute-start(f32[256,128]{1,0:T(8,128)S(1)} %get-tuple-element.17), channel_id=1, source_target_pairs={{1,2},{2,1},{3,4},{4,3},{5,6},{6,5},{7,0},{0,7},{9,10},{10,9},{11,... | collective-permute-start | bytes 393224 | tf_op jit(solution)/shard_map/ppermute | solution.py:453
  6.9 2.1 %collective-permute-done.ya = f32[256,128]{1,0:T(8,128)S(1)} collective-permute-done((f32[256,128]{1,0:T(8,128)S(1)}, f32[256,128]{1,0:T(8,128)S(1)}, u32[]{:S(2)}, u32[]{:S(2)}) %collective-permute-start) | collective-permute-done | bytes 131104 | tf_op jit(solution)/shard_map/ppermute | solution.py:454
  9.0 2.6 %collective-permute-done.1.yb = f32[256,128]{1,0:T(8,128)S(1)} collective-permute-done((f32[256,128]{1,0:T(8,128)S(1)}, f32[256,128]{1,0:T(8,128)S(1)}, u32[]{:S(2)}, u32[]{:S(2)}) %collective-permute-start.1) | collective-permute-done | bytes 131104 | tf_op jit(solution)/shard_map/ppermute | solution.py:453
  11.6 0.9 %first.1 = (f32[19,4,40,128]{3,2,1,0:T(8,128)S(1)}, f32[4,40,128]{2,1,0:T(8,128)S(1)}, f32[4,40,128]{2,1,0:T(8,128)S(1)}, f32[4,40,128]{2,1,0:T(8,128)S(1)}, f32...) custom-call(f32[19,4,32,128]{3,2,1,0:T(8,128)S(1)} %copy-done, s32[4,32,128]{2,1,0:T(8,128)S(1)} %copy-done.1, ...), custom_call_target="tpu_custom_call" | custom-call | tf_op jit(solution)/shard_map/first/pallas_call | solution.py:463
  12.5 0.1 collective-permute-start.2
  12.6 8.6 %collective-permute-start.3 = (f32[9,40,128]{2,1,0:T(8,128)S(1)}, f32[9,40,128]{2,1,0:T(8,128)S(1)}, u32[]{:S(2)}, u32[]{:S(2)}) collective-permute-start(f32[9,40,128]{2,1,0:T(8,128)S(1)} %get-tuple-element.23), channel_id=1, source_target_pairs={{8,16},{16,8},{24,32},{32,24},{40,48},{48,40},{56,64},{64,56},{72,... | collective-permute-start | bytes 552968 | tf_op jit(solution)/shard_map/ppermute | solution.py:453
  21.2 0.0 collective-permute-done.2.xa
  21.2 5.0 %collective-permute-done.3.xb = f32[9,40,128]{2,1,0:T(8,128)S(1)} collective-permute-done((f32[9,40,128]{2,1,0:T(8,128)S(1)}, f32[9,40,128]{2,1,0:T(8,128)S(1)}, u32[]{:S(2)}, u32[]{:S(2)}) %collective-permute-start.3) | collective-permute-done | bytes 184352 | tf_op jit(solution)/shard_map/ppermute | solution.py:453
  26.2 2.1 %middle.1 = (f32[19,4,40,128]{3,2,1,0:T(8,128)S(1)}, f32[4,40,128]{2,1,0:T(8,128)S(1)}, f32[4,40,128]{2,1,0:T(8,128)S(1)}, f32[2,40,128]{2,1,0:T(8,128)S(1)}, f3...) custom-call(f32[19,4,40,128]{3,2,1,0:T(8,128)S(1)} %get-tuple-element.18.s, f32[4,40,128]{2,1,0:T(8,128)S(1)} %get-tuple-element.19.rho, ...), custom_call_target="tpu_custom_call" | custom-call | tf_op jit(solution)/shard_map/middle/pallas_call | solution.py:473
  28.4 0.1 collective-permute-start.4
  28.5 6.2 %collective-permute-start.5 = (f32[8,40,128]{2,1,0:T(8,128)S(1)}, f32[8,40,128]{2,1,0:T(8,128)S(1)}, u32[]{:S(2)}, u32[]{:S(2)}) collective-permute-start(f32[8,40,128]{2,1,0:T(8,128)S(1)} %get-tuple-element.29), channel_id=1, source_target_pairs={{8,16},{16,8},{24,32},{32,24},{40,48},{48,40},{56,64},{64,56},{72,... | collective-permute-start | bytes 491528 | tf_op jit(solution)/shard_map/ppermute | solution.py:453
  34.7 0.0 collective-permute-done.4.xa
  34.7 4.8 %collective-permute-done.5.xb = f32[8,40,128]{2,1,0:T(8,128)S(1)} collective-permute-done((f32[8,40,128]{2,1,0:T(8,128)S(1)}, f32[8,40,128]{2,1,0:T(8,128)S(1)}, u32[]{:S(2)}, u32[]{:S(2)}) %collective-permute-start.5) | collective-permute-done | bytes 163872 | tf_op jit(solution)/shard_map/ppermute | solution.py:453
  39.4 2.7 %last.1 = (f32[19,4,32,128]{3,2,1,0:T(8,128)}, f32[4,32,128]{2,1,0:T(8,128)}) custom-call(f32[19,4,40,128]{3,2,1,0:T(8,128)S(1)} %get-tuple-element.24.s, f32[4,40,128]{2,1,0:T(8,128)S(1)} %get-tuple-element.25.rho, f32[4,40,128]{2,1,0:T(8,128)S(1)} %get-tuple-element.20.fl, f32[4,40,128]{2,1,0:T(8,128)S(1)} %get-tuple-element.26.p_in, ...), custom_call_target="tpu_custom_call" | custom-call | tf_op jit(solution)/shard_map/last/pallas_call | solution.py:480
Async XLA Ops:
  0.6 1.3 %copy-start = (f32[19,4,32,128]{3,2,1,0:T(8,128)S(1)}, f32[19,4,32,128]{3,2,1,0:T(8,128)}, u32[]{:S(2)}) copy-start(f32[19,4,32,128]{3,2,1,0:T(8,128)} %pops.3) | copy-start | bytes 3735556
  1.9 0.8 %copy-start.1 = (s32[4,32,128]{2,1,0:T(8,128)S(1)}, s32[4,32,128]{2,1,0:T(8,128)}, u32[]{:S(2)}) copy-start(s32[4,32,128]{2,1,0:T(8,128)} %labels.3) | copy-start | bytes 196612
  2.8 0.8 %copy-start.2 = (s32[4,32,128]{2,1,0:T(8,128)S(1)}, s32[4,32,128]{2,1,0:T(8,128)}, u32[]{:S(2)}) copy-start(s32[4,32,128]{2,1,0:T(8,128)} %solid.3) | copy-start | bytes 196612
  3.7 5.3 %collective-permute-start = (f32[256,128]{1,0:T(8,128)S(1)}, f32[256,128]{1,0:T(8,128)S(1)}, u32[]{:S(2)}, u32[]{:S(2)}) collective-permute-start(f32[256,128]{1,0:T(8,128)S(1)} %get-tuple-element.16), channel_id=1, source_target_pairs={{0,1},{1,0},{2,3},{3,2},{4,5},{5,4},{6,7},{7,6},{8,9},{9,8},{10,11... | collective-permute-start | bytes 393224 | tf_op jit(solution)/shard_map/ppermute | solution.py:454
  4.5 7.1 %collective-permute-start.1 = (f32[256,128]{1,0:T(8,128)S(1)}, f32[256,128]{1,0:T(8,128)S(1)}, u32[]{:S(2)}, u32[]{:S(2)}) collective-permute-start(f32[256,128]{1,0:T(8,128)S(1)} %get-tuple-element.17), channel_id=1, source_target_pairs={{1,2},{2,1},{3,4},{4,3},{5,6},{6,5},{7,0},{0,7},{9,10},{10,9},{11,... | collective-permute-start | bytes 393224 | tf_op jit(solution)/shard_map/ppermute | solution.py:453
  12.5 8.7 %collective-permute-start.2 = (f32[9,40,128]{2,1,0:T(8,128)S(1)}, f32[9,40,128]{2,1,0:T(8,128)S(1)}, u32[]{:S(2)}, u32[]{:S(2)}) collective-permute-start(f32[9,40,128]{2,1,0:T(8,128)S(1)} %get-tuple-element.22), channel_id=1, source_target_pairs={{0,8},{8,0},{16,24},{24,16},{32,40},{40,32},{48,56},{56,48},{64,72... | collective-permute-start | bytes 552968 | tf_op jit(solution)/shard_map/ppermute | solution.py:454
  12.6 13.6 %collective-permute-start.3 = (f32[9,40,128]{2,1,0:T(8,128)S(1)}, f32[9,40,128]{2,1,0:T(8,128)S(1)}, u32[]{:S(2)}, u32[]{:S(2)}) collective-permute-start(f32[9,40,128]{2,1,0:T(8,128)S(1)} %get-tuple-element.23), channel_id=1, source_target_pairs={{8,16},{16,8},{24,32},{32,24},{40,48},{48,40},{56,64},{64,56},{72,... | collective-permute-start | bytes 552968 | tf_op jit(solution)/shard_map/ppermute | solution.py:453
  28.4 6.3 %collective-permute-start.4 = (f32[8,40,128]{2,1,0:T(8,128)S(1)}, f32[8,40,128]{2,1,0:T(8,128)S(1)}, u32[]{:S(2)}, u32[]{:S(2)}) collective-permute-start(f32[8,40,128]{2,1,0:T(8,128)S(1)} %get-tuple-element.28), channel_id=1, source_target_pairs={{0,8},{8,0},{16,24},{24,16},{32,40},{40,32},{48,56},{56,48},{64,72... | collective-permute-start | bytes 491528 | tf_op jit(solution)/shard_map/ppermute | solution.py:454
  28.5 11.0 %collective-permute-start.5 = (f32[8,40,128]{2,1,0:T(8,128)S(1)}, f32[8,40,128]{2,1,0:T(8,128)S(1)}, u32[]{:S(2)}, u32[]{:S(2)}) collective-permute-start(f32[8,40,128]{2,1,0:T(8,128)S(1)} %get-tuple-element.29), channel_id=1, source_target_pairs={{8,16},{16,8},{24,32},{32,24},{40,48},{48,40},{56,64},{64,56},{72,... | collective-permute-start | bytes 491528 | tf_op jit(solution)/shard_map/ppermute | solution.py:453
where the time goes:
time: 42.3 us; the launch traced here: 42.1 us
  starting transfers between devices  18.2 us (43%)
  waiting for transfers between devices  14.5 us (34%)
  Pallas kernels  5.76 us (14%)
  local copies, waits for them, and re-layouts  2.96 us (7%)
  between operations  0.68 us (2%)
    ppermute x3, starting transfers between devices, swap(): got_b = lax.ppermute(b, axis, pairs(count, 1))  17.2 us
    ppermute x3, waiting for transfers between devices, swap(): got_b = lax.ppermute(b, axis, pairs(count, 1))  12.4 us
    unnamed x6, local copies, waits for them, and re-layouts  2.96 us
    pallas_call x1, Pallas kernels, on_device(): call(last_kernel, 7, [shaped(19, NXL, NYL, 128), shaped(NXL, NYL, 128)],...  2.67 us
    pallas_call x1, Pallas kernels, on_device(): call(middle_kernel, 6, [shaped(19, NXL, EXT, 128)] + [shaped(NXL, EXT, 12...  2.15 us
    ppermute x3, waiting for transfers between devices, swap(): got_a = lax.ppermute(a, axis, pairs(count, 0))  2.09 us
    ppermute x3, starting transfers between devices, swap(): got_a = lax.ppermute(a, axis, pairs(count, 0))  1.02 us
    pallas_call x1, Pallas kernels, on_device(): call(first_kernel, 5, [shaped(19, NXL, EXT, 128)] + [shaped(NXL, EXT, 128...  0.86 us
  transfers between devices with their start and end apart: 6, of which 4 were waited for; matrix products, arithmetic and copies ran while one was open for 0% of the time, Pallas kernels for 0%

commit v1 on v0

--- a/solution.py
+++ b/solution.py
@@ -199,8 +199,94 @@
     return lax.broadcasted_iota(jnp.int32, (8, 128), 0) + (8 * t - 4)
 
 
-def pack_y_kernel(pops, labels, solid, out_a, out_b):
-    odd = lax.axis_index("gy") % 2
+def face(high):
+    a = jnp.where(high, NXL - 1, 0)
+    b = jnp.where(high, NXL - 2, 1)
+    c = jnp.where(high, NXL - 3, 2)
+    out = jnp.where(high, 5, 0)
+    back = jnp.where(high, 0, 5)
+    return a, b, c, out, back
+
+
+def build_message(msg, high, tiles, s, rho, fl, ph, fp, red):
+    a, b, c, out, back = face(high)
+    gout = jnp.where(high, 3, 0)
+    gback = jnp.where(high, 0, 3)
+    for n, t in enumerate(tiles):
+        rows = pl.ds(8 * t, 8)
+        to = pl.ds(8 * n, 8)
+        row = ROW0 + 8 * t
+        for j in range(5):
+            msg[j, to, :] = s[out + j, a, rows, :]
+        for j in range(9):
+            msg[5 + j, to, :] = s[10 + j, a, rows, :]
+        total = None
+        for j in range(5):
+            ey = DIRS[j][1]
+            shifted = pl.ds(row - ey, 8)
+            msg[14 + j, to, :] = fp[out + j, b + 1, shifted, :]
+            v = fp[out + j, c + 1, shifted, :] + fp[back + j, a + 1, shifted, :]
+            total = v if total is None else total + v
+        for j in range(9):
+            total = total + fp[10 + j, b + 1, pl.ds(row - DIRS[10 + j][1], 8), :]
+        moved, rsum = None, None
+        for j in range(3):
+            shifted = pl.ds(row - GROUPS[j][1], 8)
+            v = red[gout + j, b + 1, shifted, :]
+            moved = v if moved is None else moved + v
+            v = (red[gout + j, c + 1, shifted, :] + red[gback + j, a + 1, shifted, :]) + red[
+                6 + j, b + 1, shifted, :
+            ]
+            rsum = v if rsum is None else rsum + v
+        msg[19, to, :] = rho[a, rows, :]
+        msg[20, to, :] = ph[a + 2, pl.ds(row, 8), :]
+        msg[21, to, :] = ph[b + 2, pl.ds(row, 8), :]
+        msg[22, to, :] = fl[a, rows, :]
+        msg[23, to, :] = moved
+        msg[24, to, :] = total
+        msg[25, to, :] = rsum
+
+
+def inner_step(tiles, s, rho, fl, ph, fp, red):
+    def plane(x, carry):
+        for t in tiles:
+            rows = pl.ds(8 * t, 8)
+            finish(
+                DIRS, lambda d: s[POS[d], x, rows, :], ph, rho[x, rows, :],
+                fl[x, rows, :], x + 1, ROW0 + 8 * t, fp, red,
+            )
+        return carry
+
+    lax.fori_loop(1, NXL - 1, plane, 0)
+    for x, base in ((0, 5), (NXL - 1, 0)):
+        for t in tiles:
+            row = ROW0 + 8 * t
+            frac = 0.5 + 0.5 * ph[x + 2, pl.ds(row, 8), :]
+            sums = {}
+            for d in DIRS[base:base + 5]:
+                v = s[POS[d], x, pl.ds(8 * t, 8), :]
+                fp[POS[d], x + 1, pl.ds(row, 8), :] = zroll(v, d[2])
+                r = zroll(frac * v, d[2])
+                sums[d[:2]] = r if d[:2] not in sums else sums[d[:2]] + r
+            for g, r in sums.items():
+                red[GPOS[g], x + 1, pl.ds(row, 8), :] = r
+
+
+def start_kernel(pops_hbm, labels_hbm, solid_hbm, ya, yb, s, rho, fl, ph, fp, red, xa, xb,
+                 pops, labels, solid, sems):
+    gy = lax.axis_index("gy")
+    odd = gy % 2
+    copies = [
+        pltpu.make_async_copy(labels_hbm, labels, sems.at[0]),
+        pltpu.make_async_copy(solid_hbm, solid, sems.at[1]),
+    ] + [
+        pltpu.make_async_copy(pops_hbm.at[:, x], pops.at[:, x], sems.at[2 + x])
+        for x in range(NXL)
+    ]
+    for c in copies:
+        c.start()
+    for c in copies:
+        c.wait()
 
     def pack(out, high):
         for i in range(19):
@@ -215,16 +301,45 @@
 
     @pl.when(odd == 0)
     def _():
-        pack(out_a, True)
-        pack(out_b, False)
+        pack(ya, True)
+        pack(yb, False)
 
     @pl.when(odd == 1)
     def _():
-        pack(out_a, False)
-        pack(out_b, True)
-
-
-def first_kernel(pops, labels, solid, ya, yb, s_out, rho_out, fl_out, ph_out, xa, xb, raw, aux):
+        pack(ya, False)
+        pack(yb, True)
+
+    low_edge = gy == 0
+    high_edge = gy == lax.axis_size("gy") - 1
+
+    def plane(x, carry):
+        for t in range(NYL // 8):
+            own = pl.ds(8 * t, 8)
+            rows = pl.ds(8 * t + 4, 8)
+            f = {d: pops[REF_OF[k], x, own, :] for k, d in enumerate(DIRS)}
+            is_solid = solid[x, own, :] > 0
+            y = lax.broadcasted_iota(jnp.int32, (8, 128), 0) + 8 * t
+            if t == 0:
+                is_solid = is_solid | ((y == 0) & low_edge)
+            if t == NYL // 8 - 1:
+                is_solid = is_solid | ((y == NYL - 1) & high_edge)
+            relaxed, total = collide(f)
+            for d in DIRS:
+                s[POS[d], x, rows, :] = jnp.where(is_solid, f[neg(d)], relaxed[d])
+            rho[x, rows, :] = total
+            fl[x, rows, :] = jnp.where(is_solid, 0.0, 1.0)
+            ph[x + 2, pl.ds(ROW0 + 4 + 8 * t, 8), :] = jnp.where(labels[x, own, :] > 0, 1.0, -1.0)
+        return carry
+
+    lax.fori_loop(0, NXL, plane, 0)
+    inner_step(range(NT), s, rho, fl, ph, fp, red)
+    low_a = lax.axis_index("gx") % 2 == 1
+    build_message(xb, low_a, (1, 2, 3), s, rho, fl, ph, fp, red)
+    build_message(xa, jnp.logical_not(low_a), (1, 2, 3), s, rho, fl, ph, fp, red)
+
+
+def edge_kernel(ya, yb, s_in, rho_in, fl_in, ph_in, fp_in, red_in,
+                s, rho, fl, ph, fp, red, xd, xc, raw):
     gy = lax.axis_index("gy")
     odd = gy % 2
     low_edge = gy == 0
@@ -232,12 +347,11 @@
 
     def unpack(src, top):
         r = 1 if top else 4
-        for i in range(19):
-            for x in range(NXL):
+        for x in range(NXL):
+            for i in range(19):
                 raw[i, x, pl.ds(r, 3), :] = src[pl.ds(i * 12 + x * 3, 3), :]
-        for x in range(NXL):
-            aux[0, x, pl.ds(0 if top else 4, 4), :] = src[pl.ds(228 + x * 4, 4), :]
-            aux[1, x, pl.ds(r, 3), :] = src[pl.ds(244 + x * 3, 3), :]
+            raw[19, x, pl.ds(0 if top else 4, 4), :] = src[pl.ds(228 + x * 4, 4), :]
+            raw[20, x, pl.ds(r, 3), :] = src[pl.ds(244 + x * 3, 3), :]
 
     @pl.when(odd == 0)
     def _():
@@ -249,125 +363,88 @@
         unpack(ya, True)
         unpack(yb, False)
 
+    row = lax.broadcasted_iota(jnp.int32, (8, 128), 0)
+    inside = jnp.where(row < 4, jnp.where(low_edge, 0, 1), jnp.where(high_edge, 0, 1)) > 0
+
     def plane(x, carry):
-        for t in range(NT):
-            def pick(own, halo):
-                if 1 <= t <= 3:
-                    return own(8 * t - 4, 8)
-                if t == 0:
-                    return jnp.concatenate([halo()[0:4], own(0, 4)], axis=0)
-                return jnp.concatenate([own(NYL - 4, 4), halo()[4:8]], axis=0)
-
-            f = {}
-            for k, d in enumerate(DIRS):
-                ref = REF_OF[k]
-                f[d] = pick(
-                    lambda r, n: pops[ref, x, pl.ds(r, n), :], lambda: raw[ref, x]
-                )
-            lab = pick(
-                lambda r, n: labels[x, pl.ds(r, n), :].astype(jnp.float32),
-                lambda: aux[0, x],
-            )
-            sol = pick(
-                lambda r, n: solid[x, pl.ds(r, n), :].astype(jnp.float32),
-                lambda: aux[1, x],
-            )
-            y = tile_rows(t)
-            is_solid = sol > 0.5
-            p = jnp.where(lab > 0.5, 1.0, -1.0)
-            inside = None
-            if t == 0:
-                is_solid = is_solid | ((y == 0) & low_edge)
-                inside = (y >= 0) | jnp.logical_not(low_edge)
-            if t == NT - 1:
-                is_solid = is_solid | ((y == NYL - 1) & high_edge)
-                inside = (y < NYL) | jnp.logical_not(high_edge)
-            relaxed, rho = collide(f)
-            fl = jnp.where(is_solid, 0.0, 1.0)
-            if inside is not None:
-                fl = jnp.where(inside, fl, 0.0)
-                p = jnp.where(inside, p, 0.0)
-            rows = pl.ds(8 * t, 8)
-            for d in DIRS:
-                v = jnp.where(is_solid, f[neg(d)], relaxed[d])
-                if inside is not None:
-                    v = jnp.where(inside, v, 0.0)
-                s_out[POS[d], x, rows, :] = v
-            rho_out[x, rows, :] = rho
-            fl_out[x, rows, :] = fl
-            ph_out[x, rows, :] = p
+        def put(ref, base, v):
+            ref[pl.ds(base, 4), :] = v[0:4]
+            ref[pl.ds(base + NYL + 4, 4), :] = v[4:8]
+
+        f = {d: raw[REF_OF[k], x] for k, d in enumerate(DIRS)}
+        is_solid = raw[20, x] > 0.5
+        relaxed, total = collide(f)
+        for d in DIRS:
+            v = jnp.where(is_solid, f[neg(d)], relaxed[d])
+            put(s.at[POS[d], x], 0, jnp.where(inside, v, 0.0))
+        put(rho.at[x], 0, total)
+        put(fl.at[x], 0, jnp.where(inside & jnp.logical_not(is_solid), 1.0, 0.0))
+        p = jnp.where(raw[19, x] > 0.5, 1.0, -1.0)
+        put(ph.at[x + 2], ROW0, jnp.where(inside, p, 0.0))
         return carry
 
     lax.fori_loop(0, NXL, plane, 0)
-    pack_x(s_out, ph_out, rho_out, fl_out, xa, xb)
-
-
-def pack_x(s, ph, rho, fl, xa, xb):
-    odd = lax.axis_index("gx") % 2
-
-    def pack(out, high):
-        base = jnp.where(high, 5, 0)
-        face = jnp.where(high, NXL - 1, 0)
-        second = jnp.where(high, NXL - 2, 1)
-        for j in range(5):
-            out[j] = s[base + j, face]
-        out[5] = rho[face]
-        out[6] = ph[face]
-        out[7] = ph[second]
-        if fl is not None:
-            out[8] = fl[face]
-
-    pack(xa, odd == 0)
-    pack(xb, odd == 1)
-
-
-def unpack_x(xa, xb, hx, ph, n):
-    odd = lax.axis_index("gx") % 2
-
-    def put(src, side):
-        for j in range(n):
-            if j not in (6, 7):
-                hx[side, j] = src[j]
+    inner_step((0, NT - 1), s, rho, fl, ph, fp, red)
+    low_a = lax.axis_index("gx") % 2 == 1
+    build_message(xc, low_a, (0, NT - 1), s, rho, fl, ph, fp, red)
+    build_message(xd, jnp.logical_not(low_a), (0, NT - 1), s, rho, fl, ph, fp, red)
+
+
+def last_kernel(s, rho, fl, ph_in, fp_in, red_in, xa, xb, xc, xd,
+                pops_out, phase_out, ph, fp, red, hx, s2, rho2):
+    gy = lax.axis_index("gy")
+    low_edge = gy == 0
+    high_edge = gy == lax.axis_size("gy") - 1
+    side_a = 1 - lax.axis_index("gx") % 2
+
+    def put(src, side, tiles):
         near = jnp.where(side == 1, NXL + 2, 1)
         far = jnp.where(side == 1, NXL + 3, 0)
-        ph[near, pl.ds(ROW0, EXT), :] = src[6]
-        ph[far, pl.ds(ROW0, EXT), :] = src[7]
-
-    put(xa, jnp.where(odd == 0, 1, 0))
-    put(xb, jnp.where(odd == 0, 0, 1))
-
-
-def interface(s, rho, fl, hx, hfl, ph, fp, red):
-    def plane(x, carry):
+        for n, t in enumerate(tiles):
+            part = pl.ds(8 * n, 8)
+            for j in range(26):
+                if j not in (20, 21):
+                    hx[side, j, pl.ds(8 * t, 8), :] = src[j, part, :]
+            ph[near, pl.ds(ROW0 + 8 * t, 8), :] = src[20, part, :]
+            ph[far, pl.ds(ROW0 + 8 * t, 8), :] = src[21, part, :]
+
+    put(xa, side_a, (1, 2, 3))
+    put(xd, side_a, (0, NT - 1))
+    put(xb, 1 - side_a, (1, 2, 3))
+    put(xc, 1 - side_a, (0, NT - 1))
+
+    def mask(t):
+        y = tile_rows(t)
+        if t == 0:
+            return (y >= 0) | jnp.logical_not(low_edge)
+        if t == NT - 1:
+            return (y < NYL) | jnp.logical_not(high_edge)
+        return None
+
+    sides = ((0, 0, DIRS[5:10], DIRS[0:5]), (1, NXL + 1, DIRS[0:5], DIRS[5:10]))
+
+    for x in (0, NXL - 1):
         for t in range(NT):
             rows = pl.ds(8 * t, 8)
             finish(
                 DIRS, lambda d: s[POS[d], x, rows, :], ph, rho[x, rows, :],
                 fl[x, rows, :], x + 1, ROW0 + 8 * t, fp, red,
             )
-        return carry
-
-    lax.fori_loop(0, NXL, plane, 0)
-    for side, plane_index, dirs in ((0, 0, DIRS[5:10]), (1, NXL + 1, DIRS[0:5])):
+    for side, plane_index, towards, back in sides:
         for t in range(NT):
             rows = pl.ds(8 * t, 8)
+
+            def value(d):
+                if d in back:
+                    return 0.0
+                if d in towards:
+                    return hx[side, towards.index(d), rows, :]
+                return hx[side, 5 + POS[d] - 10, rows, :]
+
             finish(
-                dirs, lambda d: hx[side, dirs.index(d), rows, :], ph, hx[side, 5, rows, :],
-                hfl[side, rows, :], plane_index, ROW0 + 8 * t, fp, red,
+                DIRS, value, ph, hx[side, 19, rows, :], hx[side, 22, rows, :],
+                plane_index, ROW0 + 8 * t, fp, red,
             )
-
-
-def middle_kernel(s, rho, fl, p_in, xa, xb, s_out, rho_out, ph_out, hfl_out, xa_out, xb_out,
-                  hx, ph, fp, red):
-    gy = lax.axis_index("gy")
-    low_edge = gy == 0
-    high_edge = gy == lax.axis_size("gy") - 1
-    unpack_x(xa, xb, hx, ph, 9)
-    for x in range(NXL):
-        ph[x + 2, pl.ds(ROW0, EXT), :] = p_in[x]
-    for side in range(2):
-        hfl_out[side] = hx[side, 8]
-    interface(s, rho, fl, hx, hfl_out, ph, fp, red)
 
     def plane(x, carry):
         for t in range(NT):
@@ -376,12 +453,7 @@
             f = {d: arrived(d, fp, x + 1, row) for d in DIRS}
             relaxed, total = collide(f)
             p = 2.0 * red_arrived(red, x + 1, row) / total - 1.0
-            y = tile_rows(t)
-            inside = None
-            if t == 0:
-                inside = (y >= 0) | jnp.logical_not(low_edge)
-            if t == NT - 1:
-                inside = (y < NYL) | jnp.logical_not(high_edge)
+            inside = mask(t)
             if inside is not None:
                 p = jnp.where(inside, p, 0.0)
             is_fluid = fl[x, rows, :] > 0.5
@@ -389,22 +461,70 @@
                 v = jnp.where(is_fluid, relaxed[d], f[neg(d)])
                 if inside is not None:
                     v = jnp.where(inside, v, 0.0)
-                s_out[POS[d], x, rows, :] = v
-            rho_out[x, rows, :] = total
-            ph_out[x, rows, :] = p
+                s2[POS[d], x + 1, rows, :] = v
+            rho2[x + 1, rows, :] = total
+            ph[x + 2, pl.ds(row, 8), :] = p
         return carry
 
     lax.fori_loop(0, NXL, plane, 0)
-    pack_x(s_out, ph_out, rho_out, None, xa_out, xb_out)
-
-
-def last_kernel(s, rho, fl, p_in, hfl, xa, xb, pops_out, phase_out, hx, ph, fp, red):
-    unpack_x(xa, xb, hx, ph, 8)
-    for x in range(NXL):
-        ph[x + 2, pl.ds(ROW0, EXT), :] = p_in[x]
-    interface(s, rho, fl, hx, hfl, ph, fp, red)
-
-    def plane(x, carry):
+    for side, index, towards, back in sides:
+        near, far = (NXL + 2, NXL + 3) if side == 1 else (1, 0)
+        for t in range(NT):
+            row = ROW0 + 8 * t
+            rows = pl.ds(8 * t, 8)
+            f = {}
+            for d in DIRS:
+                if d in towards:
+                    f[d] = hx[side, 14 + towards.index(d), rows, :]
+                else:
+                    f[d] = arrived(d, fp, index, row)
+            relaxed, total = collide(f)
+            rsum = hx[side, 23, rows, :]
+            rfar = hx[side, 25, rows, :]
+            for g in GROUPS:
+                shifted = pl.ds(row - g[1], 8)
+                if g[0] != towards[0][0]:
+                    rsum = rsum + red[GPOS[g], index - g[0], shifted, :]
+                if g[0] == back[0][0]:
+                    rfar = rfar + red[GPOS[g], index, shifted, :]
+            ffar = hx[side, 24, rows, :]
+            for d in back:
+                ffar = ffar + fp[POS[d], index, pl.ds(row - d[1], 8), :]
+            p = 2.0 * rsum / total - 1.0
+            pfar = 2.0 * rfar / ffar - 1.0
+            inside = mask(t)
+            if inside is not None:
+                p = jnp.where(inside, p, 0.0)
+                pfar = jnp.where(inside, pfar, 0.0)
+            is_fluid = hx[side, 22, rows, :] > 0.5
+            for d in towards:
+                v = jnp.where(is_fluid, relaxed[d], f[neg(d)])
+                if inside is not None:
+                    v = jnp.where(inside, v, 0.0)
+                s2[POS[d], index, rows, :] = v
+            rho2[index, rows, :] = total
+            ph[near, pl.ds(row, 8), :] = p
+            ph[far, pl.ds(row, 8), :] = pfar
+
+    def second(x, carry):
+        for t in range(NT):
+            rows = pl.ds(8 * t, 8)
+            finish(
+                DIRS, lambda d: s2[POS[d], x + 1, rows, :], ph, rho2[x + 1, rows, :],
+                fl[x, rows, :], x + 1, ROW0 + 8 * t, fp, red,
+            )
+        return carry
+
+    lax.fori_loop(0, NXL, second, 0)
+    for side, index, towards, back in sides:
+        for t in range(NT):
+            rows = pl.ds(8 * t, 8)
+            finish(
+                towards, lambda d: s2[POS[d], index, rows, :], ph, rho2[index, rows, :],
+                hx[side, 22, rows, :], index, ROW0 + 8 * t, fp, red,
+            )
+
+    def final(x, carry):
         for t in range(NYL // 8):
             row = ROW0 + 4 + 8 * t
             rows = pl.ds(8 * t, 8)
@@ -416,26 +536,29 @@
             phase_out[x, rows, :] = 2.0 * red_arrived(red, x + 1, row) / total - 1.0
         return carry
 
-    lax.fori_loop(0, NXL, plane, 0)
+    lax.fori_loop(0, NXL, final, 0)
 
 
 F32 = jnp.float32
 VM = pl.BlockSpec(memory_space=pltpu.VMEM)
-PARAMS = pltpu.CompilerParams(vmem_limit_bytes=40 * 1024 * 1024)
+HB = pl.BlockSpec(memory_space=pltpu.HBM)
+MIB = 1024 * 1024
 
 
 def shaped(*dims):
     return jax.ShapeDtypeStruct(dims, F32)
 
 
-def call(kernel, n_in, outs, scratch, name):
+def call(kernel, in_specs, outs, scratch, name, aliases=None, vmem=40, cost=0):
     return pl.pallas_call(
         kernel,
-        in_specs=[VM] * n_in,
+        in_specs=in_specs,
         out_specs=[VM] * len(outs),
         out_shape=outs,
-        scratch_shapes=[pltpu.VMEM(d, F32) for d in scratch],
-        compiler_params=PARAMS,
+        scratch_shapes=scratch,
+        input_output_aliases=aliases or {},
+        compiler_params=pltpu.CompilerParams(vmem_limit_bytes=vmem * MIB),
+        cost_estimate=pl.CostEstimate(flops=cost, bytes_accessed=cost, transcendentals=0),
         name=name,
     )
 
@@ -448,38 +571,45 @@
     return out
 
 
-def swap(a, b, axis):
-    count = lax.axis_size(axis)
-    got_b = lax.ppermute(b, axis, pairs(count, 1))
-    got_a = lax.ppermute(a, axis, pairs(count, 0))
-    return got_a, got_b
+def swap(value, axis, first):
+    return lax.ppermute(value, axis, pairs(lax.axis_size(axis), first))
 
 
 def on_device(populations, labels, solid_mask):
-    ya, yb = call(pack_y_kernel, 3, [shaped(YROWS, 128)] * 2, [], "pack_y")(
-        populations, labels, solid_mask
-    )
-    ya, yb = swap(ya, yb, "gy")
-    s, rho, fl, ph, xa, xb = call(
-        first_kernel, 5,
-        [shaped(19, NXL, EXT, 128)] + [shaped(NXL, EXT, 128)] * 3 + [shaped(9, EXT, 128)] * 2,
-        [(19, NXL, 8, 128), (2, NXL, 8, 128)], "first",
-    )(populations, labels, solid_mask, ya, yb)
-    xa, xb = swap(xa, xb, "gx")
-    work = [
-        (2, 9, EXT, 128), (NXL + 4, SROWS, 128), (19, NXL + 2, SROWS, 128),
-        (9, NXL + 2, SROWS, 128),
+    state = [
+        shaped(19, NXL, EXT, 128), shaped(NXL, EXT, 128), shaped(NXL, EXT, 128),
+        shaped(NXL + 4, SROWS, 128), shaped(19, NXL + 2, SROWS, 128),
+        shaped(9, NXL + 2, SROWS, 128),
     ]
-    s, rho, ph, hfl, xa, xb = call(
-        middle_kernel, 6,
-        [shaped(19, NXL, EXT, 128)] + [shaped(NXL, EXT, 128)] * 2
-        + [shaped(2, EXT, 128)] + [shaped(8, EXT, 128)] * 2,
-        work, "middle",
-    )(s, rho, fl, ph, xa, xb)
-    xa, xb = swap(xa, xb, "gx")
-    return call(
-        last_kernel, 7, [shaped(19, NXL, NYL, 128), shaped(NXL, NYL, 128)], work, "last",
-    )(s, rho, fl, ph, hfl, xa, xb)
+    got = call(
+        start_kernel, [HB] * 3, [shaped(YROWS, 128)] * 2 + state + [shaped(26, 24, 128)] * 2,
+        [
+            pltpu.VMEM((19, NXL, NYL, 128), F32), pltpu.VMEM((NXL, NYL, 128), jnp.int32),
+            pltpu.VMEM((NXL, NYL, 128), jnp.int32), pltpu.SemaphoreType.DMA((6,)),
+        ],
+        "start", vmem=40,
+    )(*[pltpu.with_memory_space_constraint(v, pltpu.HBM) for v in (populations, labels, solid_mask)])
+    ya, yb, *mid, xa, xb = got
+    xb = swap(xb, "gx", 1)
+    xa = swap(xa, "gx", 0)
+    ya = swap(ya, "gy", 0)
+    yb = swap(yb, "gy", 1)
+    *mid, xd, xc = call(
+        edge_kernel, [VM] * 8, state + [shaped(26, 16, 128)] * 2,
+        [pltpu.VMEM((21, NXL, 8, 128), F32)], "edge", {2 + i: i for i in range(6)},
+    )(ya, yb, *mid)
+    xc = swap(xc, "gx", 1)
+    xd = swap(xd, "gx", 0)
+    out = call(
+        last_kernel, [VM] * 10,
+        [shaped(19, NXL, NYL, 128), shaped(NXL, NYL, 128)] + state[3:],
+        [
+            pltpu.VMEM((2, 26, EXT, 128), F32), pltpu.VMEM((19, NXL + 2, EXT, 128), F32),
+            pltpu.VMEM((NXL + 2, EXT, 128), F32),
+        ],
+        "last", {3: 2, 4: 3, 5: 4},
+    )(*mid, xa, xb, xc, xd)
+    return out[0], out[1]
 
 
 def solution(mesh):

time: 42.3 us -> 34.8 us (0.82)
  the two profiles are of different devices: /device:TPU:24 before, /device:TPU:8 now
where the time goes in v1:
time: 34.8 us; the launch traced here: 34.7 us
  starting transfers between devices  13.3 us (38%)
  waiting for transfers between devices  11.8 us (34%)
  Pallas kernels  8.94 us (26%)
  between operations  0.65 us (2%)
    ppermute x6, starting transfers between devices, swap(): return lax.ppermute(value, axis, pairs(lax.axis_size(axis), first))  13.3 us
    ppermute x6, waiting for transfers between devices, swap(): return lax.ppermute(value, axis, pairs(lax.axis_size(axis), first))  11.8 us
    pallas_call x1, Pallas kernels, on_device(): call(last_kernel, [VM] * 10, [shaped(19, NXL, NYL, 128), shaped(NXL, NYL,...  5.43 us
    pallas_call x1, Pallas kernels, on_device(): call(start_kernel, [HB] * 3, [shaped(YROWS, 128)] * 2 + state + [shaped(2...  2.7 us
    pallas_call x1, Pallas kernels, on_device(): call(edge_kernel, [VM] * 8, state + [shaped(26, 16, 128)] * 2, [pltpu.VME...  0.8 us
  transfers between devices with their start and end apart: 6, of which 2 were waited for; matrix products, arithmetic and copies ran while one was open for 0% of the time, Pallas kernels for 2%

profile of v1, /device:TPU:8, one launch (start us, length us, event | category | flops | bytes accessed | tf_op | source)
XLA Modules:
  0.0 34.7 jit_solution(11516965109373997923)
XLA Ops:
  0.6 2.7 %start.1 = (f32[256,128]{1,0:T(8,128)S(1)}, f32[256,128]{1,0:T(8,128)S(1)}, f32[19,4,40,128]{3,2,1,0:T(8,128)S(1)}, f32[4,40,128]{2,1,0:T(8,128)S(1)}, f32[4,40,...) custom-call(f32[19,4,32,128]{3,2,1,0:T(8,128)} %pops_hbm.1, ...), custom_call_target="tpu_custom_call" | custom-call | tf_op jit(solution)/shard_map/start/pallas_call | solution.py:584
  3.3 2.3 %collective-permute-start = (f32[256,128]{1,0:T(8,128)S(1)}, f32[256,128]{1,0:T(8,128)S(1)}, u32[]{:S(2)}, u32[]{:S(2)}) collective-permute-start(f32[256,128]{1,0:T(8,128)S(1)} %get-tuple-element.22), channel_id=1, source_target_pairs={{0,1},{1,0},{2,3},{3,2},{4,5},{5,4},{6,7},{7,6},{8,9},{9,8},{10,11... | collective-permute-start | bytes 393224 | tf_op jit(solution)/shard_map/ppermute | solution.py:575
  5.6 0.7 %collective-permute-start.1 = (f32[256,128]{1,0:T(8,128)S(1)}, f32[256,128]{1,0:T(8,128)S(1)}, u32[]{:S(2)}, u32[]{:S(2)}) collective-permute-start(f32[256,128]{1,0:T(8,128)S(1)} %get-tuple-element.23), channel_id=1, source_target_pairs={{1,2},{2,1},{3,4},{4,3},{5,6},{6,5},{7,0},{0,7},{9,10},{10,9},{11,... | collective-permute-start | bytes 393224 | tf_op jit(solution)/shard_map/ppermute | solution.py:575
  6.3 0.0 collective-permute-start.2
  6.3 8.6 %collective-permute-start.3 = (f32[26,24,128]{2,1,0:T(8,128)S(1)}, f32[26,24,128]{2,1,0:T(8,128)S(1)}, u32[]{:S(2)}, u32[]{:S(2)}) collective-permute-start(f32[26,24,128]{2,1,0:T(8,128)S(1)} %get-tuple-element.37), channel_id=1, source_target_pairs={{8,16},{16,8},{24,32},{32,24},{40,48},{48,40},{56,64},{64,56},{72,... | collective-permute-start | bytes 958472 | tf_op jit(solution)/shard_map/ppermute | solution.py:575
  14.9 0.0 collective-permute-done.ya
  14.9 0.0 collective-permute-done.1.yb
  14.9 0.8 %edge.1 = (f32[19,4,40,128]{3,2,1,0:T(8,128)S(1)}, f32[4,40,128]{2,1,0:T(8,128)S(1)}, f32[4,40,128]{2,1,0:T(8,128)S(1)}, f32[8,56,128]{2,1,0:T(8,128)S(1)}, f32[...) custom-call(f32[256,128]{1,0:T(8,128)S(1)} %collective-permute-done., ...), custom_call_target="tpu_custom_call", output_to_operand_aliasing={{0}: (2, {}), {1}: (3, {}), {2}: (4, {}), {3}: (5, {}), {4}... | custom-call | tf_op jit(solution)/shard_map/edge/pallas_call | solution.py:597
  15.7 1.8 %collective-permute-start.4 = (f32[26,16,128]{2,1,0:T(8,128)S(1)}, f32[26,16,128]{2,1,0:T(8,128)S(1)}, u32[]{:S(2)}, u32[]{:S(2)}) collective-permute-start(f32[26,16,128]{2,1,0:T(8,128)S(1)} %get-tuple-element.38), channel_id=1, source_target_pairs={{8,16},{16,8},{24,32},{32,24},{40,48},{48,40},{56,64},{64,56},{72,... | collective-permute-start | bytes 638984 | tf_op jit(solution)/shard_map/ppermute | solution.py:575
  17.5 0.0 collective-permute-start.5
  17.5 0.0 collective-permute-done.2.xa
  17.5 4.1 %collective-permute-done.3.xb = f32[26,24,128]{2,1,0:T(8,128)S(1)} collective-permute-done((f32[26,24,128]{2,1,0:T(8,128)S(1)}, f32[26,24,128]{2,1,0:T(8,128)S(1)}, u32[]{:S(2)}, u32[]{:S(2)}) %collective-permute-start.3) | collective-permute-done | bytes 319520 | tf_op jit(solution)/shard_map/ppermute | solution.py:575
  21.6 7.7 %collective-permute-done.4.xc = f32[26,16,128]{2,1,0:T(8,128)S(1)} collective-permute-done((f32[26,16,128]{2,1,0:T(8,128)S(1)}, f32[26,16,128]{2,1,0:T(8,128)S(1)}, u32[]{:S(2)}, u32[]{:S(2)}) %collective-permute-start.4) | collective-permute-done | bytes 213024 | tf_op jit(solution)/shard_map/ppermute | solution.py:575
  29.2 0.0 collective-permute-done.5.xd
  29.2 5.4 %last.1 = (f32[19,4,32,128]{3,2,1,0:T(8,128)}, f32[4,32,128]{2,1,0:T(8,128)}, f32[8,56,128]{2,1,0:T(8,128)S(1)}, f32[19,6,56,128]{3,2,1,0:T(8,128)S(1)}, f32[9,6,56,128]{3,2,1,0:T(8,128)S(1)}) custom-call(f32[19,4,40,128]{3,2,1,0:T(8,128)S(1)} %get-tuple-element.30.s, ...), custom_call_target="tpu_custom_call", output_to_operand_aliasing={{2}: (3, {}), {3}: (4, {}), {4}: (5, {})} | custom-call | tf_op jit(solution)/shard_map/last/pallas_call | solution.py:603
Async XLA Ops:
  3.3 11.6 %collective-permute-start = (f32[256,128]{1,0:T(8,128)S(1)}, f32[256,128]{1,0:T(8,128)S(1)}, u32[]{:S(2)}, u32[]{:S(2)}) collective-permute-start(f32[256,128]{1,0:T(8,128)S(1)} %get-tuple-element.22), channel_id=1, source_target_pairs={{0,1},{1,0},{2,3},{3,2},{4,5},{5,4},{6,7},{7,6},{8,9},{9,8},{10,11... | collective-permute-start | bytes 393224 | tf_op jit(solution)/shard_map/ppermute | solution.py:575
  5.6 9.3 %collective-permute-start.1 = (f32[256,128]{1,0:T(8,128)S(1)}, f32[256,128]{1,0:T(8,128)S(1)}, u32[]{:S(2)}, u32[]{:S(2)}) collective-permute-start(f32[256,128]{1,0:T(8,128)S(1)} %get-tuple-element.23), channel_id=1, source_target_pairs={{1,2},{2,1},{3,4},{4,3},{5,6},{6,5},{7,0},{0,7},{9,10},{10,9},{11,... | collective-permute-start | bytes 393224 | tf_op jit(solution)/shard_map/ppermute | solution.py:575
  6.3 11.2 %collective-permute-start.2 = (f32[26,24,128]{2,1,0:T(8,128)S(1)}, f32[26,24,128]{2,1,0:T(8,128)S(1)}, u32[]{:S(2)}, u32[]{:S(2)}) collective-permute-start(f32[26,24,128]{2,1,0:T(8,128)S(1)} %get-tuple-element.36), channel_id=1, source_target_pairs={{0,8},{8,0},{16,24},{24,16},{32,40},{40,32},{48,56},{56,48},{64,72... | collective-permute-start | bytes 958472 | tf_op jit(solution)/shard_map/ppermute | solution.py:575
  6.3 15.3 %collective-permute-start.3 = (f32[26,24,128]{2,1,0:T(8,128)S(1)}, f32[26,24,128]{2,1,0:T(8,128)S(1)}, u32[]{:S(2)}, u32[]{:S(2)}) collective-permute-start(f32[26,24,128]{2,1,0:T(8,128)S(1)} %get-tuple-element.37), channel_id=1, source_target_pairs={{8,16},{16,8},{24,32},{32,24},{40,48},{48,40},{56,64},{64,56},{72,... | collective-permute-start | bytes 958472 | tf_op jit(solution)/shard_map/ppermute | solution.py:575
  15.7 13.5 %collective-permute-start.4 = (f32[26,16,128]{2,1,0:T(8,128)S(1)}, f32[26,16,128]{2,1,0:T(8,128)S(1)}, u32[]{:S(2)}, u32[]{:S(2)}) collective-permute-start(f32[26,16,128]{2,1,0:T(8,128)S(1)} %get-tuple-element.38), channel_id=1, source_target_pairs={{8,16},{16,8},{24,32},{32,24},{40,48},{48,40},{56,64},{64,56},{72,... | collective-permute-start | bytes 638984 | tf_op jit(solution)/shard_map/ppermute | solution.py:575
  17.5 11.8 %collective-permute-start.5 = (f32[26,16,128]{2,1,0:T(8,128)S(1)}, f32[26,16,128]{2,1,0:T(8,128)S(1)}, u32[]{:S(2)}, u32[]{:S(2)}) collective-permute-start(f32[26,16,128]{2,1,0:T(8,128)S(1)} %get-tuple-element.39), channel_id=1, source_target_pairs={{0,8},{8,0},{16,24},{24,16},{32,40},{40,32},{48,56},{56,48},{64,72... | collective-permute-start | bytes 638984 | tf_op jit(solution)/shard_map/ppermute | solution.py:575

commit v2 on v1

--- a/solution.py
+++ b/solution.py
@@ -42,9 +42,13 @@
     return pltpu.roll(v, shift % 128, 1)
 
 
-def collide(f):
+def collide(f, known=None, equilibrium=True):
     def pair(a, b):
         pa, pb = f[a], f[b]
+        if pb is None:
+            return pa, pa
+        if pa is None:
+            return pb, -pb
         return pa + pb, pa - pb
 
     s1, d1 = pair((1, 1, 0), (-1, -1, 0))
@@ -62,37 +66,44 @@
     jx = dx + (xyy + xzz)
     jy = dy + (xxy + yzz)
     jz = dz + (xxz + yyz)
-    mxx = ax + (xxyy + xxzz)
-    myy = ay + (xxyy + yyzz)
-    mzz = az + (xxzz + yyzz)
+    nxx = ax + (xxyy + xxzz)
+    nyy = ay + (xxyy + yyzz)
+    nzz = az + (xxzz + yyzz)
     rho = (f[(0, 0, 0)] + (ax + ay)) + (az + (xxyy + (xxzz + yyzz)))
-    inv = 1.0 / rho
-    ux, uy, uz = jx * inv, jy * inv, jz * inv
-    qx, qy, qz = jx * ux, jy * uy, jz * uz
-    third = rho * (1.0 / 3.0)
-    nxx = mxx - third - qx
-    nyy = myy - third - qy
-    nzz = mzz - third - qz
+    if known is not None:
+        rho, jx, jy, jz = rho + known[0], jx + known[1], jy + known[2], jz + known[3]
+    dxy, dxz, dyz = 0.3125 * xy, 0.3125 * xz, 0.3125 * yz
+    dxyy, dxzz, dxxy = 0.3 * xyy, 0.3 * xzz, 0.3 * xxy
+    dyzz, dxxz, dyyz = 0.3 * yzz, 0.3 * xxz, 0.3 * yyz
+    dxxyy, dxxzz, dyyzz = 0.35 * xxyy, 0.35 * xxzz, 0.35 * yyzz
+    if equilibrium:
+        inv = 1.0 / rho
+        ux, uy, uz = jx * inv, jy * inv, jz * inv
+        qx, qy, qz = jx * ux, jy * uy, jz * uz
+        third = rho * (1.0 / 3.0)
+        nxx = nxx - (third + qx)
+        nyy = nyy - (third + qy)
+        nzz = nzz - (third + qz)
+        dxy = 0.3125 * (xy - jx * uy)
+        dxz = 0.3125 * (xz - jx * uz)
+        dyz = 0.3125 * (yz - jy * uz)
+        kx, ky, kz = jx * 0.1, jy * 0.1, jz * 0.1
+        dxyy, dxzz = dxyy - kx, dxzz - kx
+        dxxy, dyzz = dxxy - ky, dyzz - ky
+        dxxz, dyyz = dxxz - kz, dyyz - kz
+        base = (0.35 / 9.0) * rho + (0.35 / 3.0) * (qx + qy + qz)
+        dxxyy = dxxyy - (base - 0.175 * qz)
+        dxxzz = dxxzz - (base - 0.175 * qy)
+        dyyzz = dyyzz - (base - 0.175 * qx)
     trace = nxx + nyy + nzz
     iso = trace * (-1.0 / 24.0)
     hxx = 0.625 * nxx + iso
     hyy = 0.625 * nyy + iso
     hzz = 0.625 * nzz + iso
-    dxy = 0.3125 * (xy - jx * uy)
-    dxz = 0.3125 * (xz - jx * uz)
-    dyz = 0.3125 * (yz - jy * uz)
-    kx, ky, kz = jx * 0.1, jy * 0.1, jz * 0.1
-    dxyy = 0.3 * xyy - kx
-    dxzz = 0.3 * xzz - kx
-    dxxy = 0.3 * xxy - ky
-    dyzz = 0.3 * yzz - ky
-    dxxz = 0.3 * xxz - kz
-    dyyz = 0.3 * yyz - kz
-    base = (0.35 / 9.0) * rho + (0.35 / 3.0) * (qx + qy + qz)
-    dxxyy = 0.35 * xxyy - (base - 0.175 * qz)
-    dxxzz = 0.35 * xxzz - (base - 0.175 * qy)
-    dyyzz = 0.35 * yyzz - (base - 0.175 * qx)
     out = {}
+
+    def less(d, v):
+        return -v if f[d] is None else f[d] - v
 
     def diagonal(quad, cross, la, lb, da, db):
         t1, t2 = quad + cross, quad - cross
@@ -101,10 +112,10 @@
         for sa, sb in ((1, 1), (-1, -1), (1, -1), (-1, 1)):
             e = tuple(sa * p + sb * q for p, q in zip(da, db))
             out_dirs.append(e)
-        out[out_dirs[0]] = f[out_dirs[0]] - (t1 + v1)
-        out[out_dirs[1]] = f[out_dirs[1]] - (t1 - v1)
-        out[out_dirs[2]] = f[out_dirs[2]] - (t2 + v2)
-        out[out_dirs[3]] = f[out_dirs[3]] - (t2 - v2)
+        out[out_dirs[0]] = less(out_dirs[0], t1 + v1)
+        out[out_dirs[1]] = less(out_dirs[1], t1 - v1)
+        out[out_dirs[2]] = less(out_dirs[2], t2 + v2)
+        out[out_dirs[3]] = less(out_dirs[3], t2 - v2)
 
     X, Y, Z = (1, 0, 0), (0, 1, 0), (0, 0, 1)
     diagonal(dxxyy, dxy, dxyy, dxxy, X, Y)
@@ -114,14 +125,14 @@
     def axis(half, q1, q2, l1, l2, d):
         even = half - 2.0 * (q1 + q2)
         odd = 2.0 * (l1 + l2)
-        out[d] = f[d] - (even - odd)
-        out[neg(d)] = f[neg(d)] - (even + odd)
+        out[d] = less(d, even - odd)
+        out[neg(d)] = less(neg(d), even + odd)
 
     axis(hxx, dxxyy, dxxzz, dxyy, dxzz, X)
     axis(hyy, dxxyy, dyyzz, dxxy, dyzz, Y)
     axis(hzz, dxxzz, dyyzz, dxxz, dyyz, Z)
     out[(0, 0, 0)] = f[(0, 0, 0)] + trace - 4.0 * (dxxyy + dxxzz + dyyzz)
-    return out, rho
+    return out, rho, (jx, jy, jz)
 
 
 def gradient(ph, plane, row):
@@ -171,7 +182,8 @@
                     a = comp[u] + comp[v] if key[v] > 0 else comp[u] - comp[v]
                     cache[key] = (h2 * (a * a - g2), c2 * a)
             q, c = cache[key]
-        val = s_of(d) + q
+        known = s_of(d)
+        val = q if known is None else known + q
         fp[POS[d], plane, pl.ds(row, 8), :] = zroll(val, d[2])
         r = frac * val
         if c is not None:
@@ -208,43 +220,65 @@
     return a, b, c, out, back
 
 
-def build_message(msg, high, tiles, s, rho, fl, ph, fp, red):
+def message_tile(high, row, s, rho, fl, ph, fp, red):
     a, b, c, out, back = face(high)
     gout = jnp.where(high, 3, 0)
     gback = jnp.where(high, 0, 3)
-    for n, t in enumerate(tiles):
-        rows = pl.ds(8 * t, 8)
-        to = pl.ds(8 * n, 8)
-        row = ROW0 + 8 * t
-        for j in range(5):
-            msg[j, to, :] = s[out + j, a, rows, :]
-        for j in range(9):
-            msg[5 + j, to, :] = s[10 + j, a, rows, :]
+    rows = pl.ds(row - ROW0, 8)
+    own = pl.ds(row, 8)
+
+    def plain():
+        v = [s[out + j, a, rows, :] for j in range(5)]
+        return v, [rho[a, rows, :], ph[a + 2, own, :], ph[b + 2, own, :], fl[a, rows, :]]
+
+    def moved():
+        f = {}
         total = None
         for j in range(5):
-            ey = DIRS[j][1]
-            shifted = pl.ds(row - ey, 8)
-            msg[14 + j, to, :] = fp[out + j, b + 1, shifted, :]
+            d = DIRS[5 + j]
+            shifted = pl.ds(row - d[1], 8)
+            f[d] = fp[out + j, b + 1, shifted, :]
+            f[(-1, d[1], d[2])] = None
             v = fp[out + j, c + 1, shifted, :] + fp[back + j, a + 1, shifted, :]
             total = v if total is None else total + v
-        for j in range(9):
-            total = total + fp[10 + j, b + 1, pl.ds(row - DIRS[10 + j][1], 8), :]
-        moved, rsum = None, None
+        for j in range(10, 19):
+            shifted = pl.ds(row - DIRS[j][1], 8)
+            f[DIRS[j]] = fp[j, a + 1, shifted, :]
+            total = total + fp[j, b + 1, shifted, :]
+        linear, dens, mom = collide(f, equilibrium=False)
+        at_a, at_b = None, None
         for j in range(3):
             shifted = pl.ds(row - GROUPS[j][1], 8)
-            v = red[gout + j, b + 1, shifted, :]
-            moved = v if moved is None else moved + v
+            v = red[gout + j, b + 1, shifted, :] + red[6 + j, a + 1, shifted, :]
+            at_a = v if at_a is None else at_a + v
             v = (red[gout + j, c + 1, shifted, :] + red[gback + j, a + 1, shifted, :]) + red[
                 6 + j, b + 1, shifted, :
             ]
-            rsum = v if rsum is None else rsum + v
-        msg[19, to, :] = rho[a, rows, :]
-        msg[20, to, :] = ph[a + 2, pl.ds(row, 8), :]
-        msg[21, to, :] = ph[b + 2, pl.ds(row, 8), :]
-        msg[22, to, :] = fl[a, rows, :]
-        msg[23, to, :] = moved
-        msg[24, to, :] = total
-        msg[25, to, :] = rsum
+            at_b = v if at_b is None else at_b + v
+        return [linear[DIRS[5 + j]] for j in range(5)] + [dens, *mom], [at_a, total, at_b]
+
+    return plain, moved
+
+
+PLAIN = [0, 1, 2, 3, 4, 14, 15, 16, 17]
+MOVED = [5, 6, 7, 8, 9, 10, 11, 12, 13, 18, 19, 20]
+
+
+def main_message(msg, high, state):
+    for n in range(NYL // 8):
+        plain, moved = message_tile(high, ROW0 + 4 + 8 * n, *state)
+        for kinds, part in ((PLAIN, plain()), (MOVED, moved())):
+            for j, v in zip(kinds, part[0] + part[1]):
+                msg[j, pl.ds(8 * n, 8), :] = v
+
+
+def corner_message(msg, high, state):
+    for n, (first, second) in enumerate(((0, 2), (EXT - 8, EXT - 6))):
+        plain, _ = message_tile(high, ROW0 + first, *state)
+        _, moved = message_tile(high, ROW0 + second, *state)
+        for kinds, part, r in ((PLAIN, plain(), 4 * n), (MOVED, moved(), 0)):
+            for j, v in zip(kinds, part[0] + part[1]):
+                msg[j, pl.ds(4 * n, 4), :] = v[r:r + 4]
 
 
 def inner_step(tiles, s, rho, fl, ph, fp, red):
@@ -263,7 +297,7 @@
             row = ROW0 + 8 * t
             frac = 0.5 + 0.5 * ph[x + 2, pl.ds(row, 8), :]
             sums = {}
-            for d in DIRS[base:base + 5]:
+            for d in DIRS[base:base + 5] + DIRS[10:]:
                 v = s[POS[d], x, pl.ds(8 * t, 8), :]
                 fp[POS[d], x + 1, pl.ds(row, 8), :] = zroll(v, d[2])
                 r = zroll(frac * v, d[2])
@@ -272,10 +306,46 @@
                 red[GPOS[g], x + 1, pl.ds(row, 8), :] = r
 
 
-def start_kernel(pops_hbm, labels_hbm, solid_hbm, ya, yb, s, rho, fl, ph, fp, red, xa, xb,
+def pack_kernel(pops_hbm, labels_hbm, solid_hbm, ya, yb, pops, labels, solid, sems):
+    odd = lax.axis_index("gy") % 2
+    copies = []
+    for k, r in enumerate((0, NYL - 8)):
+        ends = pl.ds(r, 8)
+        part = pl.ds(8 * k, 8)
+        copies += [
+            pltpu.make_async_copy(pops_hbm.at[:, :, ends], pops.at[:, :, part], sems.at[3 * k]),
+            pltpu.make_async_copy(labels_hbm.at[:, ends], labels.at[:, part], sems.at[3 * k + 1]),
+            pltpu.make_async_copy(solid_hbm.at[:, ends], solid.at[:, part], sems.at[3 * k + 2]),
+        ]
+    for c in copies:
+        c.start()
+    for c in copies:
+        c.wait()
+
+    def pack(out, high):
+        three = pl.ds(13 if high else 0, 3)
+        four = pl.ds(12 if high else 0, 4)
+        for i in range(19):
+            for x in range(NXL):
+                out[pl.ds(i * 12 + x * 3, 3), :] = pops[i, x, three, :]
+        for x in range(NXL):
+            out[pl.ds(228 + x * 4, 4), :] = labels[x, four, :].astype(jnp.float32)
+            out[pl.ds(244 + x * 3, 3), :] = solid[x, three, :].astype(jnp.float32)
+
+    @pl.when(odd == 0)
+    def _():
+        pack(ya, True)
+        pack(yb, False)
+
+    @pl.when(odd == 1)
+    def _():
+        pack(ya, False)
+        pack(yb, True)
+
+
+def start_kernel(pops_hbm, labels_hbm, solid_hbm, s, rho, fl, ph, fp, red, xa, xb,
                  pops, labels, solid, sems):
     gy = lax.axis_index("gy")
-    odd = gy % 2
     copies = [
         pltpu.make_async_copy(labels_hbm, labels, sems.at[0]),
         pltpu.make_async_copy(solid_hbm, solid, sems.at[1]),
@@ -288,27 +358,6 @@
     for c in copies:
         c.wait()
 
-    def pack(out, high):
-        for i in range(19):
-            for x in range(NXL):
-                r = NYL - 3 if high else 0
-                out[pl.ds(i * 12 + x * 3, 3), :] = pops[i, x, pl.ds(r, 3), :]
-        for x in range(NXL):
-            r = NYL - 4 if high else 0
-            out[pl.ds(228 + x * 4, 4), :] = labels[x, pl.ds(r, 4), :].astype(jnp.float32)
-            r = NYL - 3 if high else 0
-            out[pl.ds(244 + x * 3, 3), :] = solid[x, pl.ds(r, 3), :].astype(jnp.float32)
-
-    @pl.when(odd == 0)
-    def _():
-        pack(ya, True)
-        pack(yb, False)
-
-    @pl.when(odd == 1)
-    def _():
-        pack(ya, False)
-        pack(yb, True)
-
     low_edge = gy == 0
     high_edge = gy == lax.axis_size("gy") - 1
 
@@ -323,7 +372,7 @@
                 is_solid = is_solid | ((y == 0) & low_edge)
             if t == NYL // 8 - 1:
                 is_solid = is_solid | ((y == NYL - 1) & high_edge)
-            relaxed, total = collide(f)
+            relaxed, total, _ = collide(f)
             for d in DIRS:
                 s[POS[d], x, rows, :] = jnp.where(is_solid, f[neg(d)], relaxed[d])
             rho[x, rows, :] = total
@@ -334,8 +383,8 @@
     lax.fori_loop(0, NXL, plane, 0)
     inner_step(range(NT), s, rho, fl, ph, fp, red)
     low_a = lax.axis_index("gx") % 2 == 1
-    build_message(xb, low_a, (1, 2, 3), s, rho, fl, ph, fp, red)
-    build_message(xa, jnp.logical_not(low_a), (1, 2, 3), s, rho, fl, ph, fp, red)
+    main_message(xb, low_a, (s, rho, fl, ph, fp, red))
+    main_message(xa, jnp.logical_not(low_a), (s, rho, fl, ph, fp, red))
 
 
 def edge_kernel(ya, yb, s_in, rho_in, fl_in, ph_in, fp_in, red_in,
@@ -373,7 +422,7 @@
 
         f = {d: raw[REF_OF[k], x] for k, d in enumerate(DIRS)}
         is_solid = raw[20, x] > 0.5
-        relaxed, total = collide(f)
+        relaxed, total, _ = collide(f)
         for d in DIRS:
             v = jnp.where(is_solid, f[neg(d)], relaxed[d])
             put(s.at[POS[d], x], 0, jnp.where(inside, v, 0.0))
@@ -386,32 +435,37 @@
     lax.fori_loop(0, NXL, plane, 0)
     inner_step((0, NT - 1), s, rho, fl, ph, fp, red)
     low_a = lax.axis_index("gx") % 2 == 1
-    build_message(xc, low_a, (0, NT - 1), s, rho, fl, ph, fp, red)
-    build_message(xd, jnp.logical_not(low_a), (0, NT - 1), s, rho, fl, ph, fp, red)
+    corner_message(xc, low_a, (s, rho, fl, ph, fp, red))
+    corner_message(xd, jnp.logical_not(low_a), (s, rho, fl, ph, fp, red))
 
 
 def last_kernel(s, rho, fl, ph_in, fp_in, red_in, xa, xb, xc, xd,
-                pops_out, phase_out, ph, fp, red, hx, s2, rho2):
+                pops_hbm, phase_hbm, ph, fp, red, hx, s2, rho2, pops_out, phase_out, sems):
     gy = lax.axis_index("gy")
     low_edge = gy == 0
     high_edge = gy == lax.axis_size("gy") - 1
     side_a = 1 - lax.axis_index("gx") % 2
 
-    def put(src, side, tiles):
+    def put(src, side, corner):
         near = jnp.where(side == 1, NXL + 2, 1)
         far = jnp.where(side == 1, NXL + 3, 0)
-        for n, t in enumerate(tiles):
-            part = pl.ds(8 * n, 8)
-            for j in range(26):
-                if j not in (20, 21):
-                    hx[side, j, pl.ds(8 * t, 8), :] = src[j, part, :]
-            ph[near, pl.ds(ROW0 + 8 * t, 8), :] = src[20, part, :]
-            ph[far, pl.ds(ROW0 + 8 * t, 8), :] = src[21, part, :]
-
-    put(xa, side_a, (1, 2, 3))
-    put(xd, side_a, (0, NT - 1))
-    put(xb, 1 - side_a, (1, 2, 3))
-    put(xc, 1 - side_a, (0, NT - 1))
+        for j in range(21):
+            moved = 2 if corner and j in MOVED else 0
+            if corner:
+                spans = ((moved, 0, 4), (EXT - 4 - moved, 4, 4))
+            else:
+                spans = [(4 + 8 * n, 8 * n, 8) for n in range(NYL // 8)]
+            for to, part, n in spans:
+                v = src[j, pl.ds(part, n), :]
+                if j in (15, 16):
+                    ph[near if j == 15 else far, pl.ds(ROW0 + to, n), :] = v
+                else:
+                    hx[side, j, pl.ds(to, n), :] = v
+
+    put(xa, side_a, False)
+    put(xb, 1 - side_a, False)
+    put(xd, side_a, True)
+    put(xc, 1 - side_a, True)
 
     def mask(t):
         y = tile_rows(t)
@@ -435,14 +489,10 @@
             rows = pl.ds(8 * t, 8)
 
             def value(d):
-                if d in back:
-                    return 0.0
-                if d in towards:
-                    return hx[side, towards.index(d), rows, :]
-                return hx[side, 5 + POS[d] - 10, rows, :]
+                return hx[side, towards.index(d), rows, :] if d in towards else None
 
             finish(
-                DIRS, value, ph, hx[side, 19, rows, :], hx[side, 22, rows, :],
+                DIRS, value, ph, hx[side, 14, rows, :], hx[side, 17, rows, :],
                 plane_index, ROW0 + 8 * t, fp, red,
             )
 
@@ -451,7 +501,7 @@
             row = ROW0 + 8 * t
             rows = pl.ds(8 * t, 8)
             f = {d: arrived(d, fp, x + 1, row) for d in DIRS}
-            relaxed, total = collide(f)
+            relaxed, total, _ = collide(f)
             p = 2.0 * red_arrived(red, x + 1, row) / total - 1.0
             inside = mask(t)
             if inside is not None:
@@ -472,22 +522,22 @@
         for t in range(NT):
             row = ROW0 + 8 * t
             rows = pl.ds(8 * t, 8)
-            f = {}
-            for d in DIRS:
-                if d in towards:
-                    f[d] = hx[side, 14 + towards.index(d), rows, :]
-                else:
-                    f[d] = arrived(d, fp, index, row)
-            relaxed, total = collide(f)
-            rsum = hx[side, 23, rows, :]
-            rfar = hx[side, 25, rows, :]
+            f = {d: None if d in towards else arrived(d, fp, index, row) for d in DIRS}
+            outwards = 1.0 if towards[0][0] > 0 else -1.0
+            known = (
+                hx[side, 10, rows, :], outwards * hx[side, 11, rows, :],
+                hx[side, 12, rows, :], hx[side, 13, rows, :],
+            )
+            relaxed, total, _ = collide(f, known)
+            rsum = hx[side, 18, rows, :]
+            rfar = hx[side, 20, rows, :]
             for g in GROUPS:
                 shifted = pl.ds(row - g[1], 8)
                 if g[0] != towards[0][0]:
                     rsum = rsum + red[GPOS[g], index - g[0], shifted, :]
                 if g[0] == back[0][0]:
                     rfar = rfar + red[GPOS[g], index, shifted, :]
-            ffar = hx[side, 24, rows, :]
+            ffar = hx[side, 19, rows, :]
             for d in back:
                 ffar = ffar + fp[POS[d], index, pl.ds(row - d[1], 8), :]
             p = 2.0 * rsum / total - 1.0
@@ -496,9 +546,9 @@
             if inside is not None:
                 p = jnp.where(inside, p, 0.0)
                 pfar = jnp.where(inside, pfar, 0.0)
-            is_fluid = hx[side, 22, rows, :] > 0.5
-            for d in towards:
-                v = jnp.where(is_fluid, relaxed[d], f[neg(d)])
+            is_fluid = hx[side, 17, rows, :] > 0.5
+            for j, d in enumerate(towards):
+                v = jnp.where(is_fluid, relaxed[d] + hx[side, 5 + j, rows, :], f[neg(d)])
                 if inside is not None:
                     v = jnp.where(inside, v, 0.0)
                 s2[POS[d], index, rows, :] = v
@@ -521,8 +571,14 @@
             rows = pl.ds(8 * t, 8)
             finish(
                 towards, lambda d: s2[POS[d], index, rows, :], ph, rho2[index, rows, :],
-                hx[side, 22, rows, :], index, ROW0 + 8 * t, fp, red,
+                hx[side, 17, rows, :], index, ROW0 + 8 * t, fp, red,
             )
+
+    def out_copies(x):
+        return (
+            pltpu.make_async_copy(pops_out.at[:, x], pops_hbm.at[:, x], sems.at[2 * x]),
+            pltpu.make_async_copy(phase_out.at[x], phase_hbm.at[x], sems.at[2 * x + 1]),
+        )
 
     def final(x, carry):
         for t in range(NYL // 8):
@@ -536,7 +592,13 @@
             phase_out[x, rows, :] = 2.0 * red_arrived(red, x + 1, row) / total - 1.0
         return carry
 
-    lax.fori_loop(0, NXL, final, 0)
+    for x in range(NXL):
+        final(x, 0)
+        for copy in out_copies(x):
+            copy.start()
+    for x in range(NXL):
+        for copy in out_copies(x):
+            copy.wait()
 
 
 F32 = jnp.float32
@@ -549,11 +611,12 @@
     return jax.ShapeDtypeStruct(dims, F32)
 
 
-def call(kernel, in_specs, outs, scratch, name, aliases=None, vmem=40, cost=0):
+def call(kernel, in_specs, outs, scratch, name, aliases=None, vmem=40, cost=0,
+         out_specs=None):
     return pl.pallas_call(
         kernel,
         in_specs=in_specs,
-        out_specs=[VM] * len(outs),
+        out_specs=out_specs or [VM] * len(outs),
         out_shape=outs,
         scratch_shapes=scratch,
         input_output_aliases=aliases or {},
@@ -581,21 +644,29 @@
         shaped(NXL + 4, SROWS, 128), shaped(19, NXL + 2, SROWS, 128),
         shaped(9, NXL + 2, SROWS, 128),
     ]
-    got = call(
-        start_kernel, [HB] * 3, [shaped(YROWS, 128)] * 2 + state + [shaped(26, 24, 128)] * 2,
-        [
-            pltpu.VMEM((19, NXL, NYL, 128), F32), pltpu.VMEM((NXL, NYL, 128), jnp.int32),
-            pltpu.VMEM((NXL, NYL, 128), jnp.int32), pltpu.SemaphoreType.DMA((6,)),
-        ],
-        "start", vmem=40,
-    )(*[pltpu.with_memory_space_constraint(v, pltpu.HBM) for v in (populations, labels, solid_mask)])
-    ya, yb, *mid, xa, xb = got
+    inputs = [
+        pltpu.with_memory_space_constraint(v, pltpu.HBM)
+        for v in (populations, labels, solid_mask)
+    ]
+
+    def staging(rows):
+        return [
+            pltpu.VMEM((19, NXL, rows, 128), F32), pltpu.VMEM((NXL, rows, 128), jnp.int32),
+            pltpu.VMEM((NXL, rows, 128), jnp.int32), pltpu.SemaphoreType.DMA((6,)),
+        ]
+
+    ya, yb = call(
+        pack_kernel, [HB] * 3, [shaped(YROWS, 128)] * 2, staging(16), "pack",
+    )(*inputs)
+    ya = swap(ya, "gy", 0)
+    yb = swap(yb, "gy", 1)
+    *mid, xa, xb = call(
+        start_kernel, [HB] * 3, state + [shaped(21, NYL, 128)] * 2, staging(NYL), "start",
+    )(*inputs)
     xb = swap(xb, "gx", 1)
     xa = swap(xa, "gx", 0)
-    ya = swap(ya, "gy", 0)
-    yb = swap(yb, "gy", 1)
     *mid, xd, xc = call(
-        edge_kernel, [VM] * 8, state + [shaped(26, 16, 128)] * 2,
+        edge_kernel, [VM] * 8, state + [shaped(21, 8, 128)] * 2,
         [pltpu.VMEM((21, NXL, 8, 128), F32)], "edge", {2 + i: i for i in range(6)},
     )(ya, yb, *mid)
     xc = swap(xc, "gx", 1)
@@ -604,10 +675,11 @@
         last_kernel, [VM] * 10,
         [shaped(19, NXL, NYL, 128), shaped(NXL, NYL, 128)] + state[3:],
         [
-            pltpu.VMEM((2, 26, EXT, 128), F32), pltpu.VMEM((19, NXL + 2, EXT, 128), F32),
-            pltpu.VMEM((NXL + 2, EXT, 128), F32),
+            pltpu.VMEM((2, 21, EXT, 128), F32), pltpu.VMEM((19, NXL + 2, EXT, 128), F32),
+            pltpu.VMEM((NXL + 2, EXT, 128), F32), pltpu.VMEM((19, NXL, NYL, 128), F32),
+            pltpu.VMEM((NXL, NYL, 128), F32), pltpu.SemaphoreType.DMA((2 * NXL,)),
         ],
-        "last", {3: 2, 4: 3, 5: 4},
+        "last", {3: 2, 4: 3, 5: 4}, out_specs=[HB] * 2 + [VM] * 3,
     )(*mid, xa, xb, xc, xd)
     return out[0], out[1]
 

time: 34.8 us -> 37.1 us (1.066)
  the two profiles are of different devices: /device:TPU:8 before, /device:TPU:24 now
where the time goes in v2:
time: 37.1 us; the launch traced here: 36.9 us
  waiting for transfers between devices  13.5 us (36%)
  starting transfers between devices  12.5 us (34%)
  Pallas kernels  10.2 us (27%)
  between operations  0.67 us (2%)
    ppermute x6, waiting for transfers between devices, swap(): return lax.ppermute(value, axis, pairs(lax.axis_size(axis), first))  13.5 us
    ppermute x6, starting transfers between devices, swap(): return lax.ppermute(value, axis, pairs(lax.axis_size(axis), first))  12.5 us
    pallas_call x1, Pallas kernels, on_device(): call(last_kernel, [VM] * 10, [shaped(19, NXL, NYL, 128), shaped(NXL, NYL,...  5.28 us
    pallas_call x1, Pallas kernels, on_device(): call(start_kernel, [HB] * 3, state + [shaped(21, NYL, 128)] * 2, staging(...  2.86 us
    pallas_call x1, Pallas kernels, on_device(): call(pack_kernel, [HB] * 3, [shaped(YROWS, 128)] * 2, staging(16), 'pack')  1.21 us
    pallas_call x1, Pallas kernels, on_device(): call(edge_kernel, [VM] * 8, state + [shaped(21, 8, 128)] * 2, [pltpu.VMEM...  0.88 us
  transfers between devices with their start and end apart: 6, of which 3 were waited for; matrix products, arithmetic and copies ran while one was open for 0% of the time, Pallas kernels for 6%

profile of v2, /device:TPU:24, one launch (start us, length us, event | category | flops | bytes accessed | tf_op | source)
XLA Modules:
  0.0 36.9 jit_solution(722034917001443603)
XLA Ops:
  0.6 2.9 %start.1 = (f32[19,4,40,128]{3,2,1,0:T(8,128)S(1)}, f32[4,40,128]{2,1,0:T(8,128)S(1)}, f32[4,40,128]{2,1,0:T(8,128)S(1)}, f32[8,56,128]{2,1,0:T(8,128)S(1)}, f32...) custom-call(f32[19,4,32,128]{3,2,1,0:T(8,128)} %pops_hbm.3, ...), custom_call_target="tpu_custom_call" | custom-call | tf_op jit(solution)/shard_map/start/pallas_call | solution.py:663
  3.5 0.1 collective-permute-start.2
  3.6 8.6 %collective-permute-start.3 = (f32[21,32,128]{2,1,0:T(8,128)S(1)}, f32[21,32,128]{2,1,0:T(8,128)S(1)}, u32[]{:S(2)}, u32[]{:S(2)}) collective-permute-start(f32[21,32,128]{2,1,0:T(8,128)S(1)} %get-tuple-element.37), channel_id=1, source_target_pairs={{8,16},{16,8},{24,32},{32,24},{40,48},{48,40},{56,64},{64,56},{72,... | collective-permute-start | bytes 1032200 | tf_op jit(solution)/shard_map/ppermute | solution.py:638
  12.2 1.2 %pack.1 = (f32[256,128]{1,0:T(8,128)S(1)}, f32[256,128]{1,0:T(8,128)S(1)}) custom-call(f32[19,4,32,128]{3,2,1,0:T(8,128)} %pops_hbm.3, s32[4,32,128]{2,1,0:T(8,128)} %labels_hbm.3, s32[4,32,128]{2,1,0:T(8,128)} %solid_hbm.3), custom_call_target="tpu_custom_call" | custom-call | tf_op jit(solution)/shard_map/pack/pallas_call | solution.py:658
  13.4 0.8 %collective-permute-start = (f32[256,128]{1,0:T(8,128)S(1)}, f32[256,128]{1,0:T(8,128)S(1)}, u32[]{:S(2)}, u32[]{:S(2)}) collective-permute-start(f32[256,128]{1,0:T(8,128)S(1)} %get-tuple-element.22), channel_id=1, source_target_pairs={{0,1},{1,0},{2,3},{3,2},{4,5},{5,4},{6,7},{7,6},{8,9},{9,8},{10,11... | collective-permute-start | bytes 393224 | tf_op jit(solution)/shard_map/ppermute | solution.py:638
  14.3 1.5 %collective-permute-start.1 = (f32[256,128]{1,0:T(8,128)S(1)}, f32[256,128]{1,0:T(8,128)S(1)}, u32[]{:S(2)}, u32[]{:S(2)}) collective-permute-start(f32[256,128]{1,0:T(8,128)S(1)} %get-tuple-element.23), channel_id=1, source_target_pairs={{1,2},{2,1},{3,4},{4,3},{5,6},{6,5},{7,0},{0,7},{9,10},{10,9},{11,... | collective-permute-start | bytes 393224 | tf_op jit(solution)/shard_map/ppermute | solution.py:638
  15.8 2.7 %collective-permute-done.ya = f32[256,128]{1,0:T(8,128)S(1)} collective-permute-done((f32[256,128]{1,0:T(8,128)S(1)}, f32[256,128]{1,0:T(8,128)S(1)}, u32[]{:S(2)}, u32[]{:S(2)}) %collective-permute-start) | collective-permute-done | bytes 131104 | tf_op jit(solution)/shard_map/ppermute | solution.py:638
  18.5 4.0 %collective-permute-done.1.yb = f32[256,128]{1,0:T(8,128)S(1)} collective-permute-done((f32[256,128]{1,0:T(8,128)S(1)}, f32[256,128]{1,0:T(8,128)S(1)}, u32[]{:S(2)}, u32[]{:S(2)}) %collective-permute-start.1) | collective-permute-done | bytes 131104 | tf_op jit(solution)/shard_map/ppermute | solution.py:638
  22.5 0.9 %edge.1 = (f32[19,4,40,128]{3,2,1,0:T(8,128)S(1)}, f32[4,40,128]{2,1,0:T(8,128)S(1)}, f32[4,40,128]{2,1,0:T(8,128)S(1)}, f32[8,56,128]{2,1,0:T(8,128)S(1)}, f32[...) custom-call(f32[256,128]{1,0:T(8,128)S(1)} %collective-permute-done., ...), custom_call_target="tpu_custom_call", output_to_operand_aliasing={{0}: (2, {}), {1}: (3, {}), {2}: (4, {}), {3}: (5, {}), {4}... | custom-call | tf_op jit(solution)/shard_map/edge/pallas_call | solution.py:668
  23.4 1.4 %collective-permute-start.4 = (f32[21,8,128]{2,1,0:T(8,128)S(1)}, f32[21,8,128]{2,1,0:T(8,128)S(1)}, u32[]{:S(2)}, u32[]{:S(2)}) collective-permute-start(f32[21,8,128]{2,1,0:T(8,128)S(1)} %get-tuple-element.38), channel_id=1, source_target_pairs={{8,16},{16,8},{24,32},{32,24},{40,48},{48,40},{56,64},{64,56},{72,... | collective-permute-start | bytes 258056 | tf_op jit(solution)/shard_map/ppermute | solution.py:638
  24.9 0.0 collective-permute-start.5
  24.9 6.8 %collective-permute-done.4.xc = f32[21,8,128]{2,1,0:T(8,128)S(1)} collective-permute-done((f32[21,8,128]{2,1,0:T(8,128)S(1)}, f32[21,8,128]{2,1,0:T(8,128)S(1)}, u32[]{:S(2)}, u32[]{:S(2)}) %collective-permute-start.4) | collective-permute-done | bytes 86048 | tf_op jit(solution)/shard_map/ppermute | solution.py:638
  31.6 0.0 collective-permute-done.5.xd
  31.6 0.0 collective-permute-done.2.xa
  31.6 0.0 collective-permute-done.3.xb
  31.6 5.3 %last.1 = (f32[19,4,32,128]{3,2,1,0:T(8,128)}, f32[4,32,128]{2,1,0:T(8,128)}, f32[8,56,128]{2,1,0:T(8,128)S(1)}, f32[19,6,56,128]{3,2,1,0:T(8,128)S(1)}, f32[9,6,56,128]{3,2,1,0:T(8,128)S(1)}) custom-call(f32[19,4,40,128]{3,2,1,0:T(8,128)S(1)} %get-tuple-element.30.s, ...), custom_call_target="tpu_custom_call", output_to_operand_aliasing={{2}: (3, {}), {3}: (4, {}), {4}: (5, {})} | custom-call | tf_op jit(solution)/shard_map/last/pallas_call | solution.py:674
Async XLA Ops:
  3.5 28.1 %collective-permute-start.2 = (f32[21,32,128]{2,1,0:T(8,128)S(1)}, f32[21,32,128]{2,1,0:T(8,128)S(1)}, u32[]{:S(2)}, u32[]{:S(2)}) collective-permute-start(f32[21,32,128]{2,1,0:T(8,128)S(1)} %get-tuple-element.36), channel_id=1, source_target_pairs={{0,8},{8,0},{16,24},{24,16},{32,40},{40,32},{48,56},{56,48},{64,72... | collective-permute-start | bytes 1032200 | tf_op jit(solution)/shard_map/ppermute | solution.py:638
  3.6 28.0 %collective-permute-start.3 = (f32[21,32,128]{2,1,0:T(8,128)S(1)}, f32[21,32,128]{2,1,0:T(8,128)S(1)}, u32[]{:S(2)}, u32[]{:S(2)}) collective-permute-start(f32[21,32,128]{2,1,0:T(8,128)S(1)} %get-tuple-element.37), channel_id=1, source_target_pairs={{8,16},{16,8},{24,32},{32,24},{40,48},{48,40},{56,64},{64,56},{72,... | collective-permute-start | bytes 1032200 | tf_op jit(solution)/shard_map/ppermute | solution.py:638
  13.4 5.1 %collective-permute-start = (f32[256,128]{1,0:T(8,128)S(1)}, f32[256,128]{1,0:T(8,128)S(1)}, u32[]{:S(2)}, u32[]{:S(2)}) collective-permute-start(f32[256,128]{1,0:T(8,128)S(1)} %get-tuple-element.22), channel_id=1, source_target_pairs={{0,1},{1,0},{2,3},{3,2},{4,5},{5,4},{6,7},{7,6},{8,9},{9,8},{10,11... | collective-permute-start | bytes 393224 | tf_op jit(solution)/shard_map/ppermute | solution.py:638
  14.3 8.3 %collective-permute-start.1 = (f32[256,128]{1,0:T(8,128)S(1)}, f32[256,128]{1,0:T(8,128)S(1)}, u32[]{:S(2)}, u32[]{:S(2)}) collective-permute-start(f32[256,128]{1,0:T(8,128)S(1)} %get-tuple-element.23), channel_id=1, source_target_pairs={{1,2},{2,1},{3,4},{4,3},{5,6},{6,5},{7,0},{0,7},{9,10},{10,9},{11,... | collective-permute-start | bytes 393224 | tf_op jit(solution)/shard_map/ppermute | solution.py:638
  23.4 8.2 %collective-permute-start.4 = (f32[21,8,128]{2,1,0:T(8,128)S(1)}, f32[21,8,128]{2,1,0:T(8,128)S(1)}, u32[]{:S(2)}, u32[]{:S(2)}) collective-permute-start(f32[21,8,128]{2,1,0:T(8,128)S(1)} %get-tuple-element.38), channel_id=1, source_target_pairs={{8,16},{16,8},{24,32},{32,24},{40,48},{48,40},{56,64},{64,56},{72,... | collective-permute-start | bytes 258056 | tf_op jit(solution)/shard_map/ppermute | solution.py:638
  24.9 6.8 %collective-permute-start.5 = (f32[21,8,128]{2,1,0:T(8,128)S(1)}, f32[21,8,128]{2,1,0:T(8,128)S(1)}, u32[]{:S(2)}, u32[]{:S(2)}) collective-permute-start(f32[21,8,128]{2,1,0:T(8,128)S(1)} %get-tuple-element.39), channel_id=1, source_target_pairs={{0,8},{8,0},{16,24},{24,16},{32,40},{40,32},{48,56},{56,48},{64,72... | collective-permute-start | bytes 258056 | tf_op jit(solution)/shard_map/ppermute | solution.py:638

commit v3 on v2

--- a/solution.py
+++ b/solution.py
@@ -343,7 +343,7 @@
         pack(yb, True)
 
 
-def start_kernel(pops_hbm, labels_hbm, solid_hbm, s, rho, fl, ph, fp, red, xa, xb,
+def start_kernel(pops_hbm, labels_hbm, solid_hbm, after, s, rho, fl, ph, fp, red, xa, xb,
                  pops, labels, solid, sems):
     gy = lax.axis_index("gy")
     copies = [
@@ -658,16 +658,17 @@
     ya, yb = call(
         pack_kernel, [HB] * 3, [shaped(YROWS, 128)] * 2, staging(16), "pack",
     )(*inputs)
+    packed = ya
     ya = swap(ya, "gy", 0)
     yb = swap(yb, "gy", 1)
     *mid, xa, xb = call(
-        start_kernel, [HB] * 3, state + [shaped(21, NYL, 128)] * 2, staging(NYL), "start",
-    )(*inputs)
+        start_kernel, [HB] * 3 + [VM], state + [shaped(21, NYL, 128)] * 2, staging(NYL), "start",
+    )(*inputs, packed)
     xb = swap(xb, "gx", 1)
     xa = swap(xa, "gx", 0)
     *mid, xd, xc = call(
         edge_kernel, [VM] * 8, state + [shaped(21, 8, 128)] * 2,
-        [pltpu.VMEM((21, NXL, 8, 128), F32)], "edge", {2 + i: i for i in range(6)},
+        [pltpu.VMEM((21, NXL, 8, 128), F32)], "edge", {2 + i: i for i in range(6)}, cost=10 ** 10,
     )(ya, yb, *mid)
     xc = swap(xc, "gx", 1)
     xd = swap(xd, "gx", 0)

time: 37.1 us -> 33.2 us (0.89)
  the two profiles are of different devices: /device:TPU:24 before, /device:TPU:8 now
where the time goes in v3:
time: 33.2 us; the launch traced here: 33.1 us
  starting transfers between devices  12.9 us (39%)
  Pallas kernels  10.2 us (31%)
  waiting for transfers between devices  9.24 us (28%)
  between operations  0.68 us (2%)
    ppermute x6, starting transfers between devices, swap(): return lax.ppermute(value, axis, pairs(lax.axis_size(axis), first))  12.9 us
    ppermute x6, waiting for transfers between devices, swap(): return lax.ppermute(value, axis, pairs(lax.axis_size(axis), first))  9.24 us
    pallas_call x1, Pallas kernels, on_device(): call(last_kernel, [VM] * 10, [shaped(19, NXL, NYL, 128), shaped(NXL, NYL,...  5.28 us
    pallas_call x1, Pallas kernels, on_device(): call(start_kernel, [HB] * 3 + [VM], state + [shaped(21, NYL, 128)] * 2, s...  2.86 us
    pallas_call x1, Pallas kernels, on_device(): call(pack_kernel, [HB] * 3, [shaped(YROWS, 128)] * 2, staging(16), 'pack')  1.22 us
    pallas_call x1, Pallas kernels, on_device(): call(edge_kernel, [VM] * 8, state + [shaped(21, 8, 128)] * 2, [pltpu.VMEM...  0.89 us
  transfers between devices with their start and end apart: 6, of which 1 were waited for; matrix products, arithmetic and copies ran while one was open for 0% of the time, Pallas kernels for 11%

profile of v3, /device:TPU:8, one launch (start us, length us, event | category | flops | bytes accessed | tf_op | source)
XLA Modules:
  0.0 33.1 jit_solution(11116533382210905380)
XLA Ops:
  0.6 1.2 %pack.1 = (f32[256,128]{1,0:T(8,128)S(1)}, f32[256,128]{1,0:T(8,128)S(1)}) custom-call(f32[19,4,32,128]{3,2,1,0:T(8,128)} %pops_hbm.3, s32[4,32,128]{2,1,0:T(8,128)} %labels_hbm.3, s32[4,32,128]{2,1,0:T(8,128)} %solid_hbm.3), custom_call_target="tpu_custom_call" | custom-call | tf_op jit(solution)/shard_map/pack/pallas_call | solution.py:658
  1.9 1.7 %collective-permute-start.1 = (f32[256,128]{1,0:T(8,128)S(1)}, f32[256,128]{1,0:T(8,128)S(1)}, u32[]{:S(2)}, u32[]{:S(2)}) collective-permute-start(f32[256,128]{1,0:T(8,128)S(1)} %get-tuple-element.23), channel_id=1, source_target_pairs={{1,2},{2,1},{3,4},{4,3},{5,6},{6,5},{7,0},{0,7},{9,10},{10,9},{11,... | collective-permute-start | bytes 393224 | tf_op jit(solution)/shard_map/ppermute | solution.py:638
  3.5 3.2 %collective-permute-start = (f32[256,128]{1,0:T(8,128)S(1)}, f32[256,128]{1,0:T(8,128)S(1)}, u32[]{:S(2)}, u32[]{:S(2)}) collective-permute-start(f32[256,128]{1,0:T(8,128)S(1)} %get-tuple-element.22.after), channel_id=1, source_target_pairs={{0,1},{1,0},{2,3},{3,2},{4,5},{5,4},{6,7},{7,6},{8,9},{9,8},{10,11... | collective-permute-start | bytes 393224 | tf_op jit(solution)/shard_map/ppermute | solution.py:638
  6.8 2.9 %start.1 = (f32[19,4,40,128]{3,2,1,0:T(8,128)S(1)}, f32[4,40,128]{2,1,0:T(8,128)S(1)}, f32[4,40,128]{2,1,0:T(8,128)S(1)}, f32[8,56,128]{2,1,0:T(8,128)S(1)}, f32...) custom-call(f32[19,4,32,128]{3,2,1,0:T(8,128)} %pops_hbm.3, ...), custom_call_target="tpu_custom_call" | custom-call | tf_op jit(solution)/shard_map/start/pallas_call | solution.py:664
  9.6 0.1 collective-permute-start.2
  9.7 7.7 %collective-permute-start.3 = (f32[21,32,128]{2,1,0:T(8,128)S(1)}, f32[21,32,128]{2,1,0:T(8,128)S(1)}, u32[]{:S(2)}, u32[]{:S(2)}) collective-permute-start(f32[21,32,128]{2,1,0:T(8,128)S(1)} %get-tuple-element.37), channel_id=1, source_target_pairs={{8,16},{16,8},{24,32},{32,24},{40,48},{48,40},{56,64},{64,56},{72,... | collective-permute-start | bytes 1032200 | tf_op jit(solution)/shard_map/ppermute | solution.py:638
  17.4 0.0 collective-permute-done.1.yb
  17.4 0.0 collective-permute-done.ya
  17.4 0.9 %edge.1 = (f32[19,4,40,128]{3,2,1,0:T(8,128)S(1)}, f32[4,40,128]{2,1,0:T(8,128)S(1)}, f32[4,40,128]{2,1,0:T(8,128)S(1)}, f32[8,56,128]{2,1,0:T(8,128)S(1)}, f32[...) custom-call(f32[256,128]{1,0:T(8,128)S(1)} %collective-permute-done., ...), custom_call_target="tpu_custom_call", output_to_operand_aliasing={{0}: (2, {}), {1}: (3, {}), {2}: (4, {}), {3}: (5, {}), {4}... | custom-call | flops 10000000000 | bytes 10000000000 | tf_op jit(solution)/shard_map/edge/pallas_call | solution.py:669
  18.3 0.1 collective-permute-start.4
  18.4 0.1 collective-permute-start.5
  18.5 9.2 %collective-permute-done.4.xc = f32[21,8,128]{2,1,0:T(8,128)S(1)} collective-permute-done((f32[21,8,128]{2,1,0:T(8,128)S(1)}, f32[21,8,128]{2,1,0:T(8,128)S(1)}, u32[]{:S(2)}, u32[]{:S(2)}) %collective-permute-start.4) | collective-permute-done | bytes 86048 | tf_op jit(solution)/shard_map/ppermute | solution.py:638
  27.8 0.0 collective-permute-done.5.xd
  27.8 0.0 collective-permute-done.2.xa
  27.8 0.0 collective-permute-done.3.xb
  27.8 5.3 %last.1 = (f32[19,4,32,128]{3,2,1,0:T(8,128)}, f32[4,32,128]{2,1,0:T(8,128)}, f32[8,56,128]{2,1,0:T(8,128)S(1)}, f32[19,6,56,128]{3,2,1,0:T(8,128)S(1)}, f32[9,6,56,128]{3,2,1,0:T(8,128)S(1)}) custom-call(f32[19,4,40,128]{3,2,1,0:T(8,128)S(1)} %get-tuple-element.30.s, ...), custom_call_target="tpu_custom_call", output_to_operand_aliasing={{2}: (3, {}), {3}: (4, {}), {4}: (5, {})} | custom-call | tf_op jit(solution)/shard_map/last/pallas_call | solution.py:675
Async XLA Ops:
  1.9 15.6 %collective-permute-start.1 = (f32[256,128]{1,0:T(8,128)S(1)}, f32[256,128]{1,0:T(8,128)S(1)}, u32[]{:S(2)}, u32[]{:S(2)}) collective-permute-start(f32[256,128]{1,0:T(8,128)S(1)} %get-tuple-element.23), channel_id=1, source_target_pairs={{1,2},{2,1},{3,4},{4,3},{5,6},{6,5},{7,0},{0,7},{9,10},{10,9},{11,... | collective-permute-start | bytes 393224 | tf_op jit(solution)/shard_map/ppermute | solution.py:638
  3.5 13.9 %collective-permute-start = (f32[256,128]{1,0:T(8,128)S(1)}, f32[256,128]{1,0:T(8,128)S(1)}, u32[]{:S(2)}, u32[]{:S(2)}) collective-permute-start(f32[256,128]{1,0:T(8,128)S(1)} %get-tuple-element.22.after), channel_id=1, source_target_pairs={{0,1},{1,0},{2,3},{3,2},{4,5},{5,4},{6,7},{7,6},{8,9},{9,8},{10,11... | collective-permute-start | bytes 393224 | tf_op jit(solution)/shard_map/ppermute | solution.py:638
  9.6 18.1 %collective-permute-start.2 = (f32[21,32,128]{2,1,0:T(8,128)S(1)}, f32[21,32,128]{2,1,0:T(8,128)S(1)}, u32[]{:S(2)}, u32[]{:S(2)}) collective-permute-start(f32[21,32,128]{2,1,0:T(8,128)S(1)} %get-tuple-element.36), channel_id=1, source_target_pairs={{0,8},{8,0},{16,24},{24,16},{32,40},{40,32},{48,56},{56,48},{64,72... | collective-permute-start | bytes 1032200 | tf_op jit(solution)/shard_map/ppermute | solution.py:638
  9.7 18.0 %collective-permute-start.3 = (f32[21,32,128]{2,1,0:T(8,128)S(1)}, f32[21,32,128]{2,1,0:T(8,128)S(1)}, u32[]{:S(2)}, u32[]{:S(2)}) collective-permute-start(f32[21,32,128]{2,1,0:T(8,128)S(1)} %get-tuple-element.37), channel_id=1, source_target_pairs={{8,16},{16,8},{24,32},{32,24},{40,48},{48,40},{56,64},{64,56},{72,... | collective-permute-start | bytes 1032200 | tf_op jit(solution)/shard_map/ppermute | solution.py:638
  18.3 9.4 %collective-permute-start.4 = (f32[21,8,128]{2,1,0:T(8,128)S(1)}, f32[21,8,128]{2,1,0:T(8,128)S(1)}, u32[]{:S(2)}, u32[]{:S(2)}) collective-permute-start(f32[21,8,128]{2,1,0:T(8,128)S(1)} %get-tuple-element.38), channel_id=1, source_target_pairs={{8,16},{16,8},{24,32},{32,24},{40,48},{48,40},{56,64},{64,56},{72,... | collective-permute-start | bytes 258056 | tf_op jit(solution)/shard_map/ppermute | solution.py:638
  18.4 9.3 %collective-permute-start.5 = (f32[21,8,128]{2,1,0:T(8,128)S(1)}, f32[21,8,128]{2,1,0:T(8,128)S(1)}, u32[]{:S(2)}, u32[]{:S(2)}) collective-permute-start(f32[21,8,128]{2,1,0:T(8,128)S(1)} %get-tuple-element.39), channel_id=1, source_target_pairs={{0,8},{8,0},{16,24},{24,16},{32,40},{40,32},{48,56},{56,48},{64,72... | collective-permute-start | bytes 258056 | tf_op jit(solution)/shard_map/ppermute | solution.py:638

commit v4 on v3

--- a/solution.py
+++ b/solution.py
@@ -308,44 +308,6 @@
 
 def pack_kernel(pops_hbm, labels_hbm, solid_hbm, ya, yb, pops, labels, solid, sems):
     odd = lax.axis_index("gy") % 2
-    copies = []
-    for k, r in enumerate((0, NYL - 8)):
-        ends = pl.ds(r, 8)
-        part = pl.ds(8 * k, 8)
-        copies += [
-            pltpu.make_async_copy(pops_hbm.at[:, :, ends], pops.at[:, :, part], sems.at[3 * k]),
-            pltpu.make_async_copy(labels_hbm.at[:, ends], labels.at[:, part], sems.at[3 * k + 1]),
-            pltpu.make_async_copy(solid_hbm.at[:, ends], solid.at[:, part], sems.at[3 * k + 2]),
-        ]
-    for c in copies:
-        c.start()
-    for c in copies:
-        c.wait()
-
-    def pack(out, high):
-        three = pl.ds(13 if high else 0, 3)
-        four = pl.ds(12 if high else 0, 4)
-        for i in range(19):
-            for x in range(NXL):
-                out[pl.ds(i * 12 + x * 3, 3), :] = pops[i, x, three, :]
-        for x in range(NXL):
-            out[pl.ds(228 + x * 4, 4), :] = labels[x, four, :].astype(jnp.float32)
-            out[pl.ds(244 + x * 3, 3), :] = solid[x, three, :].astype(jnp.float32)
-
-    @pl.when(odd == 0)
-    def _():
-        pack(ya, True)
-        pack(yb, False)
-
-    @pl.when(odd == 1)
-    def _():
-        pack(ya, False)
-        pack(yb, True)
-
-
-def start_kernel(pops_hbm, labels_hbm, solid_hbm, after, s, rho, fl, ph, fp, red, xa, xb,
-                 pops, labels, solid, sems):
-    gy = lax.axis_index("gy")
     copies = [
         pltpu.make_async_copy(labels_hbm, labels, sems.at[0]),
         pltpu.make_async_copy(solid_hbm, solid, sems.at[1]),
@@ -358,6 +320,29 @@
     for c in copies:
         c.wait()
 
+    def pack(out, high):
+        three = pl.ds(NYL - 3 if high else 0, 3)
+        four = pl.ds(NYL - 4 if high else 0, 4)
+        for i in range(19):
+            for x in range(NXL):
+                out[pl.ds(i * 12 + x * 3, 3), :] = pops[i, x, three, :]
+        for x in range(NXL):
+            out[pl.ds(228 + x * 4, 4), :] = labels[x, four, :].astype(jnp.float32)
+            out[pl.ds(244 + x * 3, 3), :] = solid[x, three, :].astype(jnp.float32)
+
+    @pl.when(odd == 0)
+    def _():
+        pack(ya, True)
+        pack(yb, False)
+
+    @pl.when(odd == 1)
+    def _():
+        pack(ya, False)
+        pack(yb, True)
+
+
+def start_kernel(pops, labels, solid, s, rho, fl, ph, fp, red, xa, xb):
+    gy = lax.axis_index("gy")
     low_edge = gy == 0
     high_edge = gy == lax.axis_size("gy") - 1
 
@@ -439,7 +424,7 @@
     corner_message(xd, jnp.logical_not(low_a), (s, rho, fl, ph, fp, red))
 
 
-def last_kernel(s, rho, fl, ph_in, fp_in, red_in, xa, xb, xc, xd,
+def last_kernel(s, rho, fl, ph_in, fp_in, red_in, xb, xa, xc, xd,
                 pops_hbm, phase_hbm, ph, fp, red, hx, s2, rho2, pops_out, phase_out, sems):
     gy = lax.axis_index("gy")
     low_edge = gy == 0
@@ -649,21 +634,19 @@
         for v in (populations, labels, solid_mask)
     ]
 
-    def staging(rows):
-        return [
-            pltpu.VMEM((19, NXL, rows, 128), F32), pltpu.VMEM((NXL, rows, 128), jnp.int32),
-            pltpu.VMEM((NXL, rows, 128), jnp.int32), pltpu.SemaphoreType.DMA((6,)),
-        ]
-
-    ya, yb = call(
-        pack_kernel, [HB] * 3, [shaped(YROWS, 128)] * 2, staging(16), "pack",
+    whole = [
+        shaped(19, NXL, NYL, 128), jax.ShapeDtypeStruct((NXL, NYL, 128), jnp.int32),
+        jax.ShapeDtypeStruct((NXL, NYL, 128), jnp.int32),
+    ]
+    ya, yb, *held = call(
+        pack_kernel, [HB] * 3, [shaped(YROWS, 128)] * 2 + whole,
+        [pltpu.SemaphoreType.DMA((6,))], "pack",
     )(*inputs)
-    packed = ya
     ya = swap(ya, "gy", 0)
     yb = swap(yb, "gy", 1)
     *mid, xa, xb = call(
-        start_kernel, [HB] * 3 + [VM], state + [shaped(21, NYL, 128)] * 2, staging(NYL), "start",
-    )(*inputs, packed)
+        start_kernel, [VM] * 3, state + [shaped(21, NYL, 128)] * 2, [], "start",
+    )(*held)
     xb = swap(xb, "gx", 1)
     xa = swap(xa, "gx", 0)
     *mid, xd, xc = call(
@@ -681,7 +664,7 @@
             pltpu.VMEM((NXL, NYL, 128), F32), pltpu.SemaphoreType.DMA((2 * NXL,)),
         ],
         "last", {3: 2, 4: 3, 5: 4}, out_specs=[HB] * 2 + [VM] * 3,
-    )(*mid, xa, xb, xc, xd)
+    )(*mid, xb, xa, xc, xd)
     return out[0], out[1]
 
 

time: 33.2 us -> 30.3 us (0.913)
  the two profiles are of different devices: /device:TPU:8 before, /device:TPU:32 now
where the time goes in v4:
time: 30.3 us; the launch traced here: 30.2 us
  starting transfers between devices  12.9 us (43%)
  Pallas kernels  9.11 us (30%)
  waiting for transfers between devices  7.48 us (25%)
  between operations  0.66 us (2%)
    ppermute x6, starting transfers between devices, swap(): return lax.ppermute(value, axis, pairs(lax.axis_size(axis), first))  12.9 us
    ppermute x6, waiting for transfers between devices, swap(): return lax.ppermute(value, axis, pairs(lax.axis_size(axis), first))  7.48 us
    pallas_call x1, Pallas kernels, on_device(): call(last_kernel, [VM] * 10, [shaped(19, NXL, NYL, 128), shaped(NXL, NYL,...  5.28 us
    pallas_call x1, Pallas kernels, on_device(): call(start_kernel, [VM] * 3, state + [shaped(21, NYL, 128)] * 2, [], 'sta...  1.47 us
    pallas_call x1, Pallas kernels, on_device(): call(pack_kernel, [HB] * 3, [shaped(YROWS, 128)] * 2 + whole, [pltpu.Sema...  1.46 us
    pallas_call x1, Pallas kernels, on_device(): call(edge_kernel, [VM] * 8, state + [shaped(21, 8, 128)] * 2, [pltpu.VMEM...  0.9 us
  transfers between devices with their start and end apart: 6, of which 1 were waited for; matrix products, arithmetic and copies ran while one was open for 0% of the time, Pallas kernels for 8%

profile of v4, /device:TPU:32, one launch (start us, length us, event | category | flops | bytes accessed | tf_op | source)
XLA Modules:
  0.0 30.2 jit_solution(7453927689819836500)
XLA Ops:
  0.6 1.5 %pack.1 = (f32[256,128]{1,0:T(8,128)S(1)}, f32[256,128]{1,0:T(8,128)S(1)}, f32[19,4,32,128]{3,2,1,0:T(8,128)S(1)}, s32[4,32,128]{2,1,0:T(8,128)S(1)}, s32[4,32,128]{2,1,0:T(8,128)S(1)}) custom-call(f32[19,4,32,128]{3,2,1,0:T(8,128)} %pops_hbm.1, s32[4,32,128]{2,1,0:T(8,128)} %labels_hbm.1, s32[4,32,128]{2,1,0:T(8,128)} %solid_hbm.1), custom_call_target="tpu_custom_call" | custom-call | tf_op jit(solution)/shard_map/pack/pallas_call | solution.py:641
  2.1 1.7 %collective-permute-start = (f32[256,128]{1,0:T(8,128)S(1)}, f32[256,128]{1,0:T(8,128)S(1)}, u32[]{:S(2)}, u32[]{:S(2)}) collective-permute-start(f32[256,128]{1,0:T(8,128)S(1)} %get-tuple-element.25), channel_id=1, source_target_pairs={{0,1},{1,0},{2,3},{3,2},{4,5},{5,4},{6,7},{7,6},{8,9},{9,8},{10,11... | collective-permute-start | bytes 393224 | tf_op jit(solution)/shard_map/ppermute | solution.py:623
  3.8 1.7 %collective-permute-start.1 = (f32[256,128]{1,0:T(8,128)S(1)}, f32[256,128]{1,0:T(8,128)S(1)}, u32[]{:S(2)}, u32[]{:S(2)}) collective-permute-start(f32[256,128]{1,0:T(8,128)S(1)} %get-tuple-element.26), channel_id=1, source_target_pairs={{1,2},{2,1},{3,4},{4,3},{5,6},{6,5},{7,0},{0,7},{9,10},{10,9},{11,... | collective-permute-start | bytes 393224 | tf_op jit(solution)/shard_map/ppermute | solution.py:623
  5.5 1.5 %start.1 = (f32[19,4,40,128]{3,2,1,0:T(8,128)S(1)}, f32[4,40,128]{2,1,0:T(8,128)S(1)}, f32[4,40,128]{2,1,0:T(8,128)S(1)}, f32[8,56,128]{2,1,0:T(8,128)S(1)}, f32...) custom-call(f32[19,4,32,128]{3,2,1,0:T(8,128)S(1)} %get-tuple-elemen, ...), custom_call_target="tpu_custom_call" | custom-call | tf_op jit(solution)/shard_map/start/pallas_call | solution.py:647
  7.0 7.5 %collective-permute-start.2 = (f32[21,32,128]{2,1,0:T(8,128)S(1)}, f32[21,32,128]{2,1,0:T(8,128)S(1)}, u32[]{:S(2)}, u32[]{:S(2)}) collective-permute-start(f32[21,32,128]{2,1,0:T(8,128)S(1)} %get-tuple-element.42), channel_id=1, source_target_pairs={{8,16},{16,8},{24,32},{32,24},{40,48},{48,40},{56,64},{64,56},{72,... | collective-permute-start | bytes 1032200 | tf_op jit(solution)/shard_map/ppermute | solution.py:623
  14.4 0.0 collective-permute-start.3
  14.4 0.0 collective-permute-done.ya
  14.4 0.0 collective-permute-done.1.yb
  14.4 0.9 %edge.1 = (f32[19,4,40,128]{3,2,1,0:T(8,128)S(1)}, f32[4,40,128]{2,1,0:T(8,128)S(1)}, f32[4,40,128]{2,1,0:T(8,128)S(1)}, f32[8,56,128]{2,1,0:T(8,128)S(1)}, f32[...) custom-call(f32[256,128]{1,0:T(8,128)S(1)} %collective-permute-done., ...), custom_call_target="tpu_custom_call", output_to_operand_aliasing={{0}: (2, {}), {1}: (3, {}), {2}: (4, {}), {3}: (5, {}), {4}... | custom-call | flops 10000000000 | bytes 10000000000 | tf_op jit(solution)/shard_map/edge/pallas_call | solution.py:652
  15.3 2.1 %collective-permute-start.4 = (f32[21,8,128]{2,1,0:T(8,128)S(1)}, f32[21,8,128]{2,1,0:T(8,128)S(1)}, u32[]{:S(2)}, u32[]{:S(2)}) collective-permute-start(f32[21,8,128]{2,1,0:T(8,128)S(1)} %get-tuple-element.44), channel_id=1, source_target_pairs={{8,16},{16,8},{24,32},{32,24},{40,48},{48,40},{56,64},{64,56},{72,... | collective-permute-start | bytes 258056 | tf_op jit(solution)/shard_map/ppermute | solution.py:623
  17.4 0.0 collective-permute-start.5
  17.4 7.5 %collective-permute-done.4.xc = f32[21,8,128]{2,1,0:T(8,128)S(1)} collective-permute-done((f32[21,8,128]{2,1,0:T(8,128)S(1)}, f32[21,8,128]{2,1,0:T(8,128)S(1)}, u32[]{:S(2)}, u32[]{:S(2)}) %collective-permute-start.4) | collective-permute-done | bytes 86048 | tf_op jit(solution)/shard_map/ppermute | solution.py:623
  24.9 0.0 collective-permute-done.5.xd
  24.9 0.0 collective-permute-done.2.xb
  24.9 0.0 collective-permute-done.3.xa
  24.9 5.3 %last.1 = (f32[19,4,32,128]{3,2,1,0:T(8,128)}, f32[4,32,128]{2,1,0:T(8,128)}, f32[8,56,128]{2,1,0:T(8,128)S(1)}, f32[19,6,56,128]{3,2,1,0:T(8,128)S(1)}, f32[9,6,56,128]{3,2,1,0:T(8,128)S(1)}) custom-call(f32[19,4,40,128]{3,2,1,0:T(8,128)S(1)} %get-tuple-element.36.s, ...), custom_call_target="tpu_custom_call", output_to_operand_aliasing={{2}: (3, {}), {3}: (4, {}), {4}: (5, {})} | custom-call | tf_op jit(solution)/shard_map/last/pallas_call | solution.py:658
Async XLA Ops:
  2.1 12.3 %collective-permute-start = (f32[256,128]{1,0:T(8,128)S(1)}, f32[256,128]{1,0:T(8,128)S(1)}, u32[]{:S(2)}, u32[]{:S(2)}) collective-permute-start(f32[256,128]{1,0:T(8,128)S(1)} %get-tuple-element.25), channel_id=1, source_target_pairs={{0,1},{1,0},{2,3},{3,2},{4,5},{5,4},{6,7},{7,6},{8,9},{9,8},{10,11... | collective-permute-start | bytes 393224 | tf_op jit(solution)/shard_map/ppermute | solution.py:623
  3.8 10.7 %collective-permute-start.1 = (f32[256,128]{1,0:T(8,128)S(1)}, f32[256,128]{1,0:T(8,128)S(1)}, u32[]{:S(2)}, u32[]{:S(2)}) collective-permute-start(f32[256,128]{1,0:T(8,128)S(1)} %get-tuple-element.26), channel_id=1, source_target_pairs={{1,2},{2,1},{3,4},{4,3},{5,6},{6,5},{7,0},{0,7},{9,10},{10,9},{11,... | collective-permute-start | bytes 393224 | tf_op jit(solution)/shard_map/ppermute | solution.py:623
  7.0 17.9 %collective-permute-start.2 = (f32[21,32,128]{2,1,0:T(8,128)S(1)}, f32[21,32,128]{2,1,0:T(8,128)S(1)}, u32[]{:S(2)}, u32[]{:S(2)}) collective-permute-start(f32[21,32,128]{2,1,0:T(8,128)S(1)} %get-tuple-element.42), channel_id=1, source_target_pairs={{8,16},{16,8},{24,32},{32,24},{40,48},{48,40},{56,64},{64,56},{72,... | collective-permute-start | bytes 1032200 | tf_op jit(solution)/shard_map/ppermute | solution.py:623
  14.4 10.5 %collective-permute-start.3 = (f32[21,32,128]{2,1,0:T(8,128)S(1)}, f32[21,32,128]{2,1,0:T(8,128)S(1)}, u32[]{:S(2)}, u32[]{:S(2)}) collective-permute-start(f32[21,32,128]{2,1,0:T(8,128)S(1)} %get-tuple-element.43), channel_id=1, source_target_pairs={{0,8},{8,0},{16,24},{24,16},{32,40},{40,32},{48,56},{56,48},{64,72... | collective-permute-start | bytes 1032200 | tf_op jit(solution)/shard_map/ppermute | solution.py:623
  15.3 9.5 %collective-permute-start.4 = (f32[21,8,128]{2,1,0:T(8,128)S(1)}, f32[21,8,128]{2,1,0:T(8,128)S(1)}, u32[]{:S(2)}, u32[]{:S(2)}) collective-permute-start(f32[21,8,128]{2,1,0:T(8,128)S(1)} %get-tuple-element.44), channel_id=1, source_target_pairs={{8,16},{16,8},{24,32},{32,24},{40,48},{48,40},{56,64},{64,56},{72,... | collective-permute-start | bytes 258056 | tf_op jit(solution)/shard_map/ppermute | solution.py:623
  17.4 7.5 %collective-permute-start.5 = (f32[21,8,128]{2,1,0:T(8,128)S(1)}, f32[21,8,128]{2,1,0:T(8,128)S(1)}, u32[]{:S(2)}, u32[]{:S(2)}) collective-permute-start(f32[21,8,128]{2,1,0:T(8,128)S(1)} %get-tuple-element.45), channel_id=1, source_target_pairs={{0,8},{8,0},{16,24},{24,16},{32,40},{40,32},{48,56},{56,48},{64,72... | collective-permute-start | bytes 258056 | tf_op jit(solution)/shard_map/ppermute | solution.py:623

commit v5 on v4

--- a/solution.py
+++ b/solution.py
@@ -27,6 +27,7 @@
 NT = 5
 ROW0 = 8
 SROWS = 56
+HALF = 11
 YROWS = 256
 W1 = 1.0 / 18.0
 W2 = 1.0 / 36.0
@@ -264,21 +265,27 @@
 MOVED = [5, 6, 7, 8, 9, 10, 11, 12, 13, 18, 19, 20]
 
 
+def plane_of(msg, j):
+    if not isinstance(msg, tuple):
+        return msg.at[j]
+    return msg[0].at[j] if j < HALF else msg[1].at[j - HALF]
+
+
 def main_message(msg, high, state):
     for n in range(NYL // 8):
         plain, moved = message_tile(high, ROW0 + 4 + 8 * n, *state)
         for kinds, part in ((PLAIN, plain()), (MOVED, moved())):
             for j, v in zip(kinds, part[0] + part[1]):
-                msg[j, pl.ds(8 * n, 8), :] = v
-
-
-def corner_message(msg, high, state):
+                plane_of(msg, j)[pl.ds(8 * n, 8), :] = v
+
+
+def corner_message(msg, base, high, state):
     for n, (first, second) in enumerate(((0, 2), (EXT - 8, EXT - 6))):
         plain, _ = message_tile(high, ROW0 + first, *state)
         _, moved = message_tile(high, ROW0 + second, *state)
         for kinds, part, r in ((PLAIN, plain(), 4 * n), (MOVED, moved(), 0)):
             for j, v in zip(kinds, part[0] + part[1]):
-                msg[j, pl.ds(4 * n, 4), :] = v[r:r + 4]
+                plane_of(msg, j)[pl.ds(base + 4 * n, 4), :] = v[r:r + 4]
 
 
 def inner_step(tiles, s, rho, fl, ph, fp, red):
@@ -341,7 +348,7 @@
         pack(yb, True)
 
 
-def start_kernel(pops, labels, solid, s, rho, fl, ph, fp, red, xa, xb):
+def start_kernel(pops, labels, solid, s, rho, fl, ph, fp, red, xa, xd, xb):
     gy = lax.axis_index("gy")
     low_edge = gy == 0
     high_edge = gy == lax.axis_size("gy") - 1
@@ -369,11 +376,11 @@
     inner_step(range(NT), s, rho, fl, ph, fp, red)
     low_a = lax.axis_index("gx") % 2 == 1
     main_message(xb, low_a, (s, rho, fl, ph, fp, red))
-    main_message(xa, jnp.logical_not(low_a), (s, rho, fl, ph, fp, red))
-
-
-def edge_kernel(ya, yb, s_in, rho_in, fl_in, ph_in, fp_in, red_in,
-                s, rho, fl, ph, fp, red, xd, xc, raw):
+    main_message((xa, xd), jnp.logical_not(low_a), (s, rho, fl, ph, fp, red))
+
+
+def edge_kernel(ya, yb, s_in, rho_in, fl_in, ph_in, fp_in, red_in, xa_in, xd_in,
+                s, rho, fl, ph, fp, red, xa, xd, xc, raw):
     gy = lax.axis_index("gy")
     odd = gy % 2
     low_edge = gy == 0
@@ -420,37 +427,14 @@
     lax.fori_loop(0, NXL, plane, 0)
     inner_step((0, NT - 1), s, rho, fl, ph, fp, red)
     low_a = lax.axis_index("gx") % 2 == 1
-    corner_message(xc, low_a, (s, rho, fl, ph, fp, red))
-    corner_message(xd, jnp.logical_not(low_a), (s, rho, fl, ph, fp, red))
-
-
-def last_kernel(s, rho, fl, ph_in, fp_in, red_in, xb, xa, xc, xd,
-                pops_hbm, phase_hbm, ph, fp, red, hx, s2, rho2, pops_out, phase_out, sems):
+    corner_message(xc, 0, low_a, (s, rho, fl, ph, fp, red))
+    corner_message((xa, xd), NYL, jnp.logical_not(low_a), (s, rho, fl, ph, fp, red))
+
+
+def edges():
     gy = lax.axis_index("gy")
     low_edge = gy == 0
     high_edge = gy == lax.axis_size("gy") - 1
-    side_a = 1 - lax.axis_index("gx") % 2
-
-    def put(src, side, corner):
-        near = jnp.where(side == 1, NXL + 2, 1)
-        far = jnp.where(side == 1, NXL + 3, 0)
-        for j in range(21):
-            moved = 2 if corner and j in MOVED else 0
-            if corner:
-                spans = ((moved, 0, 4), (EXT - 4 - moved, 4, 4))
-            else:
-                spans = [(4 + 8 * n, 8 * n, 8) for n in range(NYL // 8)]
-            for to, part, n in spans:
-                v = src[j, pl.ds(part, n), :]
-                if j in (15, 16):
-                    ph[near if j == 15 else far, pl.ds(ROW0 + to, n), :] = v
-                else:
-                    hx[side, j, pl.ds(to, n), :] = v
-
-    put(xa, side_a, False)
-    put(xb, 1 - side_a, False)
-    put(xd, side_a, True)
-    put(xc, 1 - side_a, True)
 
     def mask(t):
         y = tile_rows(t)
@@ -460,104 +444,177 @@
             return (y < NYL) | jnp.logical_not(high_edge)
         return None
 
-    sides = ((0, 0, DIRS[5:10], DIRS[0:5]), (1, NXL + 1, DIRS[0:5], DIRS[5:10]))
-
-    for x in (0, NXL - 1):
-        for t in range(NT):
-            rows = pl.ds(8 * t, 8)
-            finish(
-                DIRS, lambda d: s[POS[d], x, rows, :], ph, rho[x, rows, :],
-                fl[x, rows, :], x + 1, ROW0 + 8 * t, fp, red,
-            )
-    for side, plane_index, towards, back in sides:
-        for t in range(NT):
-            rows = pl.ds(8 * t, 8)
-
-            def value(d):
-                return hx[side, towards.index(d), rows, :] if d in towards else None
-
-            finish(
-                DIRS, value, ph, hx[side, 14, rows, :], hx[side, 17, rows, :],
-                plane_index, ROW0 + 8 * t, fp, red,
-            )
-
-    def plane(x, carry):
-        for t in range(NT):
-            row = ROW0 + 8 * t
-            rows = pl.ds(8 * t, 8)
-            f = {d: arrived(d, fp, x + 1, row) for d in DIRS}
-            relaxed, total, _ = collide(f)
-            p = 2.0 * red_arrived(red, x + 1, row) / total - 1.0
-            inside = mask(t)
+    return mask
+
+
+def put_message(src, base, side, corner, hx, ph):
+    near = jnp.where(side == 1, NXL + 2, 1)
+    far = jnp.where(side == 1, NXL + 3, 0)
+    for j in range(21):
+        moved = 2 if corner and j in MOVED else 0
+        if corner:
+            spans = ((moved, 0, 4), (EXT - 4 - moved, 4, 4))
+        else:
+            spans = [(4 + 8 * n, 8 * n, 8) for n in range(NYL // 8)]
+        for to, part, n in spans:
+            v = plane_of(src, j)[pl.ds(base + part, n), :]
+            if j in (15, 16):
+                ph[near if j == 15 else far, pl.ds(ROW0 + to, n), :] = v
+            else:
+                hx[j, pl.ds(to, n), :] = v
+
+
+def by_side(side, step):
+    for k in (0, 1):
+        pl.when(side == k)(lambda: step(k))
+
+
+def side_dirs(side):
+    if side == 0:
+        return 0, DIRS[5:10], DIRS[0:5]
+    return NXL + 1, DIRS[0:5], DIRS[5:10]
+
+
+def halo_first(side, hx, ph, fp, red):
+    index, towards, _ = side_dirs(side)
+    for t in range(NT):
+        rows = pl.ds(8 * t, 8)
+        finish(
+            DIRS, lambda d: hx[towards.index(d), rows, :] if d in towards else None, ph,
+            hx[14, rows, :], hx[17, rows, :], index, ROW0 + 8 * t, fp, red,
+        )
+
+
+def halo_collide(side, hx, fp, red, ph, s2, rho2):
+    mask = edges()
+    index, towards, back = side_dirs(side)
+    near, far = (NXL + 2, NXL + 3) if side == 1 else (1, 0)
+    outwards = 1.0 if side == 0 else -1.0
+    for t in range(NT):
+        row = ROW0 + 8 * t
+        rows = pl.ds(8 * t, 8)
+        f = {d: None if d in towards else arrived(d, fp, index, row) for d in DIRS}
+        known = (
+            hx[10, rows, :], outwards * hx[11, rows, :], hx[12, rows, :], hx[13, rows, :],
+        )
+        relaxed, total, _ = collide(f, known)
+        rsum = hx[18, rows, :]
+        rfar = hx[20, rows, :]
+        for g in GROUPS:
+            shifted = pl.ds(row - g[1], 8)
+            if g[0] != towards[0][0]:
+                rsum = rsum + red[GPOS[g], index - g[0], shifted, :]
+            if g[0] == back[0][0]:
+                rfar = rfar + red[GPOS[g], index, shifted, :]
+        ffar = hx[19, rows, :]
+        for d in back:
+            ffar = ffar + fp[POS[d], index, pl.ds(row - d[1], 8), :]
+        p = 2.0 * rsum / total - 1.0
+        pfar = 2.0 * rfar / ffar - 1.0
+        inside = mask(t)
+        if inside is not None:
+            p = jnp.where(inside, p, 0.0)
+            pfar = jnp.where(inside, pfar, 0.0)
+        is_fluid = hx[17, rows, :] > 0.5
+        for j, d in enumerate(towards):
+            v = jnp.where(is_fluid, relaxed[d] + hx[5 + j, rows, :], f[neg(d)])
             if inside is not None:
-                p = jnp.where(inside, p, 0.0)
-            is_fluid = fl[x, rows, :] > 0.5
-            for d in DIRS:
-                v = jnp.where(is_fluid, relaxed[d], f[neg(d)])
-                if inside is not None:
-                    v = jnp.where(inside, v, 0.0)
-                s2[POS[d], x + 1, rows, :] = v
-            rho2[x + 1, rows, :] = total
-            ph[x + 2, pl.ds(row, 8), :] = p
+                v = jnp.where(inside, v, 0.0)
+            s2[POS[d], index, rows, :] = v
+        rho2[index, rows, :] = total
+        ph[near, pl.ds(row, 8), :] = p
+        ph[far, pl.ds(row, 8), :] = pfar
+
+
+def halo_second(side, hx, s2, rho2, ph, fp, red):
+    index, towards, _ = side_dirs(side)
+    for t in range(NT):
+        rows = pl.ds(8 * t, 8)
+        finish(
+            towards, lambda d: s2[POS[d], index, rows, :], ph, rho2[index, rows, :],
+            hx[17, rows, :], index, ROW0 + 8 * t, fp, red,
+        )
+
+
+def own_finish(x, s, k, rho, fl, ph, fp, red):
+    for t in range(NT):
+        rows = pl.ds(8 * t, 8)
+        finish(
+            DIRS, lambda d: s[POS[d], k, rows, :], ph, rho[k, rows, :], fl[x, rows, :],
+            x + 1, ROW0 + 8 * t, fp, red,
+        )
+
+
+def own_collide(x, k, fl, fp, red, ph, s2, rho2):
+    mask = edges()
+    for t in range(NT):
+        row = ROW0 + 8 * t
+        rows = pl.ds(8 * t, 8)
+        f = {d: arrived(d, fp, x + 1, row) for d in DIRS}
+        relaxed, total, _ = collide(f)
+        p = 2.0 * red_arrived(red, x + 1, row) / total - 1.0
+        inside = mask(t)
+        if inside is not None:
+            p = jnp.where(inside, p, 0.0)
+        is_fluid = fl[x, rows, :] > 0.5
+        for d in DIRS:
+            v = jnp.where(is_fluid, relaxed[d], f[neg(d)])
+            if inside is not None:
+                v = jnp.where(inside, v, 0.0)
+            s2[POS[d], k, rows, :] = v
+        rho2[k, rows, :] = total
+        ph[x + 2, pl.ds(row, 8), :] = p
+
+
+def two_planes(side, step):
+    def body(k, carry):
+        step(jnp.where(side == 1, NXL - 1 - k, k), k)
         return carry
 
-    lax.fori_loop(0, NXL, plane, 0)
-    for side, index, towards, back in sides:
-        near, far = (NXL + 2, NXL + 3) if side == 1 else (1, 0)
-        for t in range(NT):
-            row = ROW0 + 8 * t
-            rows = pl.ds(8 * t, 8)
-            f = {d: None if d in towards else arrived(d, fp, index, row) for d in DIRS}
-            outwards = 1.0 if towards[0][0] > 0 else -1.0
-            known = (
-                hx[side, 10, rows, :], outwards * hx[side, 11, rows, :],
-                hx[side, 12, rows, :], hx[side, 13, rows, :],
-            )
-            relaxed, total, _ = collide(f, known)
-            rsum = hx[side, 18, rows, :]
-            rfar = hx[side, 20, rows, :]
-            for g in GROUPS:
-                shifted = pl.ds(row - g[1], 8)
-                if g[0] != towards[0][0]:
-                    rsum = rsum + red[GPOS[g], index - g[0], shifted, :]
-                if g[0] == back[0][0]:
-                    rfar = rfar + red[GPOS[g], index, shifted, :]
-            ffar = hx[side, 19, rows, :]
-            for d in back:
-                ffar = ffar + fp[POS[d], index, pl.ds(row - d[1], 8), :]
-            p = 2.0 * rsum / total - 1.0
-            pfar = 2.0 * rfar / ffar - 1.0
-            inside = mask(t)
-            if inside is not None:
-                p = jnp.where(inside, p, 0.0)
-                pfar = jnp.where(inside, pfar, 0.0)
-            is_fluid = hx[side, 17, rows, :] > 0.5
-            for j, d in enumerate(towards):
-                v = jnp.where(is_fluid, relaxed[d] + hx[side, 5 + j, rows, :], f[neg(d)])
-                if inside is not None:
-                    v = jnp.where(inside, v, 0.0)
-                s2[POS[d], index, rows, :] = v
-            rho2[index, rows, :] = total
-            ph[near, pl.ds(row, 8), :] = p
-            ph[far, pl.ds(row, 8), :] = pfar
-
-    def second(x, carry):
-        for t in range(NT):
-            rows = pl.ds(8 * t, 8)
-            finish(
-                DIRS, lambda d: s2[POS[d], x + 1, rows, :], ph, rho2[x + 1, rows, :],
-                fl[x, rows, :], x + 1, ROW0 + 8 * t, fp, red,
-            )
+    lax.fori_loop(0, 2, body, 0)
+
+
+def near_kernel(s, rho, fl, ph_in, fp_in, red_in, xa, xd,
+                fp, red, fp2, red2, ph2, s2_next, rho2_next, ph, hx, s2, rho2, own2, orho2):
+    side = 1 - lax.axis_index("gx") % 2
+    ph[...] = ph_in[...]
+    put_message((xa, xd), 0, side, False, hx, ph)
+    put_message((xa, xd), NYL, side, True, hx, ph)
+    first = jnp.where(side == 1, NXL - 1, 0)
+    own_finish(first, s, first, rho, fl, ph, fp, red)
+    by_side(side, lambda k: halo_first(k, hx, ph, fp, red))
+    two_planes(side, lambda x, k: own_collide(x, k, fl, fp, red, ph2, own2, orho2))
+    by_side(side, lambda k: halo_collide(k, hx, fp, red, ph2, s2, rho2))
+    own_finish(first, own2, 0, orho2, fl, ph2, fp2, red2)
+    by_side(side, lambda k: halo_second(k, hx, s2, rho2, ph2, fp2, red2))
+    s2_next[...] = own2[:, 1]
+    rho2_next[...] = orho2[1]
+
+
+def far_kernel(s, rho, fl, ph_in, fp_in, red_in, fp2_in, red2_in, ph2_in, s2_next, rho2_next,
+               xb, xc, pops_hbm, phase_hbm, fp, red, fp2, red2,
+               ph, ph2, hx, s2, rho2, own2, orho2, pops_out, phase_out, sems):
+    side = lax.axis_index("gx") % 2
+    ph[...] = ph_in[...]
+    ph2[...] = ph2_in[...]
+    put_message(xb, 0, side, False, hx, ph)
+    put_message(xc, 0, side, True, hx, ph)
+    first = jnp.where(side == 1, NXL - 1, 0)
+    own_finish(first, s, first, rho, fl, ph, fp, red)
+    by_side(side, lambda k: halo_first(k, hx, ph, fp, red))
+    two_planes(side, lambda x, k: own_collide(x, k, fl, fp, red, ph2, own2, orho2))
+    by_side(side, lambda k: halo_collide(k, hx, fp, red, ph2, s2, rho2))
+    own2[:, 2] = s2_next[...]
+    orho2[2] = rho2_next[...]
+
+    def second(k, carry):
+        own_finish(
+            jnp.where(side == 1, NXL - 1 - k, k), own2, k, orho2, fl, ph2, fp2, red2
+        )
         return carry
 
-    lax.fori_loop(0, NXL, second, 0)
-    for side, index, towards, back in sides:
-        for t in range(NT):
-            rows = pl.ds(8 * t, 8)
-            finish(
-                towards, lambda d: s2[POS[d], index, rows, :], ph, rho2[index, rows, :],
-                hx[side, 17, rows, :], index, ROW0 + 8 * t, fp, red,
-            )
+    lax.fori_loop(0, 3, second, 0)
+    by_side(side, lambda k: halo_second(k, hx, s2, rho2, ph2, fp2, red2))
 
     def out_copies(x):
         return (
@@ -565,20 +622,16 @@
             pltpu.make_async_copy(phase_out.at[x], phase_hbm.at[x], sems.at[2 * x + 1]),
         )
 
-    def final(x, carry):
+    for x in range(NXL):
         for t in range(NYL // 8):
             row = ROW0 + 4 + 8 * t
             rows = pl.ds(8 * t, 8)
             total = None
             for d in DIRS:
-                v = arrived(d, fp, x + 1, row)
+                v = arrived(d, fp2, x + 1, row)
                 pops_out[REF_OF[POS[d]], x, rows, :] = v
                 total = v if total is None else total + v
-            phase_out[x, rows, :] = 2.0 * red_arrived(red, x + 1, row) / total - 1.0
-        return carry
-
-    for x in range(NXL):
-        final(x, 0)
+            phase_out[x, rows, :] = 2.0 * red_arrived(red2, x + 1, row) / total - 1.0
         for copy in out_copies(x):
             copy.start()
     for x in range(NXL):
@@ -634,6 +687,7 @@
         for v in (populations, labels, solid_mask)
     ]
 
+    split = [shaped(HALF, EXT, 128), shaped(21 - HALF, EXT, 128)]
     whole = [
         shaped(19, NXL, NYL, 128), jax.ShapeDtypeStruct((NXL, NYL, 128), jnp.int32),
         jax.ShapeDtypeStruct((NXL, NYL, 128), jnp.int32),
@@ -644,27 +698,41 @@
     )(*inputs)
     ya = swap(ya, "gy", 0)
     yb = swap(yb, "gy", 1)
-    *mid, xa, xb = call(
-        start_kernel, [VM] * 3, state + [shaped(21, NYL, 128)] * 2, [], "start",
+    *mid, xa, xd, xb = call(
+        start_kernel, [VM] * 3, state + split + [shaped(21, NYL, 128)], [], "start",
     )(*held)
     xb = swap(xb, "gx", 1)
+    *mid, xa, xd, xc = call(
+        edge_kernel, [VM] * 10, state + split + [shaped(21, 8, 128)],
+        [pltpu.VMEM((21, NXL, 8, 128), F32)], "edge", {2 + i: i for i in range(8)},
+        cost=10 ** 10,
+    )(ya, yb, *mid, xa, xd)
+    xc = swap(xc, "gx", 1)
     xa = swap(xa, "gx", 0)
-    *mid, xd, xc = call(
-        edge_kernel, [VM] * 8, state + [shaped(21, 8, 128)] * 2,
-        [pltpu.VMEM((21, NXL, 8, 128), F32)], "edge", {2 + i: i for i in range(6)}, cost=10 ** 10,
-    )(ya, yb, *mid)
-    xc = swap(xc, "gx", 1)
     xd = swap(xd, "gx", 0)
+    s, rho, fl, ph, fp, red = mid
+    halo = [
+        pltpu.VMEM((21, EXT, 128), F32), pltpu.VMEM((19, NXL + 2, EXT, 128), F32),
+        pltpu.VMEM((NXL + 2, EXT, 128), F32), pltpu.VMEM((19, 3, EXT, 128), F32),
+        pltpu.VMEM((3, EXT, 128), F32),
+    ]
+    phases = pltpu.VMEM((NXL + 4, SROWS, 128), F32)
+    fp, red, fp2, red2, ph2, s2_next, rho2_next = call(
+        near_kernel, [VM] * 8,
+        [state[4], state[5], state[4], state[5], state[3], shaped(19, EXT, 128),
+         shaped(EXT, 128)],
+        [phases] + halo, "near", {4: 0, 5: 1}, cost=0,
+    )(s, rho, fl, ph, fp, red, xa, xd)
     out = call(
-        last_kernel, [VM] * 10,
-        [shaped(19, NXL, NYL, 128), shaped(NXL, NYL, 128)] + state[3:],
-        [
-            pltpu.VMEM((2, 21, EXT, 128), F32), pltpu.VMEM((19, NXL + 2, EXT, 128), F32),
-            pltpu.VMEM((NXL + 2, EXT, 128), F32), pltpu.VMEM((19, NXL, NYL, 128), F32),
-            pltpu.VMEM((NXL, NYL, 128), F32), pltpu.SemaphoreType.DMA((2 * NXL,)),
+        far_kernel, [VM] * 13,
+        [shaped(19, NXL, NYL, 128), shaped(NXL, NYL, 128), state[4], state[5], state[4],
+         state[5]],
+        [phases, phases] + halo + [
+            pltpu.VMEM((19, NXL, NYL, 128), F32), pltpu.VMEM((NXL, NYL, 128), F32),
+            pltpu.SemaphoreType.DMA((2 * NXL,)),
         ],
-        "last", {3: 2, 4: 3, 5: 4}, out_specs=[HB] * 2 + [VM] * 3,
-    )(*mid, xb, xa, xc, xd)
+        "far", {4: 2, 5: 3, 6: 4, 7: 5}, out_specs=[HB] * 2 + [VM] * 4,
+    )(s, rho, fl, ph, fp, red, fp2, red2, ph2, s2_next, rho2_next, xb, xc)
     return out[0], out[1]
 
 

time: 30.3 us -> 30.5 us (level)
  the two profiles are of different devices: /device:TPU:32 before, /device:TPU:8 now
where the time goes in v5:
time: 30.5 us; the launch traced here: 30.4 us
  starting transfers between devices  13.5 us (44%)
  Pallas kernels  8.76 us (29%)
  waiting for transfers between devices  7.54 us (25%)
  between operations  0.67 us (2%)
    ppermute x6, starting transfers between devices, swap(): return lax.ppermute(value, axis, pairs(lax.axis_size(axis), first))  13.5 us
    ppermute x6, waiting for transfers between devices, swap(): return lax.ppermute(value, axis, pairs(lax.axis_size(axis), first))  7.54 us
    pallas_call x1, Pallas kernels, on_device(): call(far_kernel, [VM] * 13, [shaped(19, NXL, NYL, 128), shaped(NXL, NYL,...  3.35 us
    pallas_call x1, Pallas kernels, on_device(): call(near_kernel, [VM] * 8, [state[4], state[5], state[4], state[5], stat...  1.59 us
    pallas_call x1, Pallas kernels, on_device(): call(start_kernel, [VM] * 3, state + split + [shaped(21, NYL, 128)], [],...  1.47 us
    pallas_call x1, Pallas kernels, on_device(): call(pack_kernel, [HB] * 3, [shaped(YROWS, 128)] * 2 + whole, [pltpu.Sema...  1.46 us
    pallas_call x1, Pallas kernels, on_device(): call(edge_kernel, [VM] * 10, state + split + [shaped(21, 8, 128)], [pltpu...  0.89 us
  transfers between devices with their start and end apart: 6, of which 1 were waited for; matrix products, arithmetic and copies ran while one was open for 0% of the time, Pallas kernels for 13%

profile of v5, /device:TPU:8, one launch (start us, length us, event | category | flops | bytes accessed | tf_op | source)
XLA Modules:
  0.0 30.4 jit_solution(3703600894247279442)
XLA Ops:
  0.6 1.5 %pack.1 = (f32[256,128]{1,0:T(8,128)S(1)}, f32[256,128]{1,0:T(8,128)S(1)}, f32[19,4,32,128]{3,2,1,0:T(8,128)S(1)}, s32[4,32,128]{2,1,0:T(8,128)S(1)}, s32[4,32,128]{2,1,0:T(8,128)S(1)}) custom-call(f32[19,4,32,128]{3,2,1,0:T(8,128)} %pops_hbm.1, s32[4,32,128]{2,1,0:T(8,128)} %labels_hbm.1, s32[4,32,128]{2,1,0:T(8,128)} %solid_hbm.1), custom_call_target="tpu_custom_call" | custom-call | tf_op jit(solution)/shard_map/pack/pallas_call | solution.py:695
  2.1 2.3 %collective-permute-start = (f32[256,128]{1,0:T(8,128)S(1)}, f32[256,128]{1,0:T(8,128)S(1)}, u32[]{:S(2)}, u32[]{:S(2)}) collective-permute-start(f32[256,128]{1,0:T(8,128)S(1)} %get-tuple-element.34), channel_id=1, source_target_pairs={{0,1},{1,0},{2,3},{3,2},{4,5},{5,4},{6,7},{7,6},{8,9},{9,8},{10,11... | collective-permute-start | bytes 393224 | tf_op jit(solution)/shard_map/ppermute | solution.py:676
  4.4 0.7 %collective-permute-start.1 = (f32[256,128]{1,0:T(8,128)S(1)}, f32[256,128]{1,0:T(8,128)S(1)}, u32[]{:S(2)}, u32[]{:S(2)}) collective-permute-start(f32[256,128]{1,0:T(8,128)S(1)} %get-tuple-element.35), channel_id=1, source_target_pairs={{1,2},{2,1},{3,4},{4,3},{5,6},{6,5},{7,0},{0,7},{9,10},{10,9},{11,... | collective-permute-start | bytes 393224 | tf_op jit(solution)/shard_map/ppermute | solution.py:676
  5.0 1.5 %start.1 = (f32[19,4,40,128]{3,2,1,0:T(8,128)S(1)}, f32[4,40,128]{2,1,0:T(8,128)S(1)}, f32[4,40,128]{2,1,0:T(8,128)S(1)}, f32[8,56,128]{2,1,0:T(8,128)S(1)}, f32...) custom-call(f32[19,4,32,128]{3,2,1,0:T(8,128)S(1)} %get-tuple-elemen, ...), custom_call_target="tpu_custom_call" | custom-call | tf_op jit(solution)/shard_map/start/pallas_call | solution.py:701
  6.5 7.5 %collective-permute-start.4 = (f32[21,32,128]{2,1,0:T(8,128)S(1)}, f32[21,32,128]{2,1,0:T(8,128)S(1)}, u32[]{:S(2)}, u32[]{:S(2)}) collective-permute-start(f32[21,32,128]{2,1,0:T(8,128)S(1)} %get-tuple-element.62), channel_id=1, source_target_pairs={{8,16},{16,8},{24,32},{32,24},{40,48},{48,40},{56,64},{64,56},{72,... | collective-permute-start | bytes 1032200 | tf_op jit(solution)/shard_map/ppermute | solution.py:676
  14.0 0.0 collective-permute-done.ya
  14.0 0.0 collective-permute-done.1.yb
  14.0 0.9 %edge.1 = (f32[19,4,40,128]{3,2,1,0:T(8,128)S(1)}, f32[4,40,128]{2,1,0:T(8,128)S(1)}, f32[4,40,128]{2,1,0:T(8,128)S(1)}, f32[8,56,128]{2,1,0:T(8,128)S(1)}, f32[...) custom-call(f32[256,128]{1,0:T(8,128)S(1)} %collective-permute-done., ...), custom_call_target="tpu_custom_call", output_to_operand_aliasing={{0}: (2, {}), {1}: (3, {}), {2}: (4, {}), {3}: (5, {}), {4}... | custom-call | flops 10000000000 | bytes 10000000000 | tf_op jit(solution)/shard_map/edge/pallas_call | solution.py:705
  14.9 0.1 collective-permute-start.2
  15.0 0.5 %collective-permute-start.3 = (f32[10,40,128]{2,1,0:T(8,128)S(1)}, f32[10,40,128]{2,1,0:T(8,128)S(1)}, u32[]{:S(2)}, u32[]{:S(2)}) collective-permute-start(f32[10,40,128]{2,1,0:T(8,128)S(1)} %get-tuple-element.54), channel_id=1, source_target_pairs={{0,8},{8,0},{16,24},{24,16},{32,40},{40,32},{48,56},{56,48},{64,72... | collective-permute-start | bytes 614408 | tf_op jit(solution)/shard_map/ppermute | solution.py:676
  15.5 2.5 %collective-permute-start.5 = (f32[21,8,128]{2,1,0:T(8,128)S(1)}, f32[21,8,128]{2,1,0:T(8,128)S(1)}, u32[]{:S(2)}, u32[]{:S(2)}) collective-permute-start(f32[21,8,128]{2,1,0:T(8,128)S(1)} %get-tuple-element.63), channel_id=1, source_target_pairs={{8,16},{16,8},{24,32},{32,24},{40,48},{48,40},{56,64},{64,56},{72,... | collective-permute-start | bytes 258056 | tf_op jit(solution)/shard_map/ppermute | solution.py:676
  17.9 0.0 collective-permute-done.3.xd
  17.9 0.0 collective-permute-done.2.xa
  18.0 1.6 %near.1 = (f32[19,6,56,128]{3,2,1,0:T(8,128)S(1)}, f32[9,6,56,128]{3,2,1,0:T(8,128)S(1)}, f32[19,6,56,128]{3,2,1,0:T(8,128)S(1)}, f32[9,6,56,128]{3,2,1,0:T(8,12...) custom-call(f32[19,4,40,128]{3,2,1,0:T(8,128)S(1)} %get-tuple-elemen, ...), custom_call_target="tpu_custom_call", output_to_operand_aliasing={{0}: (4, {}), {1}: (5, {})} | custom-call | tf_op jit(solution)/shard_map/near/pallas_call | solution.py:720
  19.6 7.5 %collective-permute-done.5.xc = f32[21,8,128]{2,1,0:T(8,128)S(1)} collective-permute-done((f32[21,8,128]{2,1,0:T(8,128)S(1)}, f32[21,8,128]{2,1,0:T(8,128)S(1)}, u32[]{:S(2)}, u32[]{:S(2)}) %collective-permute-start.5) | collective-permute-done | bytes 86048 | tf_op jit(solution)/shard_map/ppermute | solution.py:676
  27.1 0.0 collective-permute-done.4.xb
  27.1 3.3 %far.1 = (f32[19,4,32,128]{3,2,1,0:T(8,128)}, f32[4,32,128]{2,1,0:T(8,128)}, f32[19,6,56,128]{3,2,1,0:T(8,128)S(1)}, f32[9,6,56,128]{3,2,1,0:T(8,128)S(1)}, f32[...) custom-call(f32[19,4,40,128]{3,2,1,0:T(8,128)S(1)} %get-tuple-elemen, ...), custom_call_target="tpu_custom_call", output_to_operand_aliasing={{2}: (4, {}), {3}: (5, {}), {4}: (6, {}), {5}: (7, {})} | custom-call | tf_op jit(solution)/shard_map/far/pallas_call | solution.py:726
Async XLA Ops:
  2.1 11.9 %collective-permute-start = (f32[256,128]{1,0:T(8,128)S(1)}, f32[256,128]{1,0:T(8,128)S(1)}, u32[]{:S(2)}, u32[]{:S(2)}) collective-permute-start(f32[256,128]{1,0:T(8,128)S(1)} %get-tuple-element.34), channel_id=1, source_target_pairs={{0,1},{1,0},{2,3},{3,2},{4,5},{5,4},{6,7},{7,6},{8,9},{9,8},{10,11... | collective-permute-start | bytes 393224 | tf_op jit(solution)/shard_map/ppermute | solution.py:676
  4.4 9.6 %collective-permute-start.1 = (f32[256,128]{1,0:T(8,128)S(1)}, f32[256,128]{1,0:T(8,128)S(1)}, u32[]{:S(2)}, u32[]{:S(2)}) collective-permute-start(f32[256,128]{1,0:T(8,128)S(1)} %get-tuple-element.35), channel_id=1, source_target_pairs={{1,2},{2,1},{3,4},{4,3},{5,6},{6,5},{7,0},{0,7},{9,10},{10,9},{11,... | collective-permute-start | bytes 393224 | tf_op jit(solution)/shard_map/ppermute | solution.py:676
  6.5 20.6 %collective-permute-start.4 = (f32[21,32,128]{2,1,0:T(8,128)S(1)}, f32[21,32,128]{2,1,0:T(8,128)S(1)}, u32[]{:S(2)}, u32[]{:S(2)}) collective-permute-start(f32[21,32,128]{2,1,0:T(8,128)S(1)} %get-tuple-element.62), channel_id=1, source_target_pairs={{8,16},{16,8},{24,32},{32,24},{40,48},{48,40},{56,64},{64,56},{72,... | collective-permute-start | bytes 1032200 | tf_op jit(solution)/shard_map/ppermute | solution.py:676
  14.9 3.1 %collective-permute-start.2 = (f32[11,40,128]{2,1,0:T(8,128)S(1)}, f32[11,40,128]{2,1,0:T(8,128)S(1)}, u32[]{:S(2)}, u32[]{:S(2)}) collective-permute-start(f32[11,40,128]{2,1,0:T(8,128)S(1)} %get-tuple-element.53), channel_id=1, source_target_pairs={{0,8},{8,0},{16,24},{24,16},{32,40},{40,32},{48,56},{56,48},{64,72... | collective-permute-start | bytes 675848 | tf_op jit(solution)/shard_map/ppermute | solution.py:676
  15.0 3.0 %collective-permute-start.3 = (f32[10,40,128]{2,1,0:T(8,128)S(1)}, f32[10,40,128]{2,1,0:T(8,128)S(1)}, u32[]{:S(2)}, u32[]{:S(2)}) collective-permute-start(f32[10,40,128]{2,1,0:T(8,128)S(1)} %get-tuple-element.54), channel_id=1, source_target_pairs={{0,8},{8,0},{16,24},{24,16},{32,40},{40,32},{48,56},{56,48},{64,72... | collective-permute-start | bytes 614408 | tf_op jit(solution)/shard_map/ppermute | solution.py:676
  15.5 11.6 %collective-permute-start.5 = (f32[21,8,128]{2,1,0:T(8,128)S(1)}, f32[21,8,128]{2,1,0:T(8,128)S(1)}, u32[]{:S(2)}, u32[]{:S(2)}) collective-permute-start(f32[21,8,128]{2,1,0:T(8,128)S(1)} %get-tuple-element.63), channel_id=1, source_target_pairs={{8,16},{16,8},{24,32},{32,24},{40,48},{48,40},{56,64},{64,56},{72,... | collective-permute-start | bytes 258056 | tf_op jit(solution)/shard_map/ppermute | solution.py:676

commit v6 on v5

--- a/solution.py
+++ b/solution.py
@@ -475,9 +475,9 @@
     return NXL + 1, DIRS[0:5], DIRS[5:10]
 
 
-def halo_first(side, hx, ph, fp, red):
+def halo_first(side, hx, ph, fp, red, tiles=range(NT)):
     index, towards, _ = side_dirs(side)
-    for t in range(NT):
+    for t in tiles:
         rows = pl.ds(8 * t, 8)
         finish(
             DIRS, lambda d: hx[towards.index(d), rows, :] if d in towards else None, ph,
@@ -485,12 +485,12 @@
         )
 
 
-def halo_collide(side, hx, fp, red, ph, s2, rho2):
+def halo_collide(side, hx, fp, red, ph, s2, rho2, tiles=range(NT)):
     mask = edges()
     index, towards, back = side_dirs(side)
     near, far = (NXL + 2, NXL + 3) if side == 1 else (1, 0)
     outwards = 1.0 if side == 0 else -1.0
-    for t in range(NT):
+    for t in tiles:
         row = ROW0 + 8 * t
         rows = pl.ds(8 * t, 8)
         f = {d: None if d in towards else arrived(d, fp, index, row) for d in DIRS}
@@ -526,9 +526,9 @@
         ph[far, pl.ds(row, 8), :] = pfar
 
 
-def halo_second(side, hx, s2, rho2, ph, fp, red):
+def halo_second(side, hx, s2, rho2, ph, fp, red, tiles=range(NT)):
     index, towards, _ = side_dirs(side)
-    for t in range(NT):
+    for t in tiles:
         rows = pl.ds(8 * t, 8)
         finish(
             towards, lambda d: s2[POS[d], index, rows, :], ph, rho2[index, rows, :],
@@ -536,8 +536,8 @@
         )
 
 
-def own_finish(x, s, k, rho, fl, ph, fp, red):
-    for t in range(NT):
+def own_finish(x, s, k, rho, fl, ph, fp, red, tiles=range(NT)):
+    for t in tiles:
         rows = pl.ds(8 * t, 8)
         finish(
             DIRS, lambda d: s[POS[d], k, rows, :], ph, rho[k, rows, :], fl[x, rows, :],
@@ -545,9 +545,9 @@
         )
 
 
-def own_collide(x, k, fl, fp, red, ph, s2, rho2):
+def own_collide(x, k, fl, fp, red, ph, s2, rho2, tiles=range(NT)):
     mask = edges()
-    for t in range(NT):
+    for t in tiles:
         row = ROW0 + 8 * t
         rows = pl.ds(8 * t, 8)
         f = {d: arrived(d, fp, x + 1, row) for d in DIRS}
@@ -587,56 +587,80 @@
     by_side(side, lambda k: halo_collide(k, hx, fp, red, ph2, s2, rho2))
     own_finish(first, own2, 0, orho2, fl, ph2, fp2, red2)
     by_side(side, lambda k: halo_second(k, hx, s2, rho2, ph2, fp2, red2))
-    s2_next[...] = own2[:, 1]
-    rho2_next[...] = orho2[1]
-
-
-def far_kernel(s, rho, fl, ph_in, fp_in, red_in, fp2_in, red2_in, ph2_in, s2_next, rho2_next,
-               xb, xc, pops_hbm, phase_hbm, fp, red, fp2, red2,
-               ph, ph2, hx, s2, rho2, own2, orho2, pops_out, phase_out, sems):
+    s2_next[:, 0] = own2[:, 1]
+    rho2_next[0] = orho2[1]
+
+
+def far_half(tiles, s, rho, fl, ph, fp, red, fp2, red2, ph2, s2_next, rho2_next, hx, s2,
+             rho2, own2, orho2):
     side = lax.axis_index("gx") % 2
-    ph[...] = ph_in[...]
-    ph2[...] = ph2_in[...]
-    put_message(xb, 0, side, False, hx, ph)
-    put_message(xc, 0, side, True, hx, ph)
     first = jnp.where(side == 1, NXL - 1, 0)
-    own_finish(first, s, first, rho, fl, ph, fp, red)
-    by_side(side, lambda k: halo_first(k, hx, ph, fp, red))
-    two_planes(side, lambda x, k: own_collide(x, k, fl, fp, red, ph2, own2, orho2))
-    by_side(side, lambda k: halo_collide(k, hx, fp, red, ph2, s2, rho2))
-    own2[:, 2] = s2_next[...]
-    orho2[2] = rho2_next[...]
-
-    def second(k, carry):
-        own_finish(
-            jnp.where(side == 1, NXL - 1 - k, k), own2, k, orho2, fl, ph2, fp2, red2
-        )
-        return carry
-
-    lax.fori_loop(0, 3, second, 0)
-    by_side(side, lambda k: halo_second(k, hx, s2, rho2, ph2, fp2, red2))
-
-    def out_copies(x):
-        return (
-            pltpu.make_async_copy(pops_out.at[:, x], pops_hbm.at[:, x], sems.at[2 * x]),
-            pltpu.make_async_copy(phase_out.at[x], phase_hbm.at[x], sems.at[2 * x + 1]),
-        )
+    third = jnp.where(side == 1, NXL - 3, 2)
+    own_finish(first, s, first, rho, fl, ph, fp, red, tiles)
+    by_side(side, lambda k: halo_first(k, hx, ph, fp, red, tiles))
+    two_planes(side, lambda x, k: own_collide(x, k, fl, fp, red, ph2, own2, orho2, tiles))
+    by_side(side, lambda k: halo_collide(k, hx, fp, red, ph2, s2, rho2, tiles))
+    own_finish(third, s2_next, 0, rho2_next, fl, ph2, fp2, red2, tiles)
+    two_planes(
+        side, lambda x, k: own_finish(x, own2, k, orho2, fl, ph2, fp2, red2, tiles)
+    )
+    by_side(side, lambda k: halo_second(k, hx, s2, rho2, ph2, fp2, red2, tiles))
+
+
+def write_out(starts, fp2, red2, pops_out, phase_out, pops_hbm, phase_hbm, sems):
+    def copies(x):
+        out = []
+        for n, r in enumerate(starts):
+            part, rows = pl.ds(8 * n, 8), pl.ds(r, 8)
+            out += [
+                pltpu.make_async_copy(
+                    pops_out.at[:, x, part], pops_hbm.at[:, x, rows], sems.at[4 * x + n]
+                ),
+                pltpu.make_async_copy(
+                    phase_out.at[x, part], phase_hbm.at[x, rows], sems.at[4 * x + 2 + n]
+                ),
+            ]
+        return out
 
     for x in range(NXL):
-        for t in range(NYL // 8):
-            row = ROW0 + 4 + 8 * t
-            rows = pl.ds(8 * t, 8)
+        for n, r in enumerate(starts):
+            row = ROW0 + 4 + r
+            rows = pl.ds(8 * n, 8)
             total = None
             for d in DIRS:
                 v = arrived(d, fp2, x + 1, row)
                 pops_out[REF_OF[POS[d]], x, rows, :] = v
                 total = v if total is None else total + v
             phase_out[x, rows, :] = 2.0 * red_arrived(red2, x + 1, row) / total - 1.0
-        for copy in out_copies(x):
+        for copy in copies(x):
             copy.start()
     for x in range(NXL):
-        for copy in out_copies(x):
+        for copy in copies(x):
             copy.wait()
+
+
+def far_kernel(s, rho, fl, ph_in, fp_in, red_in, fp2_in, red2_in, ph2_in, s2_next, rho2_next,
+               xb, pops_hbm, phase_hbm, fp, red, fp2, red2, ph, ph2, hx,
+               s2, rho2, own2, orho2, pops_out, phase_out, sems):
+    ph[...] = ph_in[...]
+    ph2[...] = ph2_in[...]
+    put_message(xb, 0, lax.axis_index("gx") % 2, False, hx, ph)
+    far_half(
+        range(NT), s, rho, fl, ph, fp, red, fp2, red2, ph2, s2_next, rho2_next, hx, s2,
+        rho2, own2, orho2,
+    )
+    write_out((8, 16), fp2, red2, pops_out, phase_out, pops_hbm, phase_hbm, sems)
+
+
+def end_kernel(s, rho, fl, s2_next, rho2_next, xc, pops_in, phase_in, fp_in, red_in, fp2_in,
+               red2_in, ph_in, ph2_in, hx_in, pops_hbm, phase_hbm, fp, red, fp2, red2, ph, ph2,
+               hx, s2, rho2, own2, orho2, pops_out, phase_out, sems):
+    put_message(xc, 0, lax.axis_index("gx") % 2, True, hx, ph)
+    far_half(
+        (0, NT - 1), s, rho, fl, ph, fp, red, fp2, red2, ph2, s2_next, rho2_next, hx, s2,
+        rho2, own2, orho2,
+    )
+    write_out((0, NYL - 8), fp2, red2, pops_out, phase_out, pops_hbm, phase_hbm, sems)
 
 
 F32 = jnp.float32
@@ -713,26 +737,33 @@
     s, rho, fl, ph, fp, red = mid
     halo = [
         pltpu.VMEM((21, EXT, 128), F32), pltpu.VMEM((19, NXL + 2, EXT, 128), F32),
-        pltpu.VMEM((NXL + 2, EXT, 128), F32), pltpu.VMEM((19, 3, EXT, 128), F32),
-        pltpu.VMEM((3, EXT, 128), F32),
+        pltpu.VMEM((NXL + 2, EXT, 128), F32), pltpu.VMEM((19, 2, EXT, 128), F32),
+        pltpu.VMEM((2, EXT, 128), F32),
     ]
     phases = pltpu.VMEM((NXL + 4, SROWS, 128), F32)
     fp, red, fp2, red2, ph2, s2_next, rho2_next = call(
         near_kernel, [VM] * 8,
-        [state[4], state[5], state[4], state[5], state[3], shaped(19, EXT, 128),
-         shaped(EXT, 128)],
+        [state[4], state[5], state[4], state[5], state[3], shaped(19, 1, EXT, 128),
+         shaped(1, EXT, 128)],
         [phases] + halo, "near", {4: 0, 5: 1}, cost=0,
     )(s, rho, fl, ph, fp, red, xa, xd)
+    results = [
+        shaped(19, NXL, NYL, 128), shaped(NXL, NYL, 128), state[4], state[5], state[4],
+        state[5], state[3], state[3], shaped(21, EXT, 128),
+    ]
+    work = halo[1:] + [
+        pltpu.VMEM((19, NXL, 16, 128), F32), pltpu.VMEM((NXL, 16, 128), F32),
+        pltpu.SemaphoreType.DMA((4 * NXL,)),
+    ]
+    spaces = [HB] * 2 + [VM] * 7
     out = call(
-        far_kernel, [VM] * 13,
-        [shaped(19, NXL, NYL, 128), shaped(NXL, NYL, 128), state[4], state[5], state[4],
-         state[5]],
-        [phases, phases] + halo + [
-            pltpu.VMEM((19, NXL, NYL, 128), F32), pltpu.VMEM((NXL, NYL, 128), F32),
-            pltpu.SemaphoreType.DMA((2 * NXL,)),
-        ],
-        "far", {4: 2, 5: 3, 6: 4, 7: 5}, out_specs=[HB] * 2 + [VM] * 4,
-    )(s, rho, fl, ph, fp, red, fp2, red2, ph2, s2_next, rho2_next, xb, xc)
+        far_kernel, [VM] * 12, results, work, "far", {4: 2, 5: 3, 6: 4, 7: 5},
+        out_specs=spaces,
+    )(s, rho, fl, ph, fp, red, fp2, red2, ph2, s2_next, rho2_next, xb)
+    out = call(
+        end_kernel, [VM] * 6 + spaces, results, work, "end", {6 + i: i for i in range(9)},
+        out_specs=spaces,
+    )(s, rho, fl, s2_next, rho2_next, xc, *out)
     return out[0], out[1]
 
 

time: 30.5 us -> 29.6 us (0.970)
  waiting for transfers between devices: 7.54 us -> 4.4 us
  Pallas kernels: 8.76 us -> 11 us
    ppermute x6, waiting for transfers between devices: 7.54 us -> 4.4 us  [swap(): return lax.ppermute(value, axis, pairs(lax.axis_size(axis), first))]
    pallas_call x1 -> x2, Pallas kernels: 3.35 us -> 5.55 us  [the longest x1 3.13 us: on_device(): call(far_kernel, [VM] * 12, results, work, 'far', {4: 2, 5: 3, 6: 4, 7: 5...]
  transfers between devices with their start and end apart: 6 -> 6, of which waited for: 1 -> 2; matrix products, arithmetic and copies ran while one was open for 0% -> 0% of each run, Pallas kernels for 13% -> 24%
where the time goes in v6:
time: 29.6 us; the launch traced here: 29.5 us
  starting transfers between devices  13.5 us (46%)
  Pallas kernels  11 us (37%)
  waiting for transfers between devices  4.4 us (15%)
  between operations  0.68 us (2%)
    ppermute x6, starting transfers between devices, swap(): return lax.ppermute(value, axis, pairs(lax.axis_size(axis), first))  13.5 us
    ppermute x6, waiting for transfers between devices, swap(): return lax.ppermute(value, axis, pairs(lax.axis_size(axis), first))  4.4 us
    pallas_call x1, Pallas kernels, on_device(): call(far_kernel, [VM] * 12, results, work, 'far', {4: 2, 5: 3, 6: 4, 7: 5...  3.13 us
    pallas_call x1, Pallas kernels, on_device(): call(end_kernel, [VM] * 6 + spaces, results, work, 'end', {6 + i: i for i...  2.42 us
    pallas_call x1, Pallas kernels, on_device(): call(near_kernel, [VM] * 8, [state[4], state[5], state[4], state[5], stat...  1.59 us
    pallas_call x1, Pallas kernels, on_device(): call(start_kernel, [VM] * 3, state + split + [shaped(21, NYL, 128)], [],...  1.47 us
    pallas_call x1, Pallas kernels, on_device(): call(pack_kernel, [HB] * 3, [shaped(YROWS, 128)] * 2 + whole, [pltpu.Sema...  1.46 us
    pallas_call x1, Pallas kernels, on_device(): call(edge_kernel, [VM] * 10, state + split + [shaped(21, 8, 128)], [pltpu...  0.89 us
  transfers between devices with their start and end apart: 6, of which 2 were waited for; matrix products, arithmetic and copies ran while one was open for 0% of the time, Pallas kernels for 24%

profile of v6, /device:TPU:8, one launch (start us, length us, event | category | flops | bytes accessed | tf_op | source)
XLA Modules:
  0.0 29.5 jit_solution(4719793155321268698)
XLA Ops:
  0.6 1.5 %pack.1 = (f32[256,128]{1,0:T(8,128)S(1)}, f32[256,128]{1,0:T(8,128)S(1)}, f32[19,4,32,128]{3,2,1,0:T(8,128)S(1)}, s32[4,32,128]{2,1,0:T(8,128)S(1)}, s32[4,32,128]{2,1,0:T(8,128)S(1)}) custom-call(f32[19,4,32,128]{3,2,1,0:T(8,128)} %pops_hbm.1, s32[4,32,128]{2,1,0:T(8,128)} %labels_hbm.1, s32[4,32,128]{2,1,0:T(8,128)} %solid_hbm.1), custom_call_target="tpu_custom_call" | custom-call | tf_op jit(solution)/shard_map/pack/pallas_call | solution.py:719
  2.1 2.3 %collective-permute-start = (f32[256,128]{1,0:T(8,128)S(1)}, f32[256,128]{1,0:T(8,128)S(1)}, u32[]{:S(2)}, u32[]{:S(2)}) collective-permute-start(f32[256,128]{1,0:T(8,128)S(1)} %get-tuple-element.43), channel_id=1, source_target_pairs={{0,1},{1,0},{2,3},{3,2},{4,5},{5,4},{6,7},{7,6},{8,9},{9,8},{10,11... | collective-permute-start | bytes 393224 | tf_op jit(solution)/shard_map/ppermute | solution.py:700
  4.4 0.7 %collective-permute-start.1 = (f32[256,128]{1,0:T(8,128)S(1)}, f32[256,128]{1,0:T(8,128)S(1)}, u32[]{:S(2)}, u32[]{:S(2)}) collective-permute-start(f32[256,128]{1,0:T(8,128)S(1)} %get-tuple-element.44), channel_id=1, source_target_pairs={{1,2},{2,1},{3,4},{4,3},{5,6},{6,5},{7,0},{0,7},{9,10},{10,9},{11,... | collective-permute-start | bytes 393224 | tf_op jit(solution)/shard_map/ppermute | solution.py:700
  5.0 1.5 %start.1 = (f32[19,4,40,128]{3,2,1,0:T(8,128)S(1)}, f32[4,40,128]{2,1,0:T(8,128)S(1)}, f32[4,40,128]{2,1,0:T(8,128)S(1)}, f32[8,56,128]{2,1,0:T(8,128)S(1)}, f32...) custom-call(f32[19,4,32,128]{3,2,1,0:T(8,128)S(1)} %get-tuple-elemen, ...), custom_call_target="tpu_custom_call" | custom-call | tf_op jit(solution)/shard_map/start/pallas_call | solution.py:725
  6.5 7.5 %collective-permute-start.5 = (f32[21,32,128]{2,1,0:T(8,128)S(1)}, f32[21,32,128]{2,1,0:T(8,128)S(1)}, u32[]{:S(2)}, u32[]{:S(2)}) collective-permute-start(f32[21,32,128]{2,1,0:T(8,128)S(1)} %get-tuple-element.72), channel_id=1, source_target_pairs={{8,16},{16,8},{24,32},{32,24},{40,48},{48,40},{56,64},{64,56},{72,... | collective-permute-start | bytes 1032200 | tf_op jit(solution)/shard_map/ppermute | solution.py:700
  14.0 0.0 collective-permute-done.ya
  14.0 0.0 collective-permute-done.1.yb
  14.0 0.9 %edge.1 = (f32[19,4,40,128]{3,2,1,0:T(8,128)S(1)}, f32[4,40,128]{2,1,0:T(8,128)S(1)}, f32[4,40,128]{2,1,0:T(8,128)S(1)}, f32[8,56,128]{2,1,0:T(8,128)S(1)}, f32[...) custom-call(f32[256,128]{1,0:T(8,128)S(1)} %collective-permute-done., ...), custom_call_target="tpu_custom_call", output_to_operand_aliasing={{0}: (2, {}), {1}: (3, {}), {2}: (4, {}), {3}: (5, {}), {4}... | custom-call | flops 10000000000 | bytes 10000000000 | tf_op jit(solution)/shard_map/edge/pallas_call | solution.py:729
  14.9 0.1 collective-permute-start.2
  15.0 0.5 %collective-permute-start.3 = (f32[10,40,128]{2,1,0:T(8,128)S(1)}, f32[10,40,128]{2,1,0:T(8,128)S(1)}, u32[]{:S(2)}, u32[]{:S(2)}) collective-permute-start(f32[10,40,128]{2,1,0:T(8,128)S(1)} %get-tuple-element.63), channel_id=1, source_target_pairs={{0,8},{8,0},{16,24},{24,16},{32,40},{40,32},{48,56},{56,48},{64,72... | collective-permute-start | bytes 614408 | tf_op jit(solution)/shard_map/ppermute | solution.py:700
  15.5 2.5 %collective-permute-start.4 = (f32[21,8,128]{2,1,0:T(8,128)S(1)}, f32[21,8,128]{2,1,0:T(8,128)S(1)}, u32[]{:S(2)}, u32[]{:S(2)}) collective-permute-start(f32[21,8,128]{2,1,0:T(8,128)S(1)} %get-tuple-element.66), channel_id=1, source_target_pairs={{8,16},{16,8},{24,32},{32,24},{40,48},{48,40},{56,64},{64,56},{72,... | collective-permute-start | bytes 258056 | tf_op jit(solution)/shard_map/ppermute | solution.py:700
  17.9 0.0 collective-permute-done.3.xd
  17.9 0.0 collective-permute-done.2.xa
  18.0 1.6 %near.1 = (f32[19,6,56,128]{3,2,1,0:T(8,128)S(1)}, f32[9,6,56,128]{3,2,1,0:T(8,128)S(1)}, f32[19,6,56,128]{3,2,1,0:T(8,128)S(1)}, f32[9,6,56,128]{3,2,1,0:T(8,12...) custom-call(f32[19,4,40,128]{3,2,1,0:T(8,128)S(1)} %get-tuple-elemen, ...), custom_call_target="tpu_custom_call", output_to_operand_aliasing={{0}: (4, {}), {1}: (5, {})} | custom-call | tf_op jit(solution)/shard_map/near/pallas_call | solution.py:744
  19.6 3.8 %collective-permute-done.5.xb = f32[21,32,128]{2,1,0:T(8,128)S(1)} collective-permute-done((f32[21,32,128]{2,1,0:T(8,128)S(1)}, f32[21,32,128]{2,1,0:T(8,128)S(1)}, u32[]{:S(2)}, u32[]{:S(2)}) %collective-permute-start.5) | collective-permute-done | bytes 344096 | tf_op jit(solution)/shard_map/ppermute | solution.py:700
  23.4 3.1 %far.1 = (f32[19,4,32,128]{3,2,1,0:T(8,128)}, f32[4,32,128]{2,1,0:T(8,128)}, f32[19,6,56,128]{3,2,1,0:T(8,128)S(1)}, f32[9,6,56,128]{3,2,1,0:T(8,128)S(1)}, f32[...) custom-call(f32[19,4,40,128]{3,2,1,0:T(8,128)S(1)} %get-tuple-elemen, ...), custom_call_target="tpu_custom_call", output_to_operand_aliasing={{2}: (4, {}), {3}: (5, {}), {4}: (6, {}), {5}: (7, {})} | custom-call | tf_op jit(solution)/shard_map/far/pallas_call | solution.py:759
  26.5 0.5 %collective-permute-done.4.xc = f32[21,8,128]{2,1,0:T(8,128)S(1)} collective-permute-done((f32[21,8,128]{2,1,0:T(8,128)S(1)}, f32[21,8,128]{2,1,0:T(8,128)S(1)}, u32[]{:S(2)}, u32[]{:S(2)}) %collective-permute-start.4) | collective-permute-done | bytes 86048 | tf_op jit(solution)/shard_map/ppermute | solution.py:700
  27.1 2.4 %end.1 = (f32[19,4,32,128]{3,2,1,0:T(8,128)}, f32[4,32,128]{2,1,0:T(8,128)}, f32[19,6,56,128]{3,2,1,0:T(8,128)S(1)}, f32[9,6,56,128]{3,2,1,0:T(8,128)S(1)}, f32[...) custom-call(f32[19,4,40,128]{3,2,1,0:T(8,128)S(1)} %get-tuple-elemen, ...), custom_call_target="tpu_custom_call", output_to_operand_aliasing={{0}: (6, {}), {1}: (7, {}), {2}: (8, {}), {3}: (9, {}), {4}... | custom-call | tf_op jit(solution)/shard_map/end/pallas_call | solution.py:763
Async XLA Ops:
  2.1 11.9 %collective-permute-start = (f32[256,128]{1,0:T(8,128)S(1)}, f32[256,128]{1,0:T(8,128)S(1)}, u32[]{:S(2)}, u32[]{:S(2)}) collective-permute-start(f32[256,128]{1,0:T(8,128)S(1)} %get-tuple-element.43), channel_id=1, source_target_pairs={{0,1},{1,0},{2,3},{3,2},{4,5},{5,4},{6,7},{7,6},{8,9},{9,8},{10,11... | collective-permute-start | bytes 393224 | tf_op jit(solution)/shard_map/ppermute | solution.py:700
  4.4 9.6 %collective-permute-start.1 = (f32[256,128]{1,0:T(8,128)S(1)}, f32[256,128]{1,0:T(8,128)S(1)}, u32[]{:S(2)}, u32[]{:S(2)}) collective-permute-start(f32[256,128]{1,0:T(8,128)S(1)} %get-tuple-element.44), channel_id=1, source_target_pairs={{1,2},{2,1},{3,4},{4,3},{5,6},{6,5},{7,0},{0,7},{9,10},{10,9},{11,... | collective-permute-start | bytes 393224 | tf_op jit(solution)/shard_map/ppermute | solution.py:700
  6.5 16.9 %collective-permute-start.5 = (f32[21,32,128]{2,1,0:T(8,128)S(1)}, f32[21,32,128]{2,1,0:T(8,128)S(1)}, u32[]{:S(2)}, u32[]{:S(2)}) collective-permute-start(f32[21,32,128]{2,1,0:T(8,128)S(1)} %get-tuple-element.72), channel_id=1, source_target_pairs={{8,16},{16,8},{24,32},{32,24},{40,48},{48,40},{56,64},{64,56},{72,... | collective-permute-start | bytes 1032200 | tf_op jit(solution)/shard_map/ppermute | solution.py:700
  14.9 3.1 %collective-permute-start.2 = (f32[11,40,128]{2,1,0:T(8,128)S(1)}, f32[11,40,128]{2,1,0:T(8,128)S(1)}, u32[]{:S(2)}, u32[]{:S(2)}) collective-permute-start(f32[11,40,128]{2,1,0:T(8,128)S(1)} %get-tuple-element.62), channel_id=1, source_target_pairs={{0,8},{8,0},{16,24},{24,16},{32,40},{40,32},{48,56},{56,48},{64,72... | collective-permute-start | bytes 675848 | tf_op jit(solution)/shard_map/ppermute | solution.py:700
  15.0 3.0 %collective-permute-start.3 = (f32[10,40,128]{2,1,0:T(8,128)S(1)}, f32[10,40,128]{2,1,0:T(8,128)S(1)}, u32[]{:S(2)}, u32[]{:S(2)}) collective-permute-start(f32[10,40,128]{2,1,0:T(8,128)S(1)} %get-tuple-element.63), channel_id=1, source_target_pairs={{0,8},{8,0},{16,24},{24,16},{32,40},{40,32},{48,56},{56,48},{64,72... | collective-permute-start | bytes 614408 | tf_op jit(solution)/shard_map/ppermute | solution.py:700
  15.5 11.6 %collective-permute-start.4 = (f32[21,8,128]{2,1,0:T(8,128)S(1)}, f32[21,8,128]{2,1,0:T(8,128)S(1)}, u32[]{:S(2)}, u32[]{:S(2)}) collective-permute-start(f32[21,8,128]{2,1,0:T(8,128)S(1)} %get-tuple-element.66), channel_id=1, source_target_pairs={{8,16},{16,8},{24,32},{32,24},{40,48},{48,40},{56,64},{64,56},{72,... | collective-permute-start | bytes 258056 | tf_op jit(solution)/shard_map/ppermute | solution.py:700

commit v7 on v6

--- a/solution.py
+++ b/solution.py
@@ -279,6 +279,31 @@
                 plane_of(msg, j)[pl.ds(8 * n, 8), :] = v
 
 
+def far_spans():
+    out = []
+    for i, j in enumerate(PLAIN):
+        out += [(j, NYL * i + r, r) for r in range(0, NYL, 8)]
+    base = NYL * len(PLAIN)
+    for i, j in enumerate(MOVED):
+        out += [(j, base + (NYL - 4) * i + r - 2, r) for r in (2, 10, 18, 22)]
+    return out
+
+
+FAR_ROWS = NYL * len(PLAIN) + (NYL - 4) * len(MOVED)
+
+
+def far_message(msg, high, state):
+    values = {}
+    for r in range(0, NYL, 8):
+        part = message_tile(high, ROW0 + 4 + r, *state)[0]()
+        values.update({(j, r): v for j, v in zip(PLAIN, part[0] + part[1])})
+    for r in (2, 10, 18, 22):
+        part = message_tile(high, ROW0 + 4 + r, *state)[1]()
+        values.update({(j, r): v for j, v in zip(MOVED, part[0] + part[1])})
+    for j, row, r in far_spans():
+        msg[pl.ds(row, 8), :] = values[j, r]
+
+
 def corner_message(msg, base, high, state):
     for n, (first, second) in enumerate(((0, 2), (EXT - 8, EXT - 6))):
         plain, _ = message_tile(high, ROW0 + first, *state)
@@ -375,7 +400,7 @@
     lax.fori_loop(0, NXL, plane, 0)
     inner_step(range(NT), s, rho, fl, ph, fp, red)
     low_a = lax.axis_index("gx") % 2 == 1
-    main_message(xb, low_a, (s, rho, fl, ph, fp, red))
+    far_message(xb, low_a, (s, rho, fl, ph, fp, red))
     main_message((xa, xd), jnp.logical_not(low_a), (s, rho, fl, ph, fp, red))
 
 
@@ -462,6 +487,17 @@
                 ph[near if j == 15 else far, pl.ds(ROW0 + to, n), :] = v
             else:
                 hx[j, pl.ds(to, n), :] = v
+
+
+def put_far(src, side, hx, ph):
+    near = jnp.where(side == 1, NXL + 2, 1)
+    far = jnp.where(side == 1, NXL + 3, 0)
+    for j, row, r in far_spans():
+        v = src[pl.ds(row, 8), :]
+        if j in (15, 16):
+            ph[near if j == 15 else far, pl.ds(ROW0 + 4 + r, 8), :] = v
+        else:
+            hx[j, pl.ds(4 + r, 8), :] = v
 
 
 def by_side(side, step):
@@ -607,60 +643,76 @@
     by_side(side, lambda k: halo_second(k, hx, s2, rho2, ph2, fp2, red2, tiles))
 
 
-def write_out(starts, fp2, red2, pops_out, phase_out, pops_hbm, phase_hbm, sems):
-    def copies(x):
-        out = []
-        for n, r in enumerate(starts):
-            part, rows = pl.ds(8 * n, 8), pl.ds(r, 8)
-            out += [
-                pltpu.make_async_copy(
-                    pops_out.at[:, x, part], pops_hbm.at[:, x, rows], sems.at[4 * x + n]
-                ),
-                pltpu.make_async_copy(
-                    phase_out.at[x, part], phase_hbm.at[x, rows], sems.at[4 * x + 2 + n]
-                ),
-            ]
-        return out
-
-    for x in range(NXL):
-        for n, r in enumerate(starts):
-            row = ROW0 + 4 + r
-            rows = pl.ds(8 * n, 8)
-            total = None
-            for d in DIRS:
-                v = arrived(d, fp2, x + 1, row)
-                pops_out[REF_OF[POS[d]], x, rows, :] = v
-                total = v if total is None else total + v
-            phase_out[x, rows, :] = 2.0 * red_arrived(red2, x + 1, row) / total - 1.0
-        for copy in copies(x):
-            copy.start()
-    for x in range(NXL):
-        for copy in copies(x):
-            copy.wait()
+def move_last(x, starts, fp2, red2, pops_out, phase_out):
+    for n, r in enumerate(starts):
+        row = ROW0 + 4 + r
+        rows = pl.ds(8 * n, 8)
+        total = None
+        for d in DIRS:
+            v = arrived(d, fp2, x + 1, row)
+            pops_out[REF_OF[POS[d]], x, rows, :] = v
+            total = v if total is None else total + v
+        phase_out[x, rows, :] = 2.0 * red_arrived(red2, x + 1, row) / total - 1.0
 
 
 def far_kernel(s, rho, fl, ph_in, fp_in, red_in, fp2_in, red2_in, ph2_in, s2_next, rho2_next,
-               xb, pops_hbm, phase_hbm, fp, red, fp2, red2, ph, ph2, hx,
-               s2, rho2, own2, orho2, pops_out, phase_out, sems):
+               xb, pops_mid, phase_mid, fp, red, fp2, red2, ph, ph2, hx,
+               s2, rho2, own2, orho2):
     ph[...] = ph_in[...]
     ph2[...] = ph2_in[...]
-    put_message(xb, 0, lax.axis_index("gx") % 2, False, hx, ph)
+    put_far(xb, lax.axis_index("gx") % 2, hx, ph)
     far_half(
         range(NT), s, rho, fl, ph, fp, red, fp2, red2, ph2, s2_next, rho2_next, hx, s2,
         rho2, own2, orho2,
     )
-    write_out((8, 16), fp2, red2, pops_out, phase_out, pops_hbm, phase_hbm, sems)
-
-
-def end_kernel(s, rho, fl, s2_next, rho2_next, xc, pops_in, phase_in, fp_in, red_in, fp2_in,
+    for x in range(NXL):
+        move_last(x, (8, 16), fp2, red2, pops_mid, phase_mid)
+
+
+def end_kernel(s, rho, fl, s2_next, rho2_next, xc, pops_mid, phase_mid, fp_in, red_in, fp2_in,
                red2_in, ph_in, ph2_in, hx_in, pops_hbm, phase_hbm, fp, red, fp2, red2, ph, ph2,
                hx, s2, rho2, own2, orho2, pops_out, phase_out, sems):
+    middle = pl.ds(8, 16)
+
+    def middle_copies(x):
+        return (
+            pltpu.make_async_copy(
+                pops_mid.at[:, x], pops_hbm.at[:, x, middle], sems.at[6 * x]
+            ),
+            pltpu.make_async_copy(
+                phase_mid.at[x], phase_hbm.at[x, middle], sems.at[6 * x + 1]
+            ),
+        )
+
+    def edge_copies(x):
+        out = []
+        for n, r in enumerate((0, NYL - 8)):
+            part, rows = pl.ds(8 * n, 8), pl.ds(r, 8)
+            out += [
+                pltpu.make_async_copy(
+                    pops_out.at[:, x, part], pops_hbm.at[:, x, rows], sems.at[6 * x + 2 + n]
+                ),
+                pltpu.make_async_copy(
+                    phase_out.at[x, part], phase_hbm.at[x, rows], sems.at[6 * x + 4 + n]
+                ),
+            ]
+        return out
+
+    for x in range(NXL):
+        for copy in middle_copies(x):
+            copy.start()
     put_message(xc, 0, lax.axis_index("gx") % 2, True, hx, ph)
     far_half(
         (0, NT - 1), s, rho, fl, ph, fp, red, fp2, red2, ph2, s2_next, rho2_next, hx, s2,
         rho2, own2, orho2,
     )
-    write_out((0, NYL - 8), fp2, red2, pops_out, phase_out, pops_hbm, phase_hbm, sems)
+    for x in range(NXL):
+        move_last(x, (0, NYL - 8), fp2, red2, pops_out, phase_out)
+        for copy in edge_copies(x):
+            copy.start()
+    for x in range(NXL):
+        for copy in (*middle_copies(x), *edge_copies(x)):
+            copy.wait()
 
 
 F32 = jnp.float32
@@ -723,7 +775,7 @@
     ya = swap(ya, "gy", 0)
     yb = swap(yb, "gy", 1)
     *mid, xa, xd, xb = call(
-        start_kernel, [VM] * 3, state + split + [shaped(21, NYL, 128)], [], "start",
+        start_kernel, [VM] * 3, state + split + [shaped(FAR_ROWS, 128)], [], "start",
     )(*held)
     xb = swap(xb, "gx", 1)
     *mid, xa, xd, xc = call(
@@ -747,23 +799,20 @@
          shaped(1, EXT, 128)],
         [phases] + halo, "near", {4: 0, 5: 1}, cost=0,
     )(s, rho, fl, ph, fp, red, xa, xd)
-    results = [
-        shaped(19, NXL, NYL, 128), shaped(NXL, NYL, 128), state[4], state[5], state[4],
-        state[5], state[3], state[3], shaped(21, EXT, 128),
-    ]
-    work = halo[1:] + [
-        pltpu.VMEM((19, NXL, 16, 128), F32), pltpu.VMEM((NXL, 16, 128), F32),
-        pltpu.SemaphoreType.DMA((4 * NXL,)),
-    ]
-    spaces = [HB] * 2 + [VM] * 7
-    out = call(
-        far_kernel, [VM] * 12, results, work, "far", {4: 2, 5: 3, 6: 4, 7: 5},
-        out_specs=spaces,
+    held = [state[4], state[5], state[4], state[5], state[3], state[3], shaped(21, EXT, 128)]
+    *mids, fp, red, fp2, red2, ph, ph2, hx = call(
+        far_kernel, [VM] * 12, [shaped(19, NXL, 16, 128), shaped(NXL, 16, 128)] + held,
+        halo[1:], "far", {4: 2, 5: 3, 6: 4, 7: 5},
     )(s, rho, fl, ph, fp, red, fp2, red2, ph2, s2_next, rho2_next, xb)
     out = call(
-        end_kernel, [VM] * 6 + spaces, results, work, "end", {6 + i: i for i in range(9)},
-        out_specs=spaces,
-    )(s, rho, fl, s2_next, rho2_next, xc, *out)
+        end_kernel, [VM] * 15,
+        [shaped(19, NXL, NYL, 128), shaped(NXL, NYL, 128)] + held,
+        halo[1:] + [
+            pltpu.VMEM((19, NXL, 16, 128), F32), pltpu.VMEM((NXL, 16, 128), F32),
+            pltpu.SemaphoreType.DMA((6 * NXL,)),
+        ],
+        "end", {8 + i: 2 + i for i in range(7)}, out_specs=[HB] * 2 + [VM] * 7,
+    )(s, rho, fl, s2_next, rho2_next, xc, *mids, fp, red, fp2, red2, ph, ph2, hx)
     return out[0], out[1]
 
 

time: 29.6 us -> 29.4 us (level)
  Pallas kernels: 11 us -> 10.2 us
  waiting for transfers between devices: 4.4 us -> 5.05 us
    pallas_call x3, Pallas kernels: 7.03 us -> 6.22 us  [the longest x1 2.49 us: on_device(): call(end_kernel, [VM] * 15, [shaped(19, NXL, NYL, 128), shaped(NXL, NYL,...]
    ppermute x6, waiting for transfers between devices: 4.4 us -> 5.05 us  [swap(): return lax.ppermute(value, axis, pairs(lax.axis_size(axis), first))]
  transfers between devices with their start and end apart: 6 -> 6, of which waited for: 2 -> 2; matrix products, arithmetic and copies ran while one was open for 0% -> 0% of each run, Pallas kernels for 24% -> 21%
where the time goes in v7:
time: 29.4 us; the launch traced here: 29.3 us
  starting transfers between devices  13.4 us (46%)
  Pallas kernels  10.2 us (35%)
  waiting for transfers between devices  5.05 us (17%)
  between operations  0.68 us (2%)
    ppermute x6, starting transfers between devices, swap(): return lax.ppermute(value, axis, pairs(lax.axis_size(axis), first))  13.4 us
    ppermute x6, waiting for transfers between devices, swap(): return lax.ppermute(value, axis, pairs(lax.axis_size(axis), first))  5.05 us
    pallas_call x1, Pallas kernels, on_device(): call(end_kernel, [VM] * 15, [shaped(19, NXL, NYL, 128), shaped(NXL, NYL,...  2.49 us
    pallas_call x1, Pallas kernels, on_device(): call(far_kernel, [VM] * 12, [shaped(19, NXL, 16, 128), shaped(NXL, 16, 12...  2.24 us
    pallas_call x1, Pallas kernels, on_device(): call(near_kernel, [VM] * 8, [state[4], state[5], state[4], state[5], stat...  1.59 us
    pallas_call x1, Pallas kernels, on_device(): call(start_kernel, [VM] * 3, state + split + [shaped(FAR_ROWS, 128)], [],...  1.49 us
    pallas_call x1, Pallas kernels, on_device(): call(pack_kernel, [HB] * 3, [shaped(YROWS, 128)] * 2 + whole, [pltpu.Sema...  1.46 us
    pallas_call x1, Pallas kernels, on_device(): call(edge_kernel, [VM] * 10, state + split + [shaped(21, 8, 128)], [pltpu...  0.88 us
  transfers between devices with their start and end apart: 6, of which 2 were waited for; matrix products, arithmetic and copies ran while one was open for 0% of the time, Pallas kernels for 21%

profile of v7, /device:TPU:8, one launch (start us, length us, event | category | flops | bytes accessed | tf_op | source)
XLA Modules:
  0.0 29.3 jit_solution(17020235700913920119)
XLA Ops:
  0.6 1.5 %pack.1 = (f32[256,128]{1,0:T(8,128)S(1)}, f32[256,128]{1,0:T(8,128)S(1)}, f32[19,4,32,128]{3,2,1,0:T(8,128)S(1)}, s32[4,32,128]{2,1,0:T(8,128)S(1)}, s32[4,32,128]{2,1,0:T(8,128)S(1)}) custom-call(f32[19,4,32,128]{3,2,1,0:T(8,128)} %pops_hbm.1, s32[4,32,128]{2,1,0:T(8,128)} %labels_hbm.1, s32[4,32,128]{2,1,0:T(8,128)} %solid_hbm.1), custom_call_target="tpu_custom_call" | custom-call | tf_op jit(solution)/shard_map/pack/pallas_call | solution.py:771
  2.1 2.3 %collective-permute-start = (f32[256,128]{1,0:T(8,128)S(1)}, f32[256,128]{1,0:T(8,128)S(1)}, u32[]{:S(2)}, u32[]{:S(2)}) collective-permute-start(f32[256,128]{1,0:T(8,128)S(1)} %get-tuple-element.43), channel_id=1, source_target_pairs={{0,1},{1,0},{2,3},{3,2},{4,5},{5,4},{6,7},{7,6},{8,9},{9,8},{10,11... | collective-permute-start | bytes 393224 | tf_op jit(solution)/shard_map/ppermute | solution.py:752
  4.4 0.7 %collective-permute-start.1 = (f32[256,128]{1,0:T(8,128)S(1)}, f32[256,128]{1,0:T(8,128)S(1)}, u32[]{:S(2)}, u32[]{:S(2)}) collective-permute-start(f32[256,128]{1,0:T(8,128)S(1)} %get-tuple-element.44), channel_id=1, source_target_pairs={{1,2},{2,1},{3,4},{4,3},{5,6},{6,5},{7,0},{0,7},{9,10},{10,9},{11,... | collective-permute-start | bytes 393224 | tf_op jit(solution)/shard_map/ppermute | solution.py:752
  5.0 1.5 %start.1 = (f32[19,4,40,128]{3,2,1,0:T(8,128)S(1)}, f32[4,40,128]{2,1,0:T(8,128)S(1)}, f32[4,40,128]{2,1,0:T(8,128)S(1)}, f32[8,56,128]{2,1,0:T(8,128)S(1)}, f32...) custom-call(f32[19,4,32,128]{3,2,1,0:T(8,128)S(1)} %get-tuple-elemen, ...), custom_call_target="tpu_custom_call" | custom-call | tf_op jit(solution)/shard_map/start/pallas_call | solution.py:777
  6.5 7.5 %collective-permute-start.5 = (f32[624,128]{1,0:T(8,128)S(1)}, f32[624,128]{1,0:T(8,128)S(1)}, u32[]{:S(2)}, u32[]{:S(2)}) collective-permute-start(f32[624,128]{1,0:T(8,128)S(1)} %get-tuple-element.72), channel_id=1, source_target_pairs={{8,16},{16,8},{24,32},{32,24},{40,48},{48,40},{56,64},{64,56},{72,... | collective-permute-start | bytes 958472 | tf_op jit(solution)/shard_map/ppermute | solution.py:752
  14.0 0.0 collective-permute-done.ya
  14.0 0.0 collective-permute-done.1.yb
  14.0 0.9 %edge.1 = (f32[19,4,40,128]{3,2,1,0:T(8,128)S(1)}, f32[4,40,128]{2,1,0:T(8,128)S(1)}, f32[4,40,128]{2,1,0:T(8,128)S(1)}, f32[8,56,128]{2,1,0:T(8,128)S(1)}, f32[...) custom-call(f32[256,128]{1,0:T(8,128)S(1)} %collective-permute-done., ...), custom_call_target="tpu_custom_call", output_to_operand_aliasing={{0}: (2, {}), {1}: (3, {}), {2}: (4, {}), {3}: (5, {}), {4}... | custom-call | flops 10000000000 | bytes 10000000000 | tf_op jit(solution)/shard_map/edge/pallas_call | solution.py:781
  14.9 0.1 collective-permute-start.2
  15.0 0.5 %collective-permute-start.3 = (f32[10,40,128]{2,1,0:T(8,128)S(1)}, f32[10,40,128]{2,1,0:T(8,128)S(1)}, u32[]{:S(2)}, u32[]{:S(2)}) collective-permute-start(f32[10,40,128]{2,1,0:T(8,128)S(1)} %get-tuple-element.63), channel_id=1, source_target_pairs={{0,8},{8,0},{16,24},{24,16},{32,40},{40,32},{48,56},{56,48},{64,72... | collective-permute-start | bytes 614408 | tf_op jit(solution)/shard_map/ppermute | solution.py:752
  15.5 2.4 %collective-permute-start.4 = (f32[21,8,128]{2,1,0:T(8,128)S(1)}, f32[21,8,128]{2,1,0:T(8,128)S(1)}, u32[]{:S(2)}, u32[]{:S(2)}) collective-permute-start(f32[21,8,128]{2,1,0:T(8,128)S(1)} %get-tuple-element.66), channel_id=1, source_target_pairs={{8,16},{16,8},{24,32},{32,24},{40,48},{48,40},{56,64},{64,56},{72,... | collective-permute-start | bytes 258056 | tf_op jit(solution)/shard_map/ppermute | solution.py:752
  17.9 0.0 collective-permute-done.3.xd
  17.9 0.0 collective-permute-done.2.xa
  18.0 1.6 %near.1 = (f32[19,6,56,128]{3,2,1,0:T(8,128)S(1)}, f32[9,6,56,128]{3,2,1,0:T(8,128)S(1)}, f32[19,6,56,128]{3,2,1,0:T(8,128)S(1)}, f32[9,6,56,128]{3,2,1,0:T(8,12...) custom-call(f32[19,4,40,128]{3,2,1,0:T(8,128)S(1)} %get-tuple-elemen, ...), custom_call_target="tpu_custom_call", output_to_operand_aliasing={{0}: (4, {}), {1}: (5, {})} | custom-call | tf_op jit(solution)/shard_map/near/pallas_call | solution.py:796
  19.6 3.3 %collective-permute-done.5.xb = f32[624,128]{1,0:T(8,128)S(1)} collective-permute-done((f32[624,128]{1,0:T(8,128)S(1)}, f32[624,128]{1,0:T(8,128)S(1)}, u32[]{:S(2)}, u32[]{:S(2)}) %collective-permute-start.5) | collective-permute-done | bytes 319520 | tf_op jit(solution)/shard_map/ppermute | solution.py:752
  22.9 2.2 %far.1 = (f32[19,4,16,128]{3,2,1,0:T(8,128)S(1)}, f32[4,16,128]{2,1,0:T(8,128)S(1)}, f32[19,6,56,128]{3,2,1,0:T(8,128)S(1)}, f32[9,6,56,128]{3,2,1,0:T(8,128)S(1...) custom-call(f32[19,4,40,128]{3,2,1,0:T(8,128)S(1)} %get-tuple-elemen, ...), custom_call_target="tpu_custom_call", output_to_operand_aliasing={{2}: (4, {}), {3}: (5, {}), {4}: (6, {}), {5}: (7, {})} | custom-call | tf_op jit(solution)/shard_map/far/pallas_call | solution.py:803
  25.1 1.7 %collective-permute-done.4.xc = f32[21,8,128]{2,1,0:T(8,128)S(1)} collective-permute-done((f32[21,8,128]{2,1,0:T(8,128)S(1)}, f32[21,8,128]{2,1,0:T(8,128)S(1)}, u32[]{:S(2)}, u32[]{:S(2)}) %collective-permute-start.4) | collective-permute-done | bytes 86048 | tf_op jit(solution)/shard_map/ppermute | solution.py:752
  26.8 2.5 %end.1 = (f32[19,4,32,128]{3,2,1,0:T(8,128)}, f32[4,32,128]{2,1,0:T(8,128)}, f32[19,6,56,128]{3,2,1,0:T(8,128)S(1)}, f32[9,6,56,128]{3,2,1,0:T(8,128)S(1)}, f32[...) custom-call(f32[19,4,40,128]{3,2,1,0:T(8,128)S(1)} %get-tuple-elemen, ...), custom_call_target="tpu_custom_call", output_to_operand_aliasing={{2}: (8, {}), {3}: (9, {}), {4}: (10, {}), {5}: (11, {}), {... | custom-call | tf_op jit(solution)/shard_map/end/pallas_call | solution.py:807
Async XLA Ops:
  2.1 11.9 %collective-permute-start = (f32[256,128]{1,0:T(8,128)S(1)}, f32[256,128]{1,0:T(8,128)S(1)}, u32[]{:S(2)}, u32[]{:S(2)}) collective-permute-start(f32[256,128]{1,0:T(8,128)S(1)} %get-tuple-element.43), channel_id=1, source_target_pairs={{0,1},{1,0},{2,3},{3,2},{4,5},{5,4},{6,7},{7,6},{8,9},{9,8},{10,11... | collective-permute-start | bytes 393224 | tf_op jit(solution)/shard_map/ppermute | solution.py:752
  4.4 9.6 %collective-permute-start.1 = (f32[256,128]{1,0:T(8,128)S(1)}, f32[256,128]{1,0:T(8,128)S(1)}, u32[]{:S(2)}, u32[]{:S(2)}) collective-permute-start(f32[256,128]{1,0:T(8,128)S(1)} %get-tuple-element.44), channel_id=1, source_target_pairs={{1,2},{2,1},{3,4},{4,3},{5,6},{6,5},{7,0},{0,7},{9,10},{10,9},{11,... | collective-permute-start | bytes 393224 | tf_op jit(solution)/shard_map/ppermute | solution.py:752
  6.5 16.3 %collective-permute-start.5 = (f32[624,128]{1,0:T(8,128)S(1)}, f32[624,128]{1,0:T(8,128)S(1)}, u32[]{:S(2)}, u32[]{:S(2)}) collective-permute-start(f32[624,128]{1,0:T(8,128)S(1)} %get-tuple-element.72), channel_id=1, source_target_pairs={{8,16},{16,8},{24,32},{32,24},{40,48},{48,40},{56,64},{64,56},{72,... | collective-permute-start | bytes 958472 | tf_op jit(solution)/shard_map/ppermute | solution.py:752
  14.9 3.0 %collective-permute-start.2 = (f32[11,40,128]{2,1,0:T(8,128)S(1)}, f32[11,40,128]{2,1,0:T(8,128)S(1)}, u32[]{:S(2)}, u32[]{:S(2)}) collective-permute-start(f32[11,40,128]{2,1,0:T(8,128)S(1)} %get-tuple-element.62), channel_id=1, source_target_pairs={{0,8},{8,0},{16,24},{24,16},{32,40},{40,32},{48,56},{56,48},{64,72... | collective-permute-start | bytes 675848 | tf_op jit(solution)/shard_map/ppermute | solution.py:752
  15.0 2.9 %collective-permute-start.3 = (f32[10,40,128]{2,1,0:T(8,128)S(1)}, f32[10,40,128]{2,1,0:T(8,128)S(1)}, u32[]{:S(2)}, u32[]{:S(2)}) collective-permute-start(f32[10,40,128]{2,1,0:T(8,128)S(1)} %get-tuple-element.63), channel_id=1, source_target_pairs={{0,8},{8,0},{16,24},{24,16},{32,40},{40,32},{48,56},{56,48},{64,72... | collective-permute-start | bytes 614408 | tf_op jit(solution)/shard_map/ppermute | solution.py:752
  15.5 11.3 %collective-permute-start.4 = (f32[21,8,128]{2,1,0:T(8,128)S(1)}, f32[21,8,128]{2,1,0:T(8,128)S(1)}, u32[]{:S(2)}, u32[]{:S(2)}) collective-permute-start(f32[21,8,128]{2,1,0:T(8,128)S(1)} %get-tuple-element.66), channel_id=1, source_target_pairs={{8,16},{16,8},{24,32},{32,24},{40,48},{48,40},{56,64},{64,56},{72,... | collective-permute-start | bytes 258056 | tf_op jit(solution)/shard_map/ppermute | solution.py:752

commit v8 on v7

--- a/solution.py
+++ b/solution.py
@@ -349,31 +349,32 @@
     ]
     for c in copies:
         c.start()
-    for c in copies:
-        c.wait()
-
-    def pack(out, high):
+
+    def pack(out, high, x):
         three = pl.ds(NYL - 3 if high else 0, 3)
         four = pl.ds(NYL - 4 if high else 0, 4)
         for i in range(19):
-            for x in range(NXL):
-                out[pl.ds(i * 12 + x * 3, 3), :] = pops[i, x, three, :]
-        for x in range(NXL):
-            out[pl.ds(228 + x * 4, 4), :] = labels[x, four, :].astype(jnp.float32)
-            out[pl.ds(244 + x * 3, 3), :] = solid[x, three, :].astype(jnp.float32)
-
-    @pl.when(odd == 0)
-    def _():
-        pack(ya, True)
-        pack(yb, False)
-
-    @pl.when(odd == 1)
-    def _():
-        pack(ya, False)
-        pack(yb, True)
-
-
-def start_kernel(pops, labels, solid, s, rho, fl, ph, fp, red, xa, xd, xb):
+            out[pl.ds(i * 12 + x * 3, 3), :] = pops[i, x, three, :]
+        out[pl.ds(228 + x * 4, 4), :] = labels[x, four, :].astype(jnp.float32)
+        out[pl.ds(244 + x * 3, 3), :] = solid[x, three, :].astype(jnp.float32)
+
+    copies[0].wait()
+    copies[1].wait()
+    for x in range(NXL):
+        copies[2 + x].wait()
+
+        @pl.when(odd == 0)
+        def _():
+            pack(ya, True, x)
+            pack(yb, False, x)
+
+        @pl.when(odd == 1)
+        def _():
+            pack(ya, False, x)
+            pack(yb, True, x)
+
+
+def start_kernel(pops, labels, solid, s, rho, fl, ph, fp, red, xb):
     gy = lax.axis_index("gy")
     low_edge = gy == 0
     high_edge = gy == lax.axis_size("gy") - 1
@@ -401,10 +402,9 @@
     inner_step(range(NT), s, rho, fl, ph, fp, red)
     low_a = lax.axis_index("gx") % 2 == 1
     far_message(xb, low_a, (s, rho, fl, ph, fp, red))
-    main_message((xa, xd), jnp.logical_not(low_a), (s, rho, fl, ph, fp, red))
-
-
-def edge_kernel(ya, yb, s_in, rho_in, fl_in, ph_in, fp_in, red_in, xa_in, xd_in,
+
+
+def edge_kernel(ya, yb, s_in, rho_in, fl_in, ph_in, fp_in, red_in,
                 s, rho, fl, ph, fp, red, xa, xd, xc, raw):
     gy = lax.axis_index("gy")
     odd = gy % 2
@@ -453,6 +453,7 @@
     inner_step((0, NT - 1), s, rho, fl, ph, fp, red)
     low_a = lax.axis_index("gx") % 2 == 1
     corner_message(xc, 0, low_a, (s, rho, fl, ph, fp, red))
+    main_message((xa, xd), jnp.logical_not(low_a), (s, rho, fl, ph, fp, red))
     corner_message((xa, xd), NYL, jnp.logical_not(low_a), (s, rho, fl, ph, fp, red))
 
 
@@ -774,15 +775,15 @@
     )(*inputs)
     ya = swap(ya, "gy", 0)
     yb = swap(yb, "gy", 1)
-    *mid, xa, xd, xb = call(
-        start_kernel, [VM] * 3, state + split + [shaped(FAR_ROWS, 128)], [], "start",
+    *mid, xb = call(
+        start_kernel, [VM] * 3, state + [shaped(FAR_ROWS, 128)], [], "start",
     )(*held)
     xb = swap(xb, "gx", 1)
     *mid, xa, xd, xc = call(
-        edge_kernel, [VM] * 10, state + split + [shaped(21, 8, 128)],
-        [pltpu.VMEM((21, NXL, 8, 128), F32)], "edge", {2 + i: i for i in range(8)},
+        edge_kernel, [VM] * 8, state + split + [shaped(21, 8, 128)],
+        [pltpu.VMEM((21, NXL, 8, 128), F32)], "edge", {2 + i: i for i in range(6)},
         cost=10 ** 10,
-    )(ya, yb, *mid, xa, xd)
+    )(ya, yb, *mid)
     xc = swap(xc, "gx", 1)
     xa = swap(xa, "gx", 0)
     xd = swap(xd, "gx", 0)

time: 29.4 us -> 29.4 us (level)
  no operation moved by 1% of the time
where the time goes in v8:
time: 29.4 us; the launch traced here: 29.3 us
  starting transfers between devices  13.5 us (46%)
  Pallas kernels  10.1 us (34%)
  waiting for transfers between devices  4.95 us (17%)
  between operations  0.68 us (2%)
    ppermute x6, starting transfers between devices, swap(): return lax.ppermute(value, axis, pairs(lax.axis_size(axis), first))  13.5 us
    ppermute x6, waiting for transfers between devices, swap(): return lax.ppermute(value, axis, pairs(lax.axis_size(axis), first))  4.95 us
    pallas_call x1, Pallas kernels, on_device(): call(end_kernel, [VM] * 15, [shaped(19, NXL, NYL, 128), shaped(NXL, NYL,...  2.49 us
    pallas_call x1, Pallas kernels, on_device(): call(far_kernel, [VM] * 12, [shaped(19, NXL, 16, 128), shaped(NXL, 16, 12...  2.24 us
    pallas_call x1, Pallas kernels, on_device(): call(near_kernel, [VM] * 8, [state[4], state[5], state[4], state[5], stat...  1.59 us
    pallas_call x1, Pallas kernels, on_device(): call(pack_kernel, [HB] * 3, [shaped(YROWS, 128)] * 2 + whole, [pltpu.Sema...  1.4 us
    pallas_call x1, Pallas kernels, on_device(): call(start_kernel, [VM] * 3, state + [shaped(FAR_ROWS, 128)], [], 'start')  1.39 us
    pallas_call x1, Pallas kernels, on_device(): call(edge_kernel, [VM] * 8, state + split + [shaped(21, 8, 128)], [pltpu....  0.96 us
  transfers between devices with their start and end apart: 6, of which 2 were waited for; matrix products, arithmetic and copies ran while one was open for 0% of the time, Pallas kernels for 21%

profile of v8, /device:TPU:8, one launch (start us, length us, event | category | flops | bytes accessed | tf_op | source)
XLA Modules:
  0.0 29.3 jit_solution(10482681746697696552)
XLA Ops:
  0.6 1.4 %pack.1 = (f32[256,128]{1,0:T(8,128)S(1)}, f32[256,128]{1,0:T(8,128)S(1)}, f32[19,4,32,128]{3,2,1,0:T(8,128)S(1)}, s32[4,32,128]{2,1,0:T(8,128)S(1)}, s32[4,32,128]{2,1,0:T(8,128)S(1)}) custom-call(f32[19,4,32,128]{3,2,1,0:T(8,128)} %pops_hbm.1, s32[4,32,128]{2,1,0:T(8,128)} %labels_hbm.1, s32[4,32,128]{2,1,0:T(8,128)} %solid_hbm.1), custom_call_target="tpu_custom_call" | custom-call | tf_op jit(solution)/shard_map/pack/pallas_call | solution.py:772
  2.0 2.3 %collective-permute-start = (f32[256,128]{1,0:T(8,128)S(1)}, f32[256,128]{1,0:T(8,128)S(1)}, u32[]{:S(2)}, u32[]{:S(2)}) collective-permute-start(f32[256,128]{1,0:T(8,128)S(1)} %get-tuple-element.41), channel_id=1, source_target_pairs={{0,1},{1,0},{2,3},{3,2},{4,5},{5,4},{6,7},{7,6},{8,9},{9,8},{10,11... | collective-permute-start | bytes 393224 | tf_op jit(solution)/shard_map/ppermute | solution.py:753
  4.3 0.7 %collective-permute-start.1 = (f32[256,128]{1,0:T(8,128)S(1)}, f32[256,128]{1,0:T(8,128)S(1)}, u32[]{:S(2)}, u32[]{:S(2)}) collective-permute-start(f32[256,128]{1,0:T(8,128)S(1)} %get-tuple-element.42), channel_id=1, source_target_pairs={{1,2},{2,1},{3,4},{4,3},{5,6},{6,5},{7,0},{0,7},{9,10},{10,9},{11,... | collective-permute-start | bytes 393224 | tf_op jit(solution)/shard_map/ppermute | solution.py:753
  5.0 1.4 %start.1 = (f32[19,4,40,128]{3,2,1,0:T(8,128)S(1)}, f32[4,40,128]{2,1,0:T(8,128)S(1)}, f32[4,40,128]{2,1,0:T(8,128)S(1)}, f32[8,56,128]{2,1,0:T(8,128)S(1)}, f32...) custom-call(f32[19,4,32,128]{3,2,1,0:T(8,128)S(1)} %get-tuple-element.43.pops, ...), custom_call_target="tpu_custom_call" | custom-call | tf_op jit(solution)/shard_map/start/pallas_call | solution.py:778
  6.4 7.5 %collective-permute-start.5 = (f32[624,128]{1,0:T(8,128)S(1)}, f32[624,128]{1,0:T(8,128)S(1)}, u32[]{:S(2)}, u32[]{:S(2)}) collective-permute-start(f32[624,128]{1,0:T(8,128)S(1)} %get-tuple-element.68), channel_id=1, source_target_pairs={{8,16},{16,8},{24,32},{32,24},{40,48},{48,40},{56,64},{64,56},{72,... | collective-permute-start | bytes 958472 | tf_op jit(solution)/shard_map/ppermute | solution.py:753
  13.9 0.0 collective-permute-done.ya
  13.9 0.0 collective-permute-done.1.yb
  13.9 1.0 %edge.1 = (f32[19,4,40,128]{3,2,1,0:T(8,128)S(1)}, f32[4,40,128]{2,1,0:T(8,128)S(1)}, f32[4,40,128]{2,1,0:T(8,128)S(1)}, f32[8,56,128]{2,1,0:T(8,128)S(1)}, f32[...) custom-call(f32[256,128]{1,0:T(8,128)S(1)} %collective-permute-done., ...), custom_call_target="tpu_custom_call", output_to_operand_aliasing={{0}: (2, {}), {1}: (3, {}), {2}: (4, {}), {3}: (5, {}), {4}... | custom-call | flops 10000000000 | bytes 10000000000 | tf_op jit(solution)/shard_map/edge/pallas_call | solution.py:782
  14.8 0.1 collective-permute-start.2
  14.9 0.5 %collective-permute-start.3 = (f32[10,40,128]{2,1,0:T(8,128)S(1)}, f32[10,40,128]{2,1,0:T(8,128)S(1)}, u32[]{:S(2)}, u32[]{:S(2)}) collective-permute-start(f32[10,40,128]{2,1,0:T(8,128)S(1)} %get-tuple-element.59), channel_id=1, source_target_pairs={{0,8},{8,0},{16,24},{24,16},{32,40},{40,32},{48,56},{56,48},{64,72... | collective-permute-start | bytes 614408 | tf_op jit(solution)/shard_map/ppermute | solution.py:753
  15.4 2.5 %collective-permute-start.4 = (f32[21,8,128]{2,1,0:T(8,128)S(1)}, f32[21,8,128]{2,1,0:T(8,128)S(1)}, u32[]{:S(2)}, u32[]{:S(2)}) collective-permute-start(f32[21,8,128]{2,1,0:T(8,128)S(1)} %get-tuple-element.62), channel_id=1, source_target_pairs={{8,16},{16,8},{24,32},{32,24},{40,48},{48,40},{56,64},{64,56},{72,... | collective-permute-start | bytes 258056 | tf_op jit(solution)/shard_map/ppermute | solution.py:753
  18.0 0.0 collective-permute-done.3.xd
  18.0 0.0 collective-permute-done.2.xa
  18.0 1.6 %near.1 = (f32[19,6,56,128]{3,2,1,0:T(8,128)S(1)}, f32[9,6,56,128]{3,2,1,0:T(8,128)S(1)}, f32[19,6,56,128]{3,2,1,0:T(8,128)S(1)}, f32[9,6,56,128]{3,2,1,0:T(8,12...) custom-call(f32[19,4,40,128]{3,2,1,0:T(8,128)S(1)} %get-tuple-elemen, ...), custom_call_target="tpu_custom_call", output_to_operand_aliasing={{0}: (4, {}), {1}: (5, {})} | custom-call | tf_op jit(solution)/shard_map/near/pallas_call | solution.py:797
  19.6 3.2 %collective-permute-done.5.xb = f32[624,128]{1,0:T(8,128)S(1)} collective-permute-done((f32[624,128]{1,0:T(8,128)S(1)}, f32[624,128]{1,0:T(8,128)S(1)}, u32[]{:S(2)}, u32[]{:S(2)}) %collective-permute-start.5) | collective-permute-done | bytes 319520 | tf_op jit(solution)/shard_map/ppermute | solution.py:753
  22.7 2.2 %far.1 = (f32[19,4,16,128]{3,2,1,0:T(8,128)S(1)}, f32[4,16,128]{2,1,0:T(8,128)S(1)}, f32[19,6,56,128]{3,2,1,0:T(8,128)S(1)}, f32[9,6,56,128]{3,2,1,0:T(8,128)S(1...) custom-call(f32[19,4,40,128]{3,2,1,0:T(8,128)S(1)} %get-tuple-elemen, ...), custom_call_target="tpu_custom_call", output_to_operand_aliasing={{2}: (4, {}), {3}: (5, {}), {4}: (6, {}), {5}: (7, {})} | custom-call | tf_op jit(solution)/shard_map/far/pallas_call | solution.py:804
  25.0 1.8 %collective-permute-done.4.xc = f32[21,8,128]{2,1,0:T(8,128)S(1)} collective-permute-done((f32[21,8,128]{2,1,0:T(8,128)S(1)}, f32[21,8,128]{2,1,0:T(8,128)S(1)}, u32[]{:S(2)}, u32[]{:S(2)}) %collective-permute-start.4) | collective-permute-done | bytes 86048 | tf_op jit(solution)/shard_map/ppermute | solution.py:753
  26.8 2.5 %end.1 = (f32[19,4,32,128]{3,2,1,0:T(8,128)}, f32[4,32,128]{2,1,0:T(8,128)}, f32[19,6,56,128]{3,2,1,0:T(8,128)S(1)}, f32[9,6,56,128]{3,2,1,0:T(8,128)S(1)}, f32[...) custom-call(f32[19,4,40,128]{3,2,1,0:T(8,128)S(1)} %get-tuple-elemen, ...), custom_call_target="tpu_custom_call", output_to_operand_aliasing={{2}: (8, {}), {3}: (9, {}), {4}: (10, {}), {5}: (11, {}), {... | custom-call | tf_op jit(solution)/shard_map/end/pallas_call | solution.py:808
Async XLA Ops:
  2.0 11.8 %collective-permute-start = (f32[256,128]{1,0:T(8,128)S(1)}, f32[256,128]{1,0:T(8,128)S(1)}, u32[]{:S(2)}, u32[]{:S(2)}) collective-permute-start(f32[256,128]{1,0:T(8,128)S(1)} %get-tuple-element.41), channel_id=1, source_target_pairs={{0,1},{1,0},{2,3},{3,2},{4,5},{5,4},{6,7},{7,6},{8,9},{9,8},{10,11... | collective-permute-start | bytes 393224 | tf_op jit(solution)/shard_map/ppermute | solution.py:753
  4.3 9.5 %collective-permute-start.1 = (f32[256,128]{1,0:T(8,128)S(1)}, f32[256,128]{1,0:T(8,128)S(1)}, u32[]{:S(2)}, u32[]{:S(2)}) collective-permute-start(f32[256,128]{1,0:T(8,128)S(1)} %get-tuple-element.42), channel_id=1, source_target_pairs={{1,2},{2,1},{3,4},{4,3},{5,6},{6,5},{7,0},{0,7},{9,10},{10,9},{11,... | collective-permute-start | bytes 393224 | tf_op jit(solution)/shard_map/ppermute | solution.py:753
  6.4 16.3 %collective-permute-start.5 = (f32[624,128]{1,0:T(8,128)S(1)}, f32[624,128]{1,0:T(8,128)S(1)}, u32[]{:S(2)}, u32[]{:S(2)}) collective-permute-start(f32[624,128]{1,0:T(8,128)S(1)} %get-tuple-element.68), channel_id=1, source_target_pairs={{8,16},{16,8},{24,32},{32,24},{40,48},{48,40},{56,64},{64,56},{72,... | collective-permute-start | bytes 958472 | tf_op jit(solution)/shard_map/ppermute | solution.py:753
  14.8 3.1 %collective-permute-start.2 = (f32[11,40,128]{2,1,0:T(8,128)S(1)}, f32[11,40,128]{2,1,0:T(8,128)S(1)}, u32[]{:S(2)}, u32[]{:S(2)}) collective-permute-start(f32[11,40,128]{2,1,0:T(8,128)S(1)} %get-tuple-element.58), channel_id=1, source_target_pairs={{0,8},{8,0},{16,24},{24,16},{32,40},{40,32},{48,56},{56,48},{64,72... | collective-permute-start | bytes 675848 | tf_op jit(solution)/shard_map/ppermute | solution.py:753
  14.9 3.0 %collective-permute-start.3 = (f32[10,40,128]{2,1,0:T(8,128)S(1)}, f32[10,40,128]{2,1,0:T(8,128)S(1)}, u32[]{:S(2)}, u32[]{:S(2)}) collective-permute-start(f32[10,40,128]{2,1,0:T(8,128)S(1)} %get-tuple-element.59), channel_id=1, source_target_pairs={{0,8},{8,0},{16,24},{24,16},{32,40},{40,32},{48,56},{56,48},{64,72... | collective-permute-start | bytes 614408 | tf_op jit(solution)/shard_map/ppermute | solution.py:753
  15.4 11.3 %collective-permute-start.4 = (f32[21,8,128]{2,1,0:T(8,128)S(1)}, f32[21,8,128]{2,1,0:T(8,128)S(1)}, u32[]{:S(2)}, u32[]{:S(2)}) collective-permute-start(f32[21,8,128]{2,1,0:T(8,128)S(1)} %get-tuple-element.62), channel_id=1, source_target_pairs={{8,16},{16,8},{24,32},{32,24},{40,48},{48,40},{56,64},{64,56},{72,... | collective-permute-start | bytes 258056 | tf_op jit(solution)/shard_map/ppermute | solution.py:753

commit v9 on v8

--- a/solution.py
+++ b/solution.py
@@ -279,6 +279,49 @@
                 plane_of(msg, j)[pl.ds(8 * n, 8), :] = v
 
 
+def corner_spans():
+    out, at = [], 0
+    for j in range(21):
+        if j in (15, 16):
+            rows = ((0, 4), (EXT - 4, 4))
+        elif j in PLAIN:
+            rows = ((1, 3), (EXT - 4, 3))
+        elif j in (10, 18, 19, 20):
+            rows = ((2, 4), (EXT - 6, 4))
+        else:
+            rows = ((3, 3), (EXT - 6, 3))
+        for end, (row, n) in enumerate(rows):
+            out.append((j, end, at, row, n))
+            at += n
+    return out, at
+
+
+CORNER_ROWS = corner_spans()[1]
+
+
+def far_corner(msg, high, state):
+    values = {}
+    for end, (first, second) in enumerate(((0, 2), (EXT - 8, EXT - 6))):
+        part = message_tile(high, ROW0 + first, *state)[0]()
+        values.update({(j, end): (v, first) for j, v in zip(PLAIN, part[0] + part[1])})
+        part = message_tile(high, ROW0 + second, *state)[1]()
+        values.update({(j, end): (v, second) for j, v in zip(MOVED, part[0] + part[1])})
+    for j, end, at, row, n in corner_spans()[0]:
+        v, first = values[j, end]
+        msg[pl.ds(at, n), :] = v[row - first:row - first + n]
+
+
+def put_corner(src, side, hx, ph):
+    near = jnp.where(side == 1, NXL + 2, 1)
+    far = jnp.where(side == 1, NXL + 3, 0)
+    for j, _, at, row, n in corner_spans()[0]:
+        v = src[pl.ds(at, n), :]
+        if j in (15, 16):
+            ph[near if j == 15 else far, pl.ds(ROW0 + row, n), :] = v
+        else:
+            hx[j, pl.ds(row, n), :] = v
+
+
 def far_spans():
     out = []
     for i, j in enumerate(PLAIN):
@@ -452,7 +495,7 @@
     lax.fori_loop(0, NXL, plane, 0)
     inner_step((0, NT - 1), s, rho, fl, ph, fp, red)
     low_a = lax.axis_index("gx") % 2 == 1
-    corner_message(xc, 0, low_a, (s, rho, fl, ph, fp, red))
+    far_corner(xc, low_a, (s, rho, fl, ph, fp, red))
     main_message((xa, xd), jnp.logical_not(low_a), (s, rho, fl, ph, fp, red))
     corner_message((xa, xd), NYL, jnp.logical_not(low_a), (s, rho, fl, ph, fp, red))
 
@@ -702,7 +745,7 @@
     for x in range(NXL):
         for copy in middle_copies(x):
             copy.start()
-    put_message(xc, 0, lax.axis_index("gx") % 2, True, hx, ph)
+    put_corner(xc, lax.axis_index("gx") % 2, hx, ph)
     far_half(
         (0, NT - 1), s, rho, fl, ph, fp, red, fp2, red2, ph2, s2_next, rho2_next, hx, s2,
         rho2, own2, orho2,
@@ -780,7 +823,7 @@
     )(*held)
     xb = swap(xb, "gx", 1)
     *mid, xa, xd, xc = call(
-        edge_kernel, [VM] * 8, state + split + [shaped(21, 8, 128)],
+        edge_kernel, [VM] * 8, state + split + [shaped(CORNER_ROWS, 128)],
         [pltpu.VMEM((21, NXL, 8, 128), F32)], "edge", {2 + i: i for i in range(6)},
         cost=10 ** 10,
     )(ya, yb, *mid)

time: 29.4 us -> 29.1 us (0.990)
  no operation moved by 1% of the time
where the time goes in v9:
time: 29.1 us; the launch traced here: 29 us
  starting transfers between devices  13.5 us (46%)
  Pallas kernels  10.1 us (35%)
  waiting for transfers between devices  4.69 us (16%)
  between operations  0.68 us (2%)
    ppermute x6, starting transfers between devices, swap(): return lax.ppermute(value, axis, pairs(lax.axis_size(axis), first))  13.5 us
    ppermute x6, waiting for transfers between devices, swap(): return lax.ppermute(value, axis, pairs(lax.axis_size(axis), first))  4.69 us
    pallas_call x1, Pallas kernels, on_device(): call(end_kernel, [VM] * 15, [shaped(19, NXL, NYL, 128), shaped(NXL, NYL,...  2.5 us
    pallas_call x1, Pallas kernels, on_device(): call(far_kernel, [VM] * 12, [shaped(19, NXL, 16, 128), shaped(NXL, 16, 12...  2.24 us
    pallas_call x1, Pallas kernels, on_device(): call(near_kernel, [VM] * 8, [state[4], state[5], state[4], state[5], stat...  1.59 us
    pallas_call x1, Pallas kernels, on_device(): call(pack_kernel, [HB] * 3, [shaped(YROWS, 128)] * 2 + whole, [pltpu.Sema...  1.4 us
    pallas_call x1, Pallas kernels, on_device(): call(start_kernel, [VM] * 3, state + [shaped(FAR_ROWS, 128)], [], 'start')  1.39 us
    pallas_call x1, Pallas kernels, on_device(): call(edge_kernel, [VM] * 8, state + split + [shaped(CORNER_ROWS, 128)], [...  0.96 us
  transfers between devices with their start and end apart: 6, of which 2 were waited for; matrix products, arithmetic and copies ran while one was open for 0% of the time, Pallas kernels for 21%

profile of v9, /device:TPU:8, one launch (start us, length us, event | category | flops | bytes accessed | tf_op | source)
XLA Modules:
  0.0 29.0 jit_solution(15066937899485759586)
XLA Ops:
  0.6 1.4 %pack.1 = (f32[256,128]{1,0:T(8,128)S(1)}, f32[256,128]{1,0:T(8,128)S(1)}, f32[19,4,32,128]{3,2,1,0:T(8,128)S(1)}, s32[4,32,128]{2,1,0:T(8,128)S(1)}, s32[4,32,128]{2,1,0:T(8,128)S(1)}) custom-call(f32[19,4,32,128]{3,2,1,0:T(8,128)} %pops_hbm.1, s32[4,32,128]{2,1,0:T(8,128)} %labels_hbm.1, s32[4,32,128]{2,1,0:T(8,128)} %solid_hbm.1), custom_call_target="tpu_custom_call" | custom-call | tf_op jit(solution)/shard_map/pack/pallas_call | solution.py:815
  2.0 2.3 %collective-permute-start = (f32[256,128]{1,0:T(8,128)S(1)}, f32[256,128]{1,0:T(8,128)S(1)}, u32[]{:S(2)}, u32[]{:S(2)}) collective-permute-start(f32[256,128]{1,0:T(8,128)S(1)} %get-tuple-element.41), channel_id=1, source_target_pairs={{0,1},{1,0},{2,3},{3,2},{4,5},{5,4},{6,7},{7,6},{8,9},{9,8},{10,11... | collective-permute-start | bytes 393224 | tf_op jit(solution)/shard_map/ppermute | solution.py:796
  4.3 0.7 %collective-permute-start.1 = (f32[256,128]{1,0:T(8,128)S(1)}, f32[256,128]{1,0:T(8,128)S(1)}, u32[]{:S(2)}, u32[]{:S(2)}) collective-permute-start(f32[256,128]{1,0:T(8,128)S(1)} %get-tuple-element.42), channel_id=1, source_target_pairs={{1,2},{2,1},{3,4},{4,3},{5,6},{6,5},{7,0},{0,7},{9,10},{10,9},{11,... | collective-permute-start | bytes 393224 | tf_op jit(solution)/shard_map/ppermute | solution.py:796
  5.0 1.4 %start.1 = (f32[19,4,40,128]{3,2,1,0:T(8,128)S(1)}, f32[4,40,128]{2,1,0:T(8,128)S(1)}, f32[4,40,128]{2,1,0:T(8,128)S(1)}, f32[8,56,128]{2,1,0:T(8,128)S(1)}, f32...) custom-call(f32[19,4,32,128]{3,2,1,0:T(8,128)S(1)} %get-tuple-element.43.pops, ...), custom_call_target="tpu_custom_call" | custom-call | tf_op jit(solution)/shard_map/start/pallas_call | solution.py:821
  6.4 7.5 %collective-permute-start.5 = (f32[624,128]{1,0:T(8,128)S(1)}, f32[624,128]{1,0:T(8,128)S(1)}, u32[]{:S(2)}, u32[]{:S(2)}) collective-permute-start(f32[624,128]{1,0:T(8,128)S(1)} %get-tuple-element.68), channel_id=1, source_target_pairs={{8,16},{16,8},{24,32},{32,24},{40,48},{48,40},{56,64},{64,56},{72,... | collective-permute-start | bytes 958472 | tf_op jit(solution)/shard_map/ppermute | solution.py:796
  13.9 0.0 collective-permute-done.ya
  13.9 0.0 collective-permute-done.1.yb
  13.9 1.0 %edge.1 = (f32[19,4,40,128]{3,2,1,0:T(8,128)S(1)}, f32[4,40,128]{2,1,0:T(8,128)S(1)}, f32[4,40,128]{2,1,0:T(8,128)S(1)}, f32[8,56,128]{2,1,0:T(8,128)S(1)}, f32[...) custom-call(f32[256,128]{1,0:T(8,128)S(1)} %collective-permute-done., ...), custom_call_target="tpu_custom_call", output_to_operand_aliasing={{0}: (2, {}), {1}: (3, {}), {2}: (4, {}), {3}: (5, {}), {4}... | custom-call | flops 10000000000 | bytes 10000000000 | tf_op jit(solution)/shard_map/edge/pallas_call | solution.py:825
  14.8 0.1 collective-permute-start.2
  14.9 0.5 %collective-permute-start.3 = (f32[10,40,128]{2,1,0:T(8,128)S(1)}, f32[10,40,128]{2,1,0:T(8,128)S(1)}, u32[]{:S(2)}, u32[]{:S(2)}) collective-permute-start(f32[10,40,128]{2,1,0:T(8,128)S(1)} %get-tuple-element.59), channel_id=1, source_target_pairs={{0,8},{8,0},{16,24},{24,16},{32,40},{40,32},{48,56},{56,48},{64,72... | collective-permute-start | bytes 614408 | tf_op jit(solution)/shard_map/ppermute | solution.py:796
  15.4 2.5 %collective-permute-start.4 = (f32[138,128]{1,0:T(8,128)S(1)}, f32[138,128]{1,0:T(8,128)S(1)}, u32[]{:S(2)}, u32[]{:S(2)}) collective-permute-start(f32[138,128]{1,0:T(8,128)S(1)} %get-tuple-element.62), channel_id=1, source_target_pairs={{8,16},{16,8},{24,32},{32,24},{40,48},{48,40},{56,64},{64,56},{72,... | collective-permute-start | bytes 211976 | tf_op jit(solution)/shard_map/ppermute | solution.py:796
  18.0 0.0 collective-permute-done.3.xd
  18.0 0.0 collective-permute-done.2.xa
  18.0 1.6 %near.1 = (f32[19,6,56,128]{3,2,1,0:T(8,128)S(1)}, f32[9,6,56,128]{3,2,1,0:T(8,128)S(1)}, f32[19,6,56,128]{3,2,1,0:T(8,128)S(1)}, f32[9,6,56,128]{3,2,1,0:T(8,12...) custom-call(f32[19,4,40,128]{3,2,1,0:T(8,128)S(1)} %get-tuple-elemen, ...), custom_call_target="tpu_custom_call", output_to_operand_aliasing={{0}: (4, {}), {1}: (5, {})} | custom-call | tf_op jit(solution)/shard_map/near/pallas_call | solution.py:840
  19.6 3.0 %collective-permute-done.5.xb = f32[624,128]{1,0:T(8,128)S(1)} collective-permute-done((f32[624,128]{1,0:T(8,128)S(1)}, f32[624,128]{1,0:T(8,128)S(1)}, u32[]{:S(2)}, u32[]{:S(2)}) %collective-permute-start.5) | collective-permute-done | bytes 319520 | tf_op jit(solution)/shard_map/ppermute | solution.py:796
  22.6 2.2 %far.1 = (f32[19,4,16,128]{3,2,1,0:T(8,128)S(1)}, f32[4,16,128]{2,1,0:T(8,128)S(1)}, f32[19,6,56,128]{3,2,1,0:T(8,128)S(1)}, f32[9,6,56,128]{3,2,1,0:T(8,128)S(1...) custom-call(f32[19,4,40,128]{3,2,1,0:T(8,128)S(1)} %get-tuple-elemen, ...), custom_call_target="tpu_custom_call", output_to_operand_aliasing={{2}: (4, {}), {3}: (5, {}), {4}: (6, {}), {5}: (7, {})} | custom-call | tf_op jit(solution)/shard_map/far/pallas_call | solution.py:847
  24.8 1.7 %collective-permute-done.4.xc = f32[138,128]{1,0:T(8,128)S(1)} collective-permute-done((f32[138,128]{1,0:T(8,128)S(1)}, f32[138,128]{1,0:T(8,128)S(1)}, u32[]{:S(2)}, u32[]{:S(2)}) %collective-permute-start.4) | collective-permute-done | bytes 70688 | tf_op jit(solution)/shard_map/ppermute | solution.py:796
  26.5 2.5 %end.1 = (f32[19,4,32,128]{3,2,1,0:T(8,128)}, f32[4,32,128]{2,1,0:T(8,128)}, f32[19,6,56,128]{3,2,1,0:T(8,128)S(1)}, f32[9,6,56,128]{3,2,1,0:T(8,128)S(1)}, f32[...) custom-call(f32[19,4,40,128]{3,2,1,0:T(8,128)S(1)} %get-tuple-elemen, ...), custom_call_target="tpu_custom_call", output_to_operand_aliasing={{2}: (8, {}), {3}: (9, {}), {4}: (10, {}), {5}: (11, {}), {... | custom-call | tf_op jit(solution)/shard_map/end/pallas_call | solution.py:851
Async XLA Ops:
  2.0 11.8 %collective-permute-start = (f32[256,128]{1,0:T(8,128)S(1)}, f32[256,128]{1,0:T(8,128)S(1)}, u32[]{:S(2)}, u32[]{:S(2)}) collective-permute-start(f32[256,128]{1,0:T(8,128)S(1)} %get-tuple-element.41), channel_id=1, source_target_pairs={{0,1},{1,0},{2,3},{3,2},{4,5},{5,4},{6,7},{7,6},{8,9},{9,8},{10,11... | collective-permute-start | bytes 393224 | tf_op jit(solution)/shard_map/ppermute | solution.py:796
  4.3 9.5 %collective-permute-start.1 = (f32[256,128]{1,0:T(8,128)S(1)}, f32[256,128]{1,0:T(8,128)S(1)}, u32[]{:S(2)}, u32[]{:S(2)}) collective-permute-start(f32[256,128]{1,0:T(8,128)S(1)} %get-tuple-element.42), channel_id=1, source_target_pairs={{1,2},{2,1},{3,4},{4,3},{5,6},{6,5},{7,0},{0,7},{9,10},{10,9},{11,... | collective-permute-start | bytes 393224 | tf_op jit(solution)/shard_map/ppermute | solution.py:796
  6.4 16.2 %collective-permute-start.5 = (f32[624,128]{1,0:T(8,128)S(1)}, f32[624,128]{1,0:T(8,128)S(1)}, u32[]{:S(2)}, u32[]{:S(2)}) collective-permute-start(f32[624,128]{1,0:T(8,128)S(1)} %get-tuple-element.68), channel_id=1, source_target_pairs={{8,16},{16,8},{24,32},{32,24},{40,48},{48,40},{56,64},{64,56},{72,... | collective-permute-start | bytes 958472 | tf_op jit(solution)/shard_map/ppermute | solution.py:796
  14.8 3.1 %collective-permute-start.2 = (f32[11,40,128]{2,1,0:T(8,128)S(1)}, f32[11,40,128]{2,1,0:T(8,128)S(1)}, u32[]{:S(2)}, u32[]{:S(2)}) collective-permute-start(f32[11,40,128]{2,1,0:T(8,128)S(1)} %get-tuple-element.58), channel_id=1, source_target_pairs={{0,8},{8,0},{16,24},{24,16},{32,40},{40,32},{48,56},{56,48},{64,72... | collective-permute-start | bytes 675848 | tf_op jit(solution)/shard_map/ppermute | solution.py:796
  14.9 3.0 %collective-permute-start.3 = (f32[10,40,128]{2,1,0:T(8,128)S(1)}, f32[10,40,128]{2,1,0:T(8,128)S(1)}, u32[]{:S(2)}, u32[]{:S(2)}) collective-permute-start(f32[10,40,128]{2,1,0:T(8,128)S(1)} %get-tuple-element.59), channel_id=1, source_target_pairs={{0,8},{8,0},{16,24},{24,16},{32,40},{40,32},{48,56},{56,48},{64,72... | collective-permute-start | bytes 614408 | tf_op jit(solution)/shard_map/ppermute | solution.py:796
  15.4 11.1 %collective-permute-start.4 = (f32[138,128]{1,0:T(8,128)S(1)}, f32[138,128]{1,0:T(8,128)S(1)}, u32[]{:S(2)}, u32[]{:S(2)}) collective-permute-start(f32[138,128]{1,0:T(8,128)S(1)} %get-tuple-element.62), channel_id=1, source_target_pairs={{8,16},{16,8},{24,32},{32,24},{40,48},{48,40},{56,64},{64,56},{72,... | collective-permute-start | bytes 211976 | tf_op jit(solution)/shard_map/ppermute | solution.py:796

commit v10 on v9

--- a/solution.py
+++ b/solution.py
@@ -447,7 +447,7 @@
     far_message(xb, low_a, (s, rho, fl, ph, fp, red))
 
 
-def edge_kernel(ya, yb, s_in, rho_in, fl_in, ph_in, fp_in, red_in,
+def edge_kernel(yb, ya, s_in, rho_in, fl_in, ph_in, fp_in, red_in,
                 s, rho, fl, ph, fp, red, xa, xd, xc, raw):
     gy = lax.axis_index("gy")
     odd = gy % 2
@@ -826,7 +826,7 @@
         edge_kernel, [VM] * 8, state + split + [shaped(CORNER_ROWS, 128)],
         [pltpu.VMEM((21, NXL, 8, 128), F32)], "edge", {2 + i: i for i in range(6)},
         cost=10 ** 10,
-    )(ya, yb, *mid)
+    )(yb, ya, *mid)
     xc = swap(xc, "gx", 1)
     xa = swap(xa, "gx", 0)
     xd = swap(xd, "gx", 0)

time: 29.1 us -> 30.1 us (1.034)
  starting transfers between devices: 13.5 us -> 14.6 us
    ppermute x6, starting transfers between devices: 13.5 us -> 14.6 us  [swap(): return lax.ppermute(value, axis, pairs(lax.axis_size(axis), first))]
  transfers between devices with their start and end apart: 6 -> 6, of which waited for: 2 -> 1; matrix products, arithmetic and copies ran while one was open for 0% -> 0% of each run, Pallas kernels for 21% -> 21%
where the time goes in v10:
time: 30.1 us; the launch traced here: 30 us
  starting transfers between devices  14.6 us (49%)
  Pallas kernels  10.1 us (34%)
  waiting for transfers between devices  4.67 us (16%)
  between operations  0.69 us (2%)
    ppermute x6, starting transfers between devices, swap(): return lax.ppermute(value, axis, pairs(lax.axis_size(axis), first))  14.6 us
    ppermute x6, waiting for transfers between devices, swap(): return lax.ppermute(value, axis, pairs(lax.axis_size(axis), first))  4.67 us
    pallas_call x1, Pallas kernels, on_device(): call(end_kernel, [VM] * 15, [shaped(19, NXL, NYL, 128), shaped(NXL, NYL,...  2.5 us
    pallas_call x1, Pallas kernels, on_device(): call(far_kernel, [VM] * 12, [shaped(19, NXL, 16, 128), shaped(NXL, 16, 12...  2.24 us
    pallas_call x1, Pallas kernels, on_device(): call(near_kernel, [VM] * 8, [state[4], state[5], state[4], state[5], stat...  1.59 us
    pallas_call x1, Pallas kernels, on_device(): call(pack_kernel, [HB] * 3, [shaped(YROWS, 128)] * 2 + whole, [pltpu.Sema...  1.4 us
    pallas_call x1, Pallas kernels, on_device(): call(start_kernel, [VM] * 3, state + [shaped(FAR_ROWS, 128)], [], 'start')  1.39 us
    pallas_call x1, Pallas kernels, on_device(): call(edge_kernel, [VM] * 8, state + split + [shaped(CORNER_ROWS, 128)], [...  0.96 us
  transfers between devices with their start and end apart: 6, of which 1 were waited for; matrix products, arithmetic and copies ran while one was open for 0% of the time, Pallas kernels for 21%

profile of v10, /device:TPU:8, one launch (start us, length us, event | category | flops | bytes accessed | tf_op | source)
XLA Modules:
  0.0 30.0 jit_solution(13269264032889644208)
XLA Ops:
  0.6 1.4 %pack.1 = (f32[256,128]{1,0:T(8,128)S(1)}, f32[256,128]{1,0:T(8,128)S(1)}, f32[19,4,32,128]{3,2,1,0:T(8,128)S(1)}, s32[4,32,128]{2,1,0:T(8,128)S(1)}, s32[4,32,128]{2,1,0:T(8,128)S(1)}) custom-call(f32[19,4,32,128]{3,2,1,0:T(8,128)} %pops_hbm.1, s32[4,32,128]{2,1,0:T(8,128)} %labels_hbm.1, s32[4,32,128]{2,1,0:T(8,128)} %solid_hbm.1), custom_call_target="tpu_custom_call" | custom-call | tf_op jit(solution)/shard_map/pack/pallas_call | solution.py:815
  2.0 1.7 %collective-permute-start = (f32[256,128]{1,0:T(8,128)S(1)}, f32[256,128]{1,0:T(8,128)S(1)}, u32[]{:S(2)}, u32[]{:S(2)}) collective-permute-start(f32[256,128]{1,0:T(8,128)S(1)} %get-tuple-element.41), channel_id=1, source_target_pairs={{1,2},{2,1},{3,4},{4,3},{5,6},{6,5},{7,0},{0,7},{9,10},{10,9},{11,... | collective-permute-start | bytes 393224 | tf_op jit(solution)/shard_map/ppermute | solution.py:796
  3.7 3.2 %collective-permute-start.1 = (f32[256,128]{1,0:T(8,128)S(1)}, f32[256,128]{1,0:T(8,128)S(1)}, u32[]{:S(2)}, u32[]{:S(2)}) collective-permute-start(f32[256,128]{1,0:T(8,128)S(1)} %get-tuple-element.42), channel_id=1, source_target_pairs={{0,1},{1,0},{2,3},{3,2},{4,5},{5,4},{6,7},{7,6},{8,9},{9,8},{10,11... | collective-permute-start | bytes 393224 | tf_op jit(solution)/shard_map/ppermute | solution.py:796
  6.9 1.4 %start.1 = (f32[19,4,40,128]{3,2,1,0:T(8,128)S(1)}, f32[4,40,128]{2,1,0:T(8,128)S(1)}, f32[4,40,128]{2,1,0:T(8,128)S(1)}, f32[8,56,128]{2,1,0:T(8,128)S(1)}, f32...) custom-call(f32[19,4,32,128]{3,2,1,0:T(8,128)S(1)} %get-tuple-element.43.pops, ...), custom_call_target="tpu_custom_call" | custom-call | tf_op jit(solution)/shard_map/start/pallas_call | solution.py:821
  8.3 6.6 %collective-permute-start.5 = (f32[624,128]{1,0:T(8,128)S(1)}, f32[624,128]{1,0:T(8,128)S(1)}, u32[]{:S(2)}, u32[]{:S(2)}) collective-permute-start(f32[624,128]{1,0:T(8,128)S(1)} %get-tuple-element.68), channel_id=1, source_target_pairs={{8,16},{16,8},{24,32},{32,24},{40,48},{48,40},{56,64},{64,56},{72,... | collective-permute-start | bytes 958472 | tf_op jit(solution)/shard_map/ppermute | solution.py:796
  14.9 0.0 collective-permute-done.yb
  14.9 0.0 collective-permute-done.1.ya
  14.9 1.0 %edge.1 = (f32[19,4,40,128]{3,2,1,0:T(8,128)S(1)}, f32[4,40,128]{2,1,0:T(8,128)S(1)}, f32[4,40,128]{2,1,0:T(8,128)S(1)}, f32[8,56,128]{2,1,0:T(8,128)S(1)}, f32[...) custom-call(f32[256,128]{1,0:T(8,128)S(1)} %collective-permute-done., ...), custom_call_target="tpu_custom_call", output_to_operand_aliasing={{0}: (2, {}), {1}: (3, {}), {2}: (4, {}), {3}: (5, {}), {4}... | custom-call | flops 10000000000 | bytes 10000000000 | tf_op jit(solution)/shard_map/edge/pallas_call | solution.py:825
  15.9 0.1 collective-permute-start.2
  16.0 0.5 %collective-permute-start.3 = (f32[10,40,128]{2,1,0:T(8,128)S(1)}, f32[10,40,128]{2,1,0:T(8,128)S(1)}, u32[]{:S(2)}, u32[]{:S(2)}) collective-permute-start(f32[10,40,128]{2,1,0:T(8,128)S(1)} %get-tuple-element.59), channel_id=1, source_target_pairs={{0,8},{8,0},{16,24},{24,16},{32,40},{40,32},{48,56},{56,48},{64,72... | collective-permute-start | bytes 614408 | tf_op jit(solution)/shard_map/ppermute | solution.py:796
  16.5 2.5 %collective-permute-start.4 = (f32[138,128]{1,0:T(8,128)S(1)}, f32[138,128]{1,0:T(8,128)S(1)}, u32[]{:S(2)}, u32[]{:S(2)}) collective-permute-start(f32[138,128]{1,0:T(8,128)S(1)} %get-tuple-element.62), channel_id=1, source_target_pairs={{8,16},{16,8},{24,32},{32,24},{40,48},{48,40},{56,64},{64,56},{72,... | collective-permute-start | bytes 211976 | tf_op jit(solution)/shard_map/ppermute | solution.py:796
  19.0 0.0 collective-permute-done.3.xd
  19.0 0.0 collective-permute-done.2.xa
  19.0 1.6 %near.1 = (f32[19,6,56,128]{3,2,1,0:T(8,128)S(1)}, f32[9,6,56,128]{3,2,1,0:T(8,128)S(1)}, f32[19,6,56,128]{3,2,1,0:T(8,128)S(1)}, f32[9,6,56,128]{3,2,1,0:T(8,12...) custom-call(f32[19,4,40,128]{3,2,1,0:T(8,128)S(1)} %get-tuple-elemen, ...), custom_call_target="tpu_custom_call", output_to_operand_aliasing={{0}: (4, {}), {1}: (5, {})} | custom-call | tf_op jit(solution)/shard_map/near/pallas_call | solution.py:840
  20.6 0.0 collective-permute-done.5.xb
  20.6 2.2 %far.1 = (f32[19,4,16,128]{3,2,1,0:T(8,128)S(1)}, f32[4,16,128]{2,1,0:T(8,128)S(1)}, f32[19,6,56,128]{3,2,1,0:T(8,128)S(1)}, f32[9,6,56,128]{3,2,1,0:T(8,128)S(1...) custom-call(f32[19,4,40,128]{3,2,1,0:T(8,128)S(1)} %get-tuple-elemen, ...), custom_call_target="tpu_custom_call", output_to_operand_aliasing={{2}: (4, {}), {3}: (5, {}), {4}: (6, {}), {5}: (7, {})} | custom-call | tf_op jit(solution)/shard_map/far/pallas_call | solution.py:847
  22.9 4.7 %collective-permute-done.4.xc = f32[138,128]{1,0:T(8,128)S(1)} collective-permute-done((f32[138,128]{1,0:T(8,128)S(1)}, f32[138,128]{1,0:T(8,128)S(1)}, u32[]{:S(2)}, u32[]{:S(2)}) %collective-permute-start.4) | collective-permute-done | bytes 70688 | tf_op jit(solution)/shard_map/ppermute | solution.py:796
  27.5 2.5 %end.1 = (f32[19,4,32,128]{3,2,1,0:T(8,128)}, f32[4,32,128]{2,1,0:T(8,128)}, f32[19,6,56,128]{3,2,1,0:T(8,128)S(1)}, f32[9,6,56,128]{3,2,1,0:T(8,128)S(1)}, f32[...) custom-call(f32[19,4,40,128]{3,2,1,0:T(8,128)S(1)} %get-tuple-elemen, ...), custom_call_target="tpu_custom_call", output_to_operand_aliasing={{2}: (8, {}), {3}: (9, {}), {4}: (10, {}), {5}: (11, {}), {... | custom-call | tf_op jit(solution)/shard_map/end/pallas_call | solution.py:851
Async XLA Ops:
  2.0 12.9 %collective-permute-start = (f32[256,128]{1,0:T(8,128)S(1)}, f32[256,128]{1,0:T(8,128)S(1)}, u32[]{:S(2)}, u32[]{:S(2)}) collective-permute-start(f32[256,128]{1,0:T(8,128)S(1)} %get-tuple-element.41), channel_id=1, source_target_pairs={{1,2},{2,1},{3,4},{4,3},{5,6},{6,5},{7,0},{0,7},{9,10},{10,9},{11,... | collective-permute-start | bytes 393224 | tf_op jit(solution)/shard_map/ppermute | solution.py:796
  3.7 11.2 %collective-permute-start.1 = (f32[256,128]{1,0:T(8,128)S(1)}, f32[256,128]{1,0:T(8,128)S(1)}, u32[]{:S(2)}, u32[]{:S(2)}) collective-permute-start(f32[256,128]{1,0:T(8,128)S(1)} %get-tuple-element.42), channel_id=1, source_target_pairs={{0,1},{1,0},{2,3},{3,2},{4,5},{5,4},{6,7},{7,6},{8,9},{9,8},{10,11... | collective-permute-start | bytes 393224 | tf_op jit(solution)/shard_map/ppermute | solution.py:796
  8.3 12.3 %collective-permute-start.5 = (f32[624,128]{1,0:T(8,128)S(1)}, f32[624,128]{1,0:T(8,128)S(1)}, u32[]{:S(2)}, u32[]{:S(2)}) collective-permute-start(f32[624,128]{1,0:T(8,128)S(1)} %get-tuple-element.68), channel_id=1, source_target_pairs={{8,16},{16,8},{24,32},{32,24},{40,48},{48,40},{56,64},{64,56},{72,... | collective-permute-start | bytes 958472 | tf_op jit(solution)/shard_map/ppermute | solution.py:796
  15.9 3.1 %collective-permute-start.2 = (f32[11,40,128]{2,1,0:T(8,128)S(1)}, f32[11,40,128]{2,1,0:T(8,128)S(1)}, u32[]{:S(2)}, u32[]{:S(2)}) collective-permute-start(f32[11,40,128]{2,1,0:T(8,128)S(1)} %get-tuple-element.58), channel_id=1, source_target_pairs={{0,8},{8,0},{16,24},{24,16},{32,40},{40,32},{48,56},{56,48},{64,72... | collective-permute-start | bytes 675848 | tf_op jit(solution)/shard_map/ppermute | solution.py:796
  16.0 3.0 %collective-permute-start.3 = (f32[10,40,128]{2,1,0:T(8,128)S(1)}, f32[10,40,128]{2,1,0:T(8,128)S(1)}, u32[]{:S(2)}, u32[]{:S(2)}) collective-permute-start(f32[10,40,128]{2,1,0:T(8,128)S(1)} %get-tuple-element.59), channel_id=1, source_target_pairs={{0,8},{8,0},{16,24},{24,16},{32,40},{40,32},{48,56},{56,48},{64,72... | collective-permute-start | bytes 614408 | tf_op jit(solution)/shard_map/ppermute | solution.py:796
  16.5 11.1 %collective-permute-start.4 = (f32[138,128]{1,0:T(8,128)S(1)}, f32[138,128]{1,0:T(8,128)S(1)}, u32[]{:S(2)}, u32[]{:S(2)}) collective-permute-start(f32[138,128]{1,0:T(8,128)S(1)} %get-tuple-element.62), channel_id=1, source_target_pairs={{8,16},{16,8},{24,32},{32,24},{40,48},{48,40},{56,64},{64,56},{72,... | collective-permute-start | bytes 211976 | tf_op jit(solution)/shard_map/ppermute | solution.py:796
